TPU v7x, 256 devices: a whole 4x4x8 slice. The times are simulated.
256 devices in a mesh: seq: 8 (over y, core), vocab: 32 (over z, x).
Axes of the slice: x: 4, y: 4, z: 8, core: 2. Of those that a mesh axis runs over, the one named last changes fastest.
Arguments:
- hidden: bfloat16 [2, 1024, 5120], P(None, 'seq'), may hold values from -128 to 128
- head_weight: bfloat16 [5120, 77824], P('seq', 'vocab'), may hold values from -1 to 1
- ref_logits: bfloat16 [2, 1024, 77824], P(None, 'seq', 'vocab'), may hold values from -320 to 320
- token_ids: int32 [2, 1024], P(None, 'seq'), may hold values from 0 to 77823
- end_pos: int32 [2], replicated, may hold values from 512 to 1023
- loss_mask: int32 [2, 1024], P(None, 'seq'), may hold values 0 or 1
- scores: float32 [2], replicated, may hold values from -8 to 8
Outputs:
- logit_grad: bfloat16 [2, 1024, 77824], P(None, 'seq', 'vocab')
- hidden_grad: bfloat16 [2, 1024, 5120], P(None, 'seq', 'vocab')
- advantages: float32 [2, 1024], P(None, 'seq')
All inputs are finite; a program needn't handle non-finite values. No bound on the sum of `loss_mask` on one device may be relied on, other than what follows from the above.
Results may differ from a plain program's by a relative error of at most 0.0039.
The roundings to bfloat16 on the way count: a program that leaves them out, or rounds other values in their place, can miss the bound.
Values may be sent and summed in bfloat16 or wider, within the bound.
No kernel may reach another device: no remote copies, remote signals or barrier semaphores. Data moves between devices by JAX's collectives and lax.ppermute only.
A program may use at most 128 MiB of HBM per device.

v0:
```python
import jax
import jax.numpy as jnp
from jax import lax
from jax.sharding import PartitionSpec as P


def from_behind(shard, axis, by):
    devices = lax.axis_size(axis)
    pairs = [(i, i + by) for i in range(devices) if 0 <= i + by < devices]
    return lax.ppermute(shard, axis, pairs)


def per_device(hidden, head_weight, ref_logits, token_ids, end_pos, loss_mask, scores):
    batch, segment, width = hidden.shape
    vocab_dev = head_weight.shape[1]
    seq_start = lax.axis_index("seq") * segment
    vocab_start = lax.axis_index("vocab") * vocab_dev
    whole_head = lax.all_gather(head_weight, "seq", axis=0, tiled=True)
    logits = jnp.dot(
        hidden.reshape(batch * segment, width), whole_head, preferred_element_type=jnp.float32
    ).reshape(batch, segment, vocab_dev)
    refs = ref_logits.astype(jnp.float32)
    local_top = jnp.max(logits, axis=2)
    local_rtop = jnp.max(refs, axis=2)
    top_policy, top_ref = lax.pmax((local_top, local_rtop), "vocab")
    expo = jnp.exp(logits - top_policy[:, :, None])
    total, ref_total, weighted = lax.psum(
        (
            jnp.sum(expo, axis=2),
            jnp.sum(jnp.exp(refs - top_ref[:, :, None]), axis=2),
            jnp.sum(expo * (logits - refs), axis=2),
        ),
        "vocab",
    )
    lse_policy = top_policy + jnp.log(total)
    lse_ref = top_ref + jnp.log(ref_total)
    kl_value = weighted / total - lse_policy + lse_ref
    position = seq_start + lax.broadcasted_iota(jnp.int32, (1, segment), 1)
    live = ((loss_mask == 1) & (position <= end_pos[:, None])).astype(jnp.float32)
    at_end = (position == end_pos[:, None]).astype(jnp.float32)
    reward = -0.01 * kl_value * live + scores[:, None] * at_end
    upper = (
        lax.broadcasted_iota(jnp.int32, (segment, segment), 0)
        >= lax.broadcasted_iota(jnp.int32, (segment, segment), 1)
    ).astype(jnp.float32)
    local_returns = jnp.dot(reward, upper, precision=lax.Precision.HIGHEST)
    totals = jnp.sum(reward, axis=1)
    carried = jnp.zeros_like(totals)
    for _ in range(lax.axis_size("seq") - 1):
        carried = from_behind(totals + carried, "seq", -1)
    returns = local_returns + carried[:, None]
    count, first_moment, second_moment = lax.psum(
        (jnp.sum(live), jnp.sum(live * returns), jnp.sum(live * returns * returns)), "seq"
    )
    count = jnp.maximum(count, 1.0)
    mean = first_moment / count
    var = second_moment / count - mean * mean
    advantages = (returns - mean) / jnp.sqrt(var + 1e-05)
    factor = live * advantages / count
    prob = jnp.exp(logits - lse_policy[:, :, None])
    column = vocab_start + lax.broadcasted_iota(jnp.int32, (1, 1, vocab_dev), 2)
    onehot = (column == token_ids[:, :, None]).astype(jnp.float32)
    logit_grad = (factor[:, :, None] * (prob - onehot)).astype(jnp.bfloat16)
    partial_grad = lax.dot_general(
        logit_grad.reshape(batch * segment, vocab_dev),
        whole_head,
        (((1,), (1,)), ((), ())),
        preferred_element_type=jnp.float32,
    ).reshape(batch, segment, width)
    hidden_grad = lax.psum_scatter(partial_grad, "vocab", scatter_dimension=2, tiled=True).astype(
        jnp.bfloat16
    )
    return (logit_grad, hidden_grad, advantages)


def solution(mesh):
    in_specs = (
        P(None, "seq", None),
        P("seq", "vocab"),
        P(None, "seq", "vocab"),
        P(None, "seq"),
        P(),
        P(None, "seq"),
        P(),
    )
    out_specs = (P(None, "seq", "vocab"), P(None, "seq", "vocab"), P(None, "seq"))
    return jax.shard_map(
        per_device, mesh=mesh, in_specs=in_specs, out_specs=out_specs, check_vma=False
    )
```

profile of v0, /device:TPU:30, one launch (start us, length us, event | category | flops | bytes accessed | tf_op | source)
XLA Modules:
  0.0 591.9 jit_solution(15525419192187923961)
XLA Ops:
  7.2 0.0 all-gather.2.cloned.1.call-start
  7.2 0.7 all-gather.2.cloned.1.call-update
  7.9 0.0 reduce-scatter.2.cloned.1.call-start
  8.0 1.5 reduce_max.24
  9.5 123.7 %all-gather.2.cloned.1.call-done = bf16[5120,2432]{1,0:T(8,128)(2,1)} async-done(((bf16[640,2432]{1,0:T(8,128)(2,1)}), bf16[5120,2432]{1,0:T(8,128)(2,1)}) %all-gather.2.cloned.1.call-update) | async-done | bytes 24903696 | tf_op jit(solution)/shard_map/all_gather | solution.py:18
  133.2 13.4 %fusion.14 = (f32[2,128]{1,0:T(2,128)S(1)}, f32[2,128,2432]{2,1,0:T(8,128)}) fusion(bf16[2,128,5120]{2,1,0:T(8,128)(2,1)S(1)} %copy-done, bf16[5120,2432]{1,0:T(8,128)(2,1)} %all-gather.2.cloned.1.call-done), kind=kOutput, calls=%fused_computation.28 | convolution fusion | flops 6375964672 | bytes 30016512 | tf_op jit(solution)/shard_map/dot_general | solution.py:19
  146.6 67.3 %all-reduce.1 = (f32[2,128]{1,0:T(2,128)S(1)}, f32[2,128]{1,0:T(2,128)S(1)}) all-reduce(f32[2,128]{1,0:T(2,128)S(1)} %get-tuple-element.23, bf16[2,128]{1,0:T(2,128)(2,1)S(1)} %reduce_max.24), channel_id=1, replica_groups=mesh['seq'=8,'vocab'=32] {'vocab'}, use_global_device_ids=true, to_apply=%region_1.0 | all-reduce | flops 512 | bytes 3584 | tf_op jit(solution)/shard_map/pmax | solution.py:25
  213.9 3.2 fusion.5
  217.2 74.2 %all-reduce = (f32[2,128]{1,0:T(2,128)S(1)}, f32[2,128]{1,0:T(2,128)S(1)}, f32[2,128]{1,0:T(2,128)S(1)}) all-reduce(f32[2,128]{1,0:T(2,128)S(1)} %get-tuple-element.4, f32[2,128]{1,0:T(2,128)S(1)} %get-tuple-element.5, f32[2,128]{1,0:T(2,128)S(1)} %get-tuple-element.3), channel_id=1, replica_groups=mesh['seq'=8,'vocab'=32] {'vocab'}, use_global_device_ids=true, to_apply=%region_5.0 | all-reduce | flops 768 | bytes 6144 | tf_op jit(solution)/shard_map/psum | solution.py:27
  291.3 0.2 fusion.12
  291.5 1.9 collective-permute-start
  293.4 1.3 collective-permute-done
  294.7 3.6 collective-permute-start.1
  298.3 1.3 collective-permute-done.1
  299.6 3.6 collective-permute-start.2
  303.1 1.3 collective-permute-done.2
  304.4 3.6 collective-permute-start.3
  308.0 1.3 collective-permute-done.3
  309.3 3.6 collective-permute-start.4
  312.9 1.3 collective-permute-done.4
  314.1 3.6 collective-permute-start.5
  317.7 1.3 collective-permute-done.5
  319.0 3.6 collective-permute-start.6
  322.6 1.3 collective-permute-done.6
  323.8 0.8 select_reduce_fusion
  324.6 12.3 %all-reduce.2 = (f32[]{:T(128)}, f32[]{:T(128)}, f32[]{:T(128)}) all-reduce(f32[]{:T(128)} %get-tuple-element.7, f32[]{:T(128)} %get-tuple-element.8, f32[]{:T(128)} %get-tuple-element.6), channel_id=1, replica_groups=mesh['seq'=8,'vocab'=32] {'seq'}, use_global_device_ids=true, to_apply=%region_16.0 | all-reduce | flops 3 | bytes 24 | tf_op jit(solution)/shard_map/psum | solution.py:52
  338.9 0.6 select_divide_fusion
  339.5 2.5 multiply_convert_fusion
  342.0 1.0 copy-done.1
  343.0 14.2 %fusion = f32[2,128,5120]{1,2,0:T(8,128)} fusion(bf16[2,128,2432]{2,1,0:T(8,128)(2,1)S(1)} %multiply_convert_fusion, bf16[5120,2432]{1,0:T(8,128)(2,1)} %all-gather.2.cloned.1.call-done), kind=kOutput, calls=%fused_computation | convolution fusion | flops 6375342080 | bytes 31391744 | tf_op jit(solution)/shard_map/dot_general | solution.py:64
  357.2 226.3 %reduce-scatter.2.cloned.1.call-done = f32[2,128,160]{1,2,0:T(8,128)} async-done(((f32[2,128,5120]{1,2,0:T(8,128)}), f32[2,128,160]{1,2,0:T(8,128)}) %reduce-scatter.2.cloned.1.call-update) | async-done | bytes 163856 | tf_op jit(solution)/shard_map/reduce_scatter | solution.py:70
  583.5 1.6 convert_element_type.21
  (20 shorter events, 0.1 us)
Async XLA Ops:
  7.2 126.1 %copy-start = (bf16[2,128,5120]{2,1,0:T(8,128)(2,1)S(1)}, bf16[2,128,5120]{2,1,0:T(8,128)(2,1)}, u32[]{:S(2)}) copy-start(bf16[2,128,5120]{2,1,0:T(8,128)(2,1)} %param.7) | copy-start | bytes 7864324
  7.2 126.0 %all-gather.2.cloned.1.call-start = ((), (), s32[]{:S(2)}) async-start(), calls=%async_computation.1 | async-start | bytes 28016640 | tf_op jit(solution)/shard_map/all_gather | solution.py:18
  7.9 575.6 %reduce-scatter.2.cloned.1.call-start = ((), (), s32[]{:S(2)}) async-start(), calls=%async_computation.2 | async-start | bytes 5406720 | tf_op jit(solution)/shard_map/reduce_scatter | solution.py:70
  146.6 144.7 %copy-start.3 = (s32[2,128]{1,0:T(2,128)S(1)}, s32[2,128]{1,0:T(2,128)}, u32[]{:S(2)}) copy-start(s32[2,128]{1,0:T(2,128)} %param.12) | copy-start | bytes 3076
  146.6 144.7 %copy-start.4 = (f32[2]{0:T(128)S(1)}, f32[2]{0:T(128)}, u32[]{:S(2)}) copy-start(f32[2]{0:T(128)} %param.13) | copy-start | bytes 28
  146.6 144.7 %copy-start.5 = (s32[2]{0:T(128)S(1)}, s32[2]{0:T(128)}, u32[]{:S(2)}) copy-start(s32[2]{0:T(128)} %param.11) | copy-start | bytes 28
  146.6 192.9 %copy-start.2 = (s32[2,128]{1,0:T(2,128)S(1)}, s32[2,128]{1,0:T(2,128)}, u32[]{:S(2)}) copy-start(s32[2,128]{1,0:T(2,128)} %param.10) | copy-start | bytes 3076
  291.5 3.2 collective-permute-start
  294.7 4.8 collective-permute-start.1
  299.6 4.8 collective-permute-start.2
  304.4 4.8 collective-permute-start.3
  309.3 4.8 collective-permute-start.4
  314.1 4.8 collective-permute-start.5
  319.0 4.8 collective-permute-start.6
  342.0 1.0 copy-start.1
Sparse Core Ops, SparseCore 0:
  9.8 123.3 all-gather.1
  357.4 226.1 reduce-scatter.1
where the time goes:
time: 594 us; the launch traced here: 592 us
  waiting for transfers between devices  360 us (61%)
  blocking collectives  154 us (26%)
  matrix products  28.3 us (5%)
  starting transfers between devices  23.4 us (4%)
  between operations  16.2 us (3%)
  other arithmetic  9.68 us (2%)
    reduce_scatter x1, waiting for transfers between devices, per_device(): lax.psum_scatter(partial_grad, 'vocab', scatter_dimension=2, tiled=True)  226 us
    all_gather x1, waiting for transfers between devices, per_device(): whole_head = lax.all_gather(head_weight, 'seq', axis=0, tiled=True)  124 us
    psum x1, blocking collectives, per_device(): lax.psum((jnp.sum(expo, axis=2), jnp.sum(jnp.exp(refs - top_ref[:, :, Non...  74.2 us
    pmax x1, blocking collectives, per_device(): top_policy, top_ref = lax.pmax((local_top, local_rtop), 'vocab')  67.3 us
    ppermute x7, starting transfers between devices, from_behind(): return lax.ppermute(shard, axis, pairs)  23.3 us
    dot_general x1, matrix products, per_device(): lax.dot_general(logit_grad.reshape(batch * segment, vocab_dev), whole_hea...  14.2 us
    dot_general x1, matrix products, per_device(): jnp.dot(hidden.reshape(batch * segment, width), whole_head, preferred_ele...  13.4 us
    psum x1, blocking collectives, per_device(): lax.psum((jnp.sum(live), jnp.sum(live * returns), jnp.sum(live * returns...  12.3 us
  transfers between devices with their start and end apart: 9, of which 9 were waited for; matrix products, arithmetic and copies ran while one was open for 0% of the time, Pallas kernels for 0%

commit v1 on v0

v1 whole, which is shorter than its diff:
```python
import jax
import jax.numpy as jnp
from jax import lax
from jax.sharding import Mesh, PartitionSpec as P

SEQ = ("y", "c")
VOC = ("z", "x")
BOUNDS = ((0, 256), (256, 512), (512, 640))


def spread(value, axes):
    count = lax.axis_size(axes)
    return lax.all_to_all(jnp.broadcast_to(value[None], (count,) + value.shape), axes, 0, 0)


def per_device(hidden, head_weight, ref_logits, token_ids, end_pos, loss_mask, scores):
    batch, segment, width = hidden.shape
    rows = batch * segment
    depth, vocab_dev = head_weight.shape
    seqs = lax.axis_size(SEQ)
    seq_index = lax.axis_index(SEQ)
    seq_start = seq_index * segment
    vocab_start = lax.axis_index(VOC) * vocab_dev

    heads = [lax.all_gather(head_weight[lo:hi], SEQ, axis=0, tiled=True) for lo, hi in BOUNDS]

    refs = ref_logits.astype(jnp.float32).reshape(rows, vocab_dev)
    ref_top = jnp.max(refs, axis=1)
    ref_lse = ref_top + jnp.log(jnp.sum(jnp.exp(refs - ref_top[:, None]), axis=1))

    states = hidden.reshape(rows, seqs, depth)
    logits = None
    for (lo, hi), head in zip(BOUNDS, heads):
        term = jnp.dot(
            states[:, :, lo:hi].reshape(rows, seqs * (hi - lo)), head, preferred_element_type=jnp.float32
        )
        logits = term if logits is None else logits + term
    top = jnp.max(logits, axis=1)
    expo = jnp.exp(logits - top[:, None])
    stats = jnp.stack(
        [top, jnp.sum(expo, axis=1), jnp.sum(expo * (logits - refs), axis=1), ref_lse]
    )
    stats = spread(stats, VOC)
    tops = stats[:, 0]
    top_policy = jnp.max(tops, axis=0)
    scale = jnp.exp(tops - top_policy[None])
    total = jnp.sum(stats[:, 1] * scale, axis=0)
    weighted = jnp.sum(stats[:, 2] * scale, axis=0)
    top_ref = jnp.max(stats[:, 3], axis=0)
    lse_ref = top_ref + jnp.log(jnp.sum(jnp.exp(stats[:, 3] - top_ref[None]), axis=0))
    lse_policy = top_policy + jnp.log(total)
    kl_value = (weighted / total - lse_policy + lse_ref).reshape(batch, segment)

    position = seq_start + lax.broadcasted_iota(jnp.int32, (1, segment), 1)
    live = ((loss_mask == 1) & (position <= end_pos[:, None])).astype(jnp.float32)
    at_end = (position == end_pos[:, None]).astype(jnp.float32)
    reward = -0.01 * kl_value * live + scores[:, None] * at_end
    both = spread(jnp.stack([reward, live]), SEQ)
    rewards, lives = both[:, 0], both[:, 1]
    upper = (
        lax.broadcasted_iota(jnp.int32, (segment, segment), 0)
        >= lax.broadcasted_iota(jnp.int32, (segment, segment), 1)
    ).astype(jnp.float32)
    suffix = jnp.dot(
        rewards.reshape(seqs * batch, segment), upper, precision=lax.Precision.HIGHEST
    ).reshape(seqs, batch, segment)
    totals = jnp.sum(rewards, axis=2)
    later = (
        lax.broadcasted_iota(jnp.int32, (seqs, seqs, 1), 1)
        > lax.broadcasted_iota(jnp.int32, (seqs, seqs, 1), 0)
    ).astype(jnp.float32)
    carried = jnp.sum(later * totals[None], axis=1)
    returns_all = suffix + carried[:, :, None]
    count = jnp.maximum(jnp.sum(lives), 1.0)
    mean = jnp.sum(lives * returns_all) / count
    var = jnp.sum(lives * returns_all * returns_all) / count - mean * mean
    returns = lax.dynamic_index_in_dim(returns_all, seq_index, 0, keepdims=False)
    advantages = (returns - mean) / jnp.sqrt(var + 1e-05)
    factor = live * advantages / count

    prob = jnp.exp(logits - lse_policy[:, None])
    column = vocab_start + lax.broadcasted_iota(jnp.int32, (1, vocab_dev), 1)
    onehot = (column == token_ids.reshape(rows, 1)).astype(jnp.float32)
    logit_grad = (factor.reshape(rows, 1) * (prob - onehot)).astype(jnp.bfloat16)

    pieces = []
    for (lo, hi), head in zip(BOUNDS[::-1], heads[::-1]):
        part = lax.dot_general(
            head, logit_grad, (((1,), (1,)), ((), ())), preferred_element_type=jnp.float32
        ).reshape(seqs, hi - lo, rows)
        pieces.append(lax.psum_scatter(part, "z", scatter_dimension=0, tiled=False))
    mine = jnp.concatenate(pieces[::-1], axis=0)
    mine = mine.reshape(lax.axis_size("x"), depth // lax.axis_size("x"), rows)
    mine = lax.psum_scatter(mine, "x", scatter_dimension=0, tiled=False)
    hidden_grad = mine.T.reshape(batch, segment, -1).astype(jnp.bfloat16)
    return (logit_grad.reshape(batch, segment, vocab_dev), hidden_grad, advantages)


def solution(mesh):
    chips = mesh.devices.reshape(4, 2, 8, 4)
    fine = Mesh(chips, ("y", "c", "z", "x"))
    in_specs = (
        P(None, SEQ, None),
        P(SEQ, VOC),
        P(None, SEQ, VOC),
        P(None, SEQ),
        P(),
        P(None, SEQ),
        P(),
    )
    out_specs = (P(None, SEQ, VOC), P(None, SEQ, VOC), P(None, SEQ))
    return jax.shard_map(
        per_device, mesh=fine, in_specs=in_specs, out_specs=out_specs, check_vma=False
    )
```

time: 594 us -> 375 us (0.63)
  blocking collectives: 154 us -> 0 us
  waiting for transfers between devices: 360 us -> 279 us
  local copies, waits for them, and re-layouts: 1.05 us -> 16 us
  matrix products: 28.3 us -> 37.4 us
  starting transfers between devices: 23.4 us -> 16.2 us
    reduce_scatter x1 -> x4, waiting for transfers between devices: 226 us -> 128 us  [the longest x3 106 us: per_device(): pieces.append(lax.psum_scatter(part, 'z', scatter_dimension=0, tiled=False))]
    psum x2 -> x0, blocking collectives: 86.4 us -> none  [the longest x1 74.2 us: per_device(): lax.psum((jnp.sum(expo, axis=2), jnp.sum(jnp.exp(refs - top_ref[:, :, Non...]
    pmax x1 -> x0, blocking collectives: 67.3 us -> none  [per_device(): top_policy, top_ref = lax.pmax((local_top, local_rtop), 'vocab')]
    ppermute x7 -> x0, starting transfers between devices: 23.3 us -> none  [from_behind(): return lax.ppermute(shard, axis, pairs)]
    all_to_all x0 -> x2, starting transfers between devices: none -> 15.8 us  [spread(): lax.all_to_all(jnp.broadcast_to(value[None], (count,) + value.shape), axe...]
    all_gather x1 -> x3, waiting for transfers between devices: 124 us -> 138 us  [per_device(): lax.all_gather(head_weight[lo:hi], SEQ, axis=0, tiled=True)]
    all_to_all x0 -> x2, waiting for transfers between devices: none -> 12.5 us  [spread(): lax.all_to_all(jnp.broadcast_to(value[None], (count,) + value.shape), axe...]
    dot_general x3 -> x7, matrix products: 28.3 us -> 37.4 us  [the longest x3 21.6 us: per_device(): jnp.dot(states[:, :, lo:hi].reshape(rows, seqs * (hi - lo)), head, prefer...]
  transfers between devices with their start and end apart: 9 -> 9, of which waited for: 9 -> 9; matrix products, arithmetic and copies ran while one was open for 0% -> 10% of each run, Pallas kernels for 0% -> 0%
where the time goes in v1:
time: 375 us; the launch traced here: 372 us
  waiting for transfers between devices  279 us (74%)
  matrix products  37.4 us (10%)
  between operations  16.4 us (4%)
  starting transfers between devices  16.2 us (4%)
  local copies, waits for them, and re-layouts  16 us (4%)
  other arithmetic  7.08 us (2%)
    all_gather x3, waiting for transfers between devices, per_device(): lax.all_gather(head_weight[lo:hi], SEQ, axis=0, tiled=True)  138 us
    reduce_scatter x3, waiting for transfers between devices, per_device(): pieces.append(lax.psum_scatter(part, 'z', scatter_dimension=0, tiled=False))  106 us
    reduce_scatter x1, waiting for transfers between devices, per_device(): mine = lax.psum_scatter(mine, 'x', scatter_dimension=0, tiled=False)  21.8 us
    dot_general x3, matrix products, per_device(): jnp.dot(states[:, :, lo:hi].reshape(rows, seqs * (hi - lo)), head, prefer...  21.6 us
    all_to_all x2, starting transfers between devices, spread(): lax.all_to_all(jnp.broadcast_to(value[None], (count,) + value.shape), axe...  15.8 us
    dot_general x3, matrix products, per_device(): lax.dot_general(head, logit_grad, (((1,), (1,)), ((), ())), preferred_ele...  15.1 us
    all_to_all x2, waiting for transfers between devices, spread(): lax.all_to_all(jnp.broadcast_to(value[None], (count,) + value.shape), axe...  12.5 us
  transfers between devices with their start and end apart: 9, of which 9 were waited for; matrix products, arithmetic and copies ran while one was open for 10% of the time, Pallas kernels for 0%

profile of v1, /device:TPU:30, one launch (start us, length us, event | category | flops | bytes accessed | tf_op | source)
XLA Modules:
  0.0 372.3 jit_solution(1781459673582744261)
XLA Ops:
  7.2 3.4 fusion.19
  10.7 0.7 all-gather.6.cloned.1.call-update
  11.4 2.0 slice.42
  14.1 1.3 copy.59
  15.4 1.3 copy.60
  17.5 53.1 %all-gather.4.cloned.1.call-done = bf16[2048,2432]{1,0:T(8,128)(2,1)} async-done(((bf16[256,2432]{1,0:T(8,128)(2,1)}), bf16[2048,2432]{1,0:T(8,128)(2,1)}) %all-gather.4.cloned.1.call-update) | async-done | bytes 9961488 | tf_op jit(solution)/shard_map/all_gather | solution.py:25
  70.6 8.3 %fusion.22 = f32[256,2432]{1,0:T(8,128)} fusion(bf16[256,2048]{1,0:T(8,128)(2,1)S(1)} %bitcast.124, bf16[2048,2432]{1,0:T(8,128)(2,1)} %all-gather.4.cloned.1.call-done), kind=kOutput, calls=%fused_computation.60 | convolution fusion | flops 2550136832 | bytes 13500416 | tf_op jit(solution)/shard_map/dot_general | solution.py:34
  78.9 53.3 %all-gather.6.cloned.1.call-done = bf16[2048,2432]{1,0:T(8,128)(2,1)} async-done(((bf16[256,2432]{1,0:T(8,128)(2,1)}), bf16[2048,2432]{1,0:T(8,128)(2,1)}) %all-gather.6.cloned.1.call-update) | async-done | bytes 9961488 | tf_op jit(solution)/shard_map/all_gather | solution.py:25
  132.2 8.4 %convolution_add_fusion.1 = f32[256,2432]{1,0:T(8,128)} fusion(f32[256,2432]{1,0:T(8,128)} %fusion.22, bf16[256,2048]{1,0:T(8,128)(2,1)S(1)} %bitcast.123, bf16[2048,2432]{1,0:T(8,128)(2,1)} %all-gather.6.cloned.1.call-done), kind=kOutput, calls=%fused_computation.1 | convolution fusion | flops 2550759424 | bytes 15990784 | tf_op jit(solution)/shard_map/dot_general | solution.py:34
  140.5 31.6 %all-gather.8.cloned.1.call-done = bf16[1024,2432]{1,0:T(8,128)(2,1)} async-done(((bf16[128,2432]{1,0:T(8,128)(2,1)}), bf16[1024,2432]{1,0:T(8,128)(2,1)}) %all-gather.8.cloned.1.call-update) | async-done | bytes 4980752 | tf_op jit(solution)/shard_map/all_gather | solution.py:25
  172.1 4.9 %fusion.21 = (f32[256]{0:T(256)S(1)}, f32[256,2432]{1,0:T(8,128)S(1)}) fusion(f32[256,2432]{1,0:T(8,128)} %convolution_add_fusion.1, bf16[1024,2432]{1,0:T(8,128)(2,1)} %all-gather.8.cloned.1.call-done, bf16[32,8,8,128]{3,2,1,0:T(8,128)(2,1)S(1)} %bitcast.119), kind=kOutput, calls=%fused_computation.59 | convolution fusion | flops 1276313344 | bytes 10486784 | tf_op jit(solution)/shard_map/dot_general | solution.py:34
  177.1 0.9 fusion.2
  178.0 0.7 broadcast_in_dim.4
  178.7 10.1 %all-to-all-start = ((f32[32,4,256]{2,1,0:T(4,128)}), f32[32,4,256]{2,1,0:T(4,128)S(1)}, u32[]{:S(2)}, u32[]{:S(2)}) async-start(f32[32,4,256]{2,1,0:T(4,128)} %broadcast_in_dim.4), calls=%async_computation | async-start | bytes 262144 | tf_op jit(solution)/shard_map/all_to_all | solution.py:13
  188.8 9.2 %all-to-all-done = f32[32,4,256]{2,1,0:T(4,128)S(1)} async-done(((f32[32,4,256]{2,1,0:T(4,128)}), f32[32,4,256]{2,1,0:T(4,128)S(1)}, u32[]{:S(2)}, u32[]{:S(2)}) %all-to-all-start) | async-done | bytes 131104 | tf_op jit(solution)/shard_map/all_to_all | solution.py:13
  198.9 5.7 %all-to-all-start.1 = ((f32[8,2,2,128]{3,2,1,0:T(2,128)}), f32[8,2,2,128]{3,2,1,0:T(2,128)S(1)}, u32[]{:S(2)}, u32[]{:S(2)}) async-start(f32[8,2,2,128]{3,2,1,0:T(2,128)} %broadcast_in_dim.5), calls=%async_computation.1 | async-start | bytes 32768 | tf_op jit(solution)/shard_map/all_to_all | solution.py:13
  204.6 3.3 all-to-all-done.1
  209.3 0.8 fusion.15
  211.5 0.8 multiply_convert_fusion
  212.3 1.0 copy-done.3
  213.4 4.0 %convolution_bitcast_fusion.2 = f32[1024,256]{0,1:T(8,128)S(1)} fusion(bf16[256,2432]{1,0:T(8,128)(2,1)S(1)} %multiply_convert_fusion, bf16[1024,2432]{1,0:T(8,128)(2,1)} %all-gather.8.cloned.1.call-done), kind=kOutput, calls=%fused_computation.11 | convolution fusion | flops 1275068416 | bytes 7274496 | tf_op jit(solution)/shard_map/dot_general | solution.py:88
  217.3 1.3 copy.46
  218.9 5.5 %convolution_bitcast_fusion.1 = f32[2048,256]{0,1:T(8,128)S(1)} fusion(bf16[256,2432]{1,0:T(8,128)(2,1)S(1)} %copy-done.4, bf16[2048,2432]{1,0:T(8,128)(2,1)} %all-gather.4.cloned.1.call-done), kind=kOutput, calls=%fused_computation.3 | convolution fusion | flops 2550136832 | bytes 13303808 | tf_op jit(solution)/shard_map/dot_general | solution.py:88
  224.5 1.8 copy.44
  226.4 5.6 %convolution_bitcast_fusion = f32[2048,256]{0,1:T(8,128)S(1)} fusion(bf16[256,2432]{1,0:T(8,128)(2,1)S(1)} %copy-done.4, bf16[2048,2432]{1,0:T(8,128)(2,1)} %all-gather.6.cloned.1.call-done), kind=kOutput, calls=%fused_computation.2 | convolution fusion | flops 2550136832 | bytes 13303808 | tf_op jit(solution)/shard_map/dot_general | solution.py:88
  231.9 1.9 copy.45
  233.9 19.6 %reduce-scatter.9.cloned.1.call-done = f32[1,128,256]{2,1,0:T(8,128)} async-done(((f32[8,128,256]{2,1,0:T(8,128)}), f32[1,128,256]{2,1,0:T(8,128)}) %reduce-scatter.9.cloned.1.call-update) | async-done | bytes 131088 | tf_op jit(solution)/shard_map/reduce_scatter | solution.py:91
  253.5 43.2 %reduce-scatter.5.cloned.1.call-done = f32[1,256,256]{2,1,0:T(8,128)} async-done(((f32[8,256,256]{2,1,0:T(8,128)}), f32[1,256,256]{2,1,0:T(8,128)}) %reduce-scatter.5.cloned.1.call-update) | async-done | bytes 262160 | tf_op jit(solution)/shard_map/reduce_scatter | solution.py:91
  296.7 43.4 %reduce-scatter.7.cloned.1.call-done = f32[1,256,256]{2,1,0:T(8,128)} async-done(((f32[8,256,256]{2,1,0:T(8,128)}), f32[1,256,256]{2,1,0:T(8,128)}) %reduce-scatter.7.cloned.1.call-update) | async-done | bytes 262160 | tf_op jit(solution)/shard_map/reduce_scatter | solution.py:91
  340.1 2.0 pad_maximum_fusion
  342.1 21.8 %reduce-scatter.11.cloned.1.call-done = f32[1,160,256]{2,1,0:T(8,128)} async-done(((f32[4,160,256]{2,1,0:T(8,128)}), f32[1,160,256]{2,1,0:T(8,128)}) %reduce-scatter.11.cloned.1.call-update) | async-done | bytes 163856 | tf_op jit(solution)/shard_map/reduce_scatter | solution.py:94
  363.9 1.6 copy_bitcast_fusion
  (58 shorter events, 3.7 us)
Async XLA Ops:
  7.2 63.4 %all-gather.4.cloned.1.call-start = ((), (), s32[]{:S(2)}) async-start(), calls=%async_computation.6 | async-start | bytes 11206656 | tf_op jit(solution)/shard_map/all_gather | solution.py:25
  10.6 2.8 copy-start.2
  10.6 121.6 %all-gather.6.cloned.1.call-start = ((), (), s32[]{:S(2)}) async-start(), calls=%async_computation.7 | async-start | bytes 11206656 | tf_op jit(solution)/shard_map/all_gather | solution.py:25
  11.4 160.8 %all-gather.8.cloned.1.call-start = ((), (), s32[]{:S(2)}) async-start(), calls=%async_computation.8 | async-start | bytes 5603328 | tf_op jit(solution)/shard_map/all_gather | solution.py:25
  14.1 2.6 copy-start
  16.7 53.9 %copy-start.6 = (bf16[32,8,8,256]{3,1,2,0:T(8,128)(2,1)S(1)}, bf16[32,8,8,256]{3,1,2,0:T(8,128)(2,1)}, u32[]{:S(2)}) copy-start(bf16[32,8,8,256]{3,1,2,0:T(8,128)(2,1)} %copy.59) | copy-start | bytes 3145732
  70.6 61.6 %copy-start.5 = (bf16[32,8,8,256]{3,1,2,0:T(8,128)(2,1)S(1)}, bf16[32,8,8,256]{3,1,2,0:T(8,128)(2,1)}, u32[]{:S(2)}) copy-start(bf16[32,8,8,256]{3,1,2,0:T(8,128)(2,1)} %copy.60) | copy-start | bytes 3145732
  172.1 5.0 %copy-start.1 = (bf16[2,128,2432]{2,1,0:T(8,128)(2,1)S(1)}, bf16[2,128,2432]{2,1,0:T(8,128)(2,1)}, u32[]{:S(2)}) copy-start(bf16[2,128,2432]{2,1,0:T(8,128)(2,1)} %param.9) | copy-start | bytes 3735556
  177.0 21.2 %copy-start.9 = (s32[2,128]{1,0:T(2,128)S(1)}, s32[2,128]{1,0:T(2,128)}, u32[]{:S(2)}) copy-start(s32[2,128]{1,0:T(2,128)} %param.12) | copy-start | bytes 3076
  177.0 21.2 %copy-start.10 = (f32[2]{0:T(128)S(1)}, f32[2]{0:T(128)}, u32[]{:S(2)}) copy-start(f32[2]{0:T(128)} %param.13) | copy-start | bytes 28
  177.0 21.2 %copy-start.11 = (s32[2]{0:T(128)S(1)}, s32[2]{0:T(128)}, u32[]{:S(2)}) copy-start(s32[2]{0:T(128)} %param.11) | copy-start | bytes 28
  177.1 34.4 %copy-start.8 = (s32[2,128]{1,0:T(2,128)S(1)}, s32[2,128]{1,0:T(2,128)}, u32[]{:S(2)}) copy-start(s32[2,128]{1,0:T(2,128)} %param.10) | copy-start | bytes 3076
  178.7 19.4 %all-to-all-start = ((f32[32,4,256]{2,1,0:T(4,128)}), f32[32,4,256]{2,1,0:T(4,128)S(1)}, u32[]{:S(2)}, u32[]{:S(2)}) async-start(f32[32,4,256]{2,1,0:T(4,128)} %broadcast_in_dim.4), calls=%async_computation | async-start | bytes 262144 | tf_op jit(solution)/shard_map/all_to_all | solution.py:13
  198.9 8.9 %all-to-all-start.1 = ((f32[8,2,2,128]{3,2,1,0:T(2,128)}), f32[8,2,2,128]{3,2,1,0:T(2,128)S(1)}, u32[]{:S(2)}, u32[]{:S(2)}) async-start(f32[8,2,2,128]{3,2,1,0:T(2,128)} %broadcast_in_dim.5), calls=%async_computation.1 | async-start | bytes 32768 | tf_op jit(solution)/shard_map/all_to_all | solution.py:13
  204.6 48.9 %reduce-scatter.9.cloned.1.call-start = ((), (), s32[]{:S(2)}) async-start(), calls=%async_computation.11 | async-start | bytes 1179648 | tf_op jit(solution)/shard_map/reduce_scatter | solution.py:91
  211.4 5.9 %copy-start.7 = (f32[1,2,128]{2,0,1:T(1,128)}, f32[1,2,128]{2,0,1:T(1,128)S(1)}, u32[]{:S(2)}) copy-start(f32[1,2,128]{2,0,1:T(1,128)S(1)} %subtract_divide_fusion) | copy-start | bytes 3076
  212.3 1.0 copy-start.3
  217.3 1.6 copy-start.4
  218.7 78.0 %reduce-scatter.5.cloned.1.call-start = ((), (), s32[]{:S(2)}) async-start(), calls=%async_computation.9 | async-start | bytes 2359296 | tf_op jit(solution)/shard_map/reduce_scatter | solution.py:91
  226.3 113.8 %reduce-scatter.7.cloned.1.call-start = ((), (), s32[]{:S(2)}) async-start(), calls=%async_computation.10 | async-start | bytes 2359296 | tf_op jit(solution)/shard_map/reduce_scatter | solution.py:91
  233.8 130.1 %reduce-scatter.11.cloned.1.call-start = ((), (), s32[]{:S(2)}) async-start(), calls=%async_computation.12 | async-start | bytes 819200 | tf_op jit(solution)/shard_map/reduce_scatter | solution.py:94
Sparse Core Ops, SparseCore 0:
  10.7 59.7 all-gather.3
  73.0 59.1 all-gather.5
  134.0 38.0 all-gather.7
  218.8 34.6 reduce-scatter.8
  255.9 40.7 reduce-scatter.4
  299.1 40.9 reduce-scatter.6
  342.7 21.1 reduce-scatter.10

commit v2 on v1

v2 whole, which is shorter than its diff:
```python
import functools

import jax
import jax.numpy as jnp
from jax import lax
from jax.experimental import pallas as pl
from jax.experimental.pallas import tpu as pltpu
from jax.sharding import Mesh, PartitionSpec as P

SEQ = ("y", "c")
VOC = ("z", "x")
STRIP = 16
TILE = 128


def spread(value, axes):
    count = lax.axis_size(axes)
    return lax.all_to_all(jnp.broadcast_to(value[None], (count,) + value.shape), axes, 0, 0)


def head_kernel(
    blocks, state_ref, ref_ref, token_ref, head_hbm, logit_ref, stat_ref, back_ref, head, expo, turned, sems
):
    rows, columns = logit_ref.shape
    depth = head.shape[0] // blocks
    parts = back_ref.shape[0]
    piece = depth // parts

    def fetch(block):
        span = pl.ds(pl.multiple_of(block * depth, depth), depth)
        return pltpu.make_async_copy(head_hbm.at[span], head.at[span], sems.at[block])

    for block in range(blocks):
        fetch(block).start()
    logit_ref[...] = jnp.zeros_like(logit_ref)

    @pl.loop(0, blocks)
    def _(block):
        fetch(block).wait()
        span = pl.ds(pl.multiple_of(block * depth, depth), depth)
        logit_ref[...] += jnp.dot(
            state_ref[:, span], head[span, :], preferred_element_type=jnp.float32
        )

    column = lax.broadcasted_iota(jnp.int32, (STRIP, columns), 1)
    lane = lax.broadcasted_iota(jnp.int32, (STRIP, TILE), 1)

    @pl.loop(0, rows // STRIP)
    def _(strip):
        span = pl.ds(pl.multiple_of(strip * STRIP, STRIP), STRIP)
        values = logit_ref[span, :]
        top = jnp.max(values, axis=1, keepdims=True)
        powers = jnp.exp(values - top)
        total = jnp.sum(powers, axis=1, keepdims=True)
        gap = values - ref_ref[span, :].astype(jnp.float32)
        weighted = jnp.sum(powers * gap, axis=1, keepdims=True)
        hit = column == token_ref[span, :]
        own = jnp.sum(jnp.where(hit, values, 0.0), axis=1, keepdims=True)
        expo[span, :] = jnp.where(hit, 0.0, powers)
        stat_ref[span, :] = jnp.where(
            lane == 0, top, jnp.where(lane == 1, total, jnp.where(lane == 2, weighted, own))
        )

    @pl.loop(0, columns // TILE)
    def _(tile):
        span = pl.ds(pl.multiple_of(tile * TILE, TILE), TILE)
        turned[span, :] = expo[:, span].T.astype(jnp.bfloat16)

    @pl.loop(0, blocks)
    def _(block):
        span = pl.ds(pl.multiple_of(block * depth, depth), depth)
        result = jnp.dot(head[span, :], turned[...], preferred_element_type=jnp.float32)
        result = result.astype(jnp.bfloat16)
        target = pl.ds(pl.multiple_of(block * piece, piece), piece)
        for part in range(parts):
            back_ref[part, target, :] = result[part * piece : (part + 1) * piece]


def run_head(states, refs, tokens, head, blocks, parts):
    rows, width = states.shape
    columns = head.shape[1]
    vmem = pl.BlockSpec(memory_space=pltpu.VMEM)
    return pl.pallas_call(
        functools.partial(head_kernel, blocks),
        out_shape=(
            jax.ShapeDtypeStruct((rows, columns), jnp.float32),
            jax.ShapeDtypeStruct((rows, TILE), jnp.float32),
            jax.ShapeDtypeStruct((parts, width // parts, rows), jnp.bfloat16),
        ),
        in_specs=[vmem, vmem, vmem, pl.BlockSpec(memory_space=pl.ANY)],
        out_specs=(vmem, vmem, vmem),
        scratch_shapes=[
            pltpu.VMEM((width, columns), jnp.bfloat16),
            pltpu.VMEM((rows, columns), jnp.float32),
            pltpu.VMEM((columns, rows), jnp.bfloat16),
            pltpu.SemaphoreType.DMA((blocks,)),
        ],
        compiler_params=pltpu.CompilerParams(vmem_limit_bytes=56 << 20),
        cost_estimate=pl.CostEstimate(
            flops=4 * rows * width * columns,
            bytes_accessed=2 * width * columns + 8 * rows * columns,
            transcendentals=rows * columns,
        ),
        name="head",
    )(states, refs, tokens, head)


def token_columns(head_weight, token_ids, vocab_start):
    depth, vocab_dev = head_weight.shape
    seqs, zs, xs = lax.axis_size(SEQ), lax.axis_size("z"), lax.axis_size("x")
    rows = token_ids.size
    ids = spread(token_ids.reshape(rows), SEQ).reshape(seqs * rows, 1)
    column = vocab_start + lax.broadcasted_iota(jnp.int32, (1, vocab_dev), 1)
    onehot = (column == ids).astype(jnp.bfloat16)
    found = lax.dot_general(
        head_weight, onehot, (((1,), (1,)), ((), ())), preferred_element_type=jnp.float32
    ).astype(jnp.bfloat16)
    found = found.reshape(xs, depth // xs, seqs, rows).transpose(0, 2, 1, 3)
    found = lax.all_to_all(found, "x", 0, 0)
    found = jnp.sum(found.astype(jnp.float32), axis=0).astype(jnp.bfloat16)
    found = lax.all_to_all(found, "z", 0, 0)
    found = jnp.sum(found.astype(jnp.float32), axis=0).astype(jnp.bfloat16)
    pairs = [(i * zs + j, j * zs + i) for i in range(seqs) for j in range(zs)]
    return lax.ppermute(found, SEQ + ("z",), pairs)


def per_device(hidden, head_weight, ref_logits, token_ids, end_pos, loss_mask, scores):
    batch, segment, width = hidden.shape
    rows = batch * segment
    vocab_dev = head_weight.shape[1]
    seqs, xs = lax.axis_size(SEQ), lax.axis_size("x")
    seq_index = lax.axis_index(SEQ)
    seq_start = seq_index * segment
    vocab_start = lax.axis_index(VOC) * vocab_dev

    whole_head = lax.all_gather(head_weight, SEQ, axis=0, tiled=True)
    own_columns = token_columns(head_weight, token_ids, vocab_start)

    refs = ref_logits.reshape(rows, vocab_dev)
    wide = refs.astype(jnp.float32)
    ref_top = jnp.max(wide, axis=1)
    ref_lse = ref_top + jnp.log(jnp.sum(jnp.exp(wide - ref_top[:, None]), axis=1))
    states, own_columns, ref_lse = lax.optimization_barrier(
        (hidden.reshape(rows, width), own_columns, ref_lse)
    )
    tokens = token_ids.reshape(rows, 1)
    logits, local, back = run_head(states, refs, tokens - vocab_start, whole_head, seqs, xs)

    stats = jnp.concatenate([local[:, :4].T, ref_lse[None]], axis=0)
    stats = spread(stats, VOC)
    back = lax.all_to_all(back, "x", 0, 0)

    tops = stats[:, 0]
    top_policy = jnp.max(tops, axis=0)
    scale = jnp.exp(tops - top_policy[None])
    total = jnp.sum(stats[:, 1] * scale, axis=0)
    weighted = jnp.sum(stats[:, 2] * scale, axis=0)
    own_logit = jnp.sum(stats[:, 3], axis=0)
    top_ref = jnp.max(stats[:, 4], axis=0)
    lse_ref = top_ref + jnp.log(jnp.sum(jnp.exp(stats[:, 4] - top_ref[None]), axis=0))
    lse_policy = top_policy + jnp.log(total)
    kl_value = (weighted / total - lse_policy + lse_ref).reshape(batch, segment)

    z_start = lax.axis_index("z") * xs
    share = lax.dynamic_slice_in_dim(scale, z_start, xs, 0) / total[None]
    back = back.reshape(xs, seqs, -1, rows)
    back = jnp.sum(back.astype(jnp.float32) * share[:, None, None, :], axis=0).astype(jnp.bfloat16)
    back = lax.all_to_all(back, "z", 0, 0)
    back = jnp.sum(back.astype(jnp.float32), axis=0)

    position = seq_start + lax.broadcasted_iota(jnp.int32, (1, segment), 1)
    live = ((loss_mask == 1) & (position <= end_pos[:, None])).astype(jnp.float32)
    at_end = (position == end_pos[:, None]).astype(jnp.float32)
    reward = -0.01 * kl_value * live + scores[:, None] * at_end
    both = spread(jnp.stack([reward, live]), SEQ)
    rewards, lives = both[:, 0], both[:, 1]
    upper = (
        lax.broadcasted_iota(jnp.int32, (segment, segment), 0)
        >= lax.broadcasted_iota(jnp.int32, (segment, segment), 1)
    ).astype(jnp.float32)
    suffix = jnp.dot(
        rewards.reshape(seqs * batch, segment), upper, precision=lax.Precision.HIGHEST
    ).reshape(seqs, batch, segment)
    totals = jnp.sum(rewards, axis=2)
    later = (
        lax.broadcasted_iota(jnp.int32, (seqs, seqs, 1), 1)
        > lax.broadcasted_iota(jnp.int32, (seqs, seqs, 1), 0)
    ).astype(jnp.float32)
    carried = jnp.sum(later * totals[None], axis=1)
    returns_all = suffix + carried[:, :, None]
    count = jnp.maximum(jnp.sum(lives), 1.0)
    mean = jnp.sum(lives * returns_all) / count
    var = jnp.sum(lives * returns_all * returns_all) / count - mean * mean
    returns = lax.dynamic_index_in_dim(returns_all, seq_index, 0, keepdims=False)
    advantages = (returns - mean) / jnp.sqrt(var + 1e-05)
    factor = (live * advantages / count).reshape(rows)

    prob = jnp.exp(logits - lse_policy[:, None])
    column = vocab_start + lax.broadcasted_iota(jnp.int32, (1, vocab_dev), 1)
    onehot = (column == tokens).astype(jnp.float32)
    logit_grad = (factor[:, None] * (prob - onehot)).astype(jnp.bfloat16)

    own_grad = (factor * (jnp.exp(own_logit - lse_policy) - 1.0)).astype(jnp.bfloat16)
    hidden_grad = factor[None] * back + own_grad.astype(jnp.float32)[None] * own_columns.astype(jnp.float32)
    hidden_grad = hidden_grad.T.reshape(batch, segment, -1).astype(jnp.bfloat16)
    return (logit_grad.reshape(batch, segment, vocab_dev), hidden_grad, advantages)


def solution(mesh):
    chips = mesh.devices.reshape(4, 2, 8, 4)
    fine = Mesh(chips, ("y", "c", "z", "x"))
    in_specs = (
        P(None, SEQ, None),
        P(SEQ, VOC),
        P(None, SEQ, VOC),
        P(None, SEQ),
        P(),
        P(None, SEQ),
        P(),
    )
    out_specs = (P(None, SEQ, VOC), P(None, SEQ, VOC), P(None, SEQ))
    return jax.shard_map(
        per_device, mesh=fine, in_specs=in_specs, out_specs=out_specs, check_vma=False
    )
```

time: 375 us -> 268 us (0.71)
  waiting for transfers between devices: 279 us -> 112 us
  blocking collectives: 0 us -> 42.4 us
  Pallas kernels: 0 us -> 28.6 us
  matrix products: 37.4 us -> 10.2 us
  starting transfers between devices: 16.2 us -> 37.1 us
  local copies, waits for them, and re-layouts: 16 us -> 8.58 us
    reduce_scatter x4 -> x0, waiting for transfers between devices: 128 us -> none  [the longest x3 106 us: per_device(): pieces.append(lax.psum_scatter(part, 'z', scatter_dimension=0, tiled=False))]
    all_gather x3 -> x1, waiting for transfers between devices: 138 us -> 29.8 us  [per_device(): whole_head = lax.all_gather(head_weight, SEQ, axis=0, tiled=True)]
    all_to_all x0 -> x3, waiting for transfers between devices: none -> 60.9 us  [the longest x1 29.3 us: per_device(): back = lax.all_to_all(back, 'x', 0, 0)]
    all_to_all x0 -> x2, blocking collectives: none -> 42.4 us  [the longest x1 34.5 us: token_columns(): found = lax.all_to_all(found, 'x', 0, 0)]
    pallas_call x0 -> x1, Pallas kernels: none -> 28.6 us  [run_head(): pl.pallas_call(functools.partial(head_kernel, blocks), out_shape=(jax.Sha...]
    dot_general x6 -> x1, matrix products: 36.6 us -> 9.47 us  [token_columns(): lax.dot_general(head_weight, onehot, (((1,), (1,)), ((), ())), preferred_...]
    all_to_all x0 -> x3, starting transfers between devices: none -> 17.6 us  [the longest x1 8.44 us: token_columns(): found = lax.all_to_all(found, 'z', 0, 0)]
    ppermute x0 -> x1, waiting for transfers between devices: none -> 6.23 us  [token_columns(): return lax.ppermute(found, SEQ + ('z',), pairs)]
  transfers between devices with their start and end apart: 9 -> 7, of which waited for: 9 -> 7; matrix products, arithmetic and copies ran while one was open for 10% -> 9% of each run, Pallas kernels for 0% -> 0%
where the time goes in v2:
time: 268 us; the launch traced here: 264 us
  waiting for transfers between devices  112 us (42%)
  blocking collectives  42.4 us (16%)
  starting transfers between devices  37.1 us (14%)
  Pallas kernels  28.6 us (11%)
  between operations  16.2 us (6%)
  matrix products  10.2 us (4%)
  local copies, waits for them, and re-layouts  8.58 us (3%)
  other arithmetic  8.53 us (3%)
    all_to_all x1, blocking collectives, token_columns(): found = lax.all_to_all(found, 'x', 0, 0)  34.5 us
    all_gather x1, waiting for transfers between devices, per_device(): whole_head = lax.all_gather(head_weight, SEQ, axis=0, tiled=True)  29.8 us
    all_to_all x1, waiting for transfers between devices, per_device(): back = lax.all_to_all(back, 'x', 0, 0)  29.3 us
    pallas_call x1, Pallas kernels, run_head(): pl.pallas_call(functools.partial(head_kernel, blocks), out_shape=(jax.Sha...  28.6 us
    all_to_all x1, waiting for transfers between devices, token_columns(): found = lax.all_to_all(found, 'z', 0, 0)  18.3 us
    all_to_all x2, starting transfers between devices, spread(): lax.all_to_all(jnp.broadcast_to(value[None], (count,) + value.shape), axe...  15.6 us
    all_to_all x2, waiting for transfers between devices, spread(): lax.all_to_all(jnp.broadcast_to(value[None], (count,) + value.shape), axe...  14.9 us
    all_to_all x1, waiting for transfers between devices, per_device(): back = lax.all_to_all(back, 'z', 0, 0)  13.2 us
  transfers between devices with their start and end apart: 7, of which 7 were waited for; matrix products, arithmetic and copies ran while one was open for 9% of the time, Pallas kernels for 0%

profile of v2, /device:TPU:30, one launch (start us, length us, event | category | flops | bytes accessed | tf_op | source)
XLA Modules:
  0.0 264.1 jit_solution(13903276195520366646)
XLA Ops:
  7.2 0.7 all-gather.2.cloned.1.call-update
  8.0 0.6 broadcast_in_dim.11
  8.6 4.7 %all-to-all-start = ((s32[8,1,256]{2,1,0:T(1,128)}), s32[8,1,256]{2,1,0:T(1,128)S(1)}, u32[]{:S(2)}, u32[]{:S(2)}) async-start(s32[8,1,256]{2,1,0:T(1,128)} %broadcast_in_dim.11), calls=%async_computation | async-start | bytes 16384 | tf_op jit(solution)/shard_map/all_to_all | solution.py:18
  13.3 3.2 %all-to-all-done = s32[8,1,256]{2,1,0:T(1,128)S(1)} async-done(((s32[8,1,256]{2,1,0:T(1,128)}), s32[8,1,256]{2,1,0:T(1,128)S(1)}, u32[]{:S(2)}, u32[]{:S(2)}) %all-to-all-start) | async-done | bytes 8224 | tf_op jit(solution)/shard_map/all_to_all | solution.py:18
  16.5 9.5 %fusion.7 = bf16[640,2048]{0,1:T(8,128)(2,1)} fusion(bf16[640,2432]{1,0:T(8,128)(2,1)S(1)} %copy-done.1, s32[2432]{0:T(1024)S(1)} %iota_add_fusion, s32[2048]{0:T(1024)S(1)} %bitcast.87), kind=kOutput, calls=%fused_computation.6 | convolution fusion | flops 6381633536 | bytes 5752320 | tf_op jit(solution)/shard_map/dot_general | solution.py:115
  26.0 3.2 %copy.35 = bf16[640,2048]{1,0:T(8,128)(2,1)S(1)} copy(bf16[640,2048]{0,1:T(8,128)(2,1)} %fusion.7) | data formatting | bytes 5242880 | tf_op jit(solution)/shard_map/convert_element_type | solution.py:117
  29.3 0.9 copy.54
  30.3 34.5 %all_to_all.36 = bf16[4,8,160,256]{3,1,2,0:T(8,128)(2,1)S(1)} all-to-all(bf16[4,8,160,256]{3,1,2,0:T(8,128)(2,1)S(1)} %bitcast_bitcast_fusion), channel_id=1, replica_groups=mesh['y'=4,'c'=2,'z'=8,'x'=4] {'x'}, dimensions={0} | all-to-all | bytes 5242880 | tf_op jit(solution)/shard_map/all_to_all | solution.py:119
  64.8 0.8 reduce_sum.132
  65.6 1.0 copy.36
  66.6 8.4 %all-to-all-start.2 = ((bf16[8,160,256]{2,1,0:T(8,128)(2,1)}), bf16[8,160,256]{2,1,0:T(8,128)(2,1)S(1)}, u32[]{:S(2)}, u32[]{:S(2)}) async-start(bf16[8,160,256]{2,1,0:T(8,128)(2,1)} %copy.36), calls=%async_computation.2 | async-start | bytes 1310720 | tf_op jit(solution)/shard_map/all_to_all | solution.py:121
  75.3 0.6 exponential_reduce_fusion
  75.9 18.3 %all-to-all-done.2 = bf16[8,160,256]{2,1,0:T(8,128)(2,1)S(1)} async-done(((bf16[8,160,256]{2,1,0:T(8,128)(2,1)}), bf16[8,160,256]{2,1,0:T(8,128)(2,1)S(1)}, u32[]{:S(2)}, u32[]{:S(2)}) %all-to-all-start.2) | async-done | bytes 655392 | tf_op jit(solution)/shard_map/all_to_all | solution.py:121
  94.3 3.9 %collective-permute-start = (bf16[160,256]{1,0:T(8,128)(2,1)S(1)}, bf16[160,256]{1,0:T(8,128)(2,1)S(1)}, u32[]{:S(2)}, u32[]{:S(2)}) collective-permute-start(bf16[160,256]{1,0:T(8,128)(2,1)S(1)} %reduce_sum.133), channel_id=1, source_target_pairs={{0,0},{4,32},{8,64},{12,96},{16,128},{20,160},{24,192},{28,224},{3... | collective-permute-start | bytes 245768 | tf_op jit(solution)/shard_map/ppermute | solution.py:124
  98.2 0.8 copy.37.token_ref
  99.0 6.2 %collective-permute-done = bf16[160,256]{1,0:T(8,128)(2,1)S(1)} collective-permute-done((bf16[160,256]{1,0:T(8,128)(2,1)S(1)}, bf16[160,256]{1,0:T(8,128)(2,1)S(1)}, u32[]{:S(2)}, u32[]{:S(2)}) %collective-permute-start) | collective-permute-done | bytes 81952 | tf_op jit(solution)/shard_map/ppermute | solution.py:124
  105.2 29.8 %all-gather.2.cloned.1.call-done.head_hbm = bf16[5120,2432]{1,0:T(8,128)(2,1)} async-done(((bf16[640,2432]{1,0:T(8,128)(2,1)}), bf16[5120,2432]{1,0:T(8,128)(2,1)}) %all-gather.2.cloned.1.call-update) | async-done | bytes 24903696 | tf_op jit(solution)/shard_map/all_gather | solution.py:136
  135.0 28.6 %head.1 = (f32[256,2432]{1,0:T(8,128)}, f32[256,128]{1,0:T(8,128)}, bf16[4,1280,256]{2,1,0:T(8,128)(2,1)}) custom-call(bf16[256,5120]{1,0:T(8,128)(2,1)} %bitcast.92, bf16[256,2432]{1,0:T(8,128)(2,1)} %bitcast.83, s32[256,1]{1,0:T(8,128)} %copy.37.token_ref, bf16[5120,2432]{1,0:T(8,128)(2,1)} %all-gather.2.cloned.1.call-done.head_hbm), custom_call_target="tpu_custom_call" | custom-call | flops 12750684160 | bytes 29884416 | tf_op jit(solution)/shard_map/head/pallas_call | solution.py:83
  163.6 0.9 slice_bitcast_fusion
  164.6 0.7 broadcast_in_dim.13
  165.4 10.9 %all-to-all-start.3 = ((f32[32,5,256]{2,1,0:T(8,128)}), f32[32,5,256]{2,1,0:T(8,128)S(1)}, u32[]{:S(2)}, u32[]{:S(2)}) async-start(f32[32,5,256]{2,1,0:T(8,128)} %broadcast_in_dim.13), calls=%async_computation.3 | async-start | bytes 524288 | tf_op jit(solution)/shard_map/all_to_all | solution.py:18
  176.3 11.6 %all-to-all-done.3 = f32[32,5,256]{2,1,0:T(8,128)S(1)} async-done(((f32[32,5,256]{2,1,0:T(8,128)}), f32[32,5,256]{2,1,0:T(8,128)S(1)}, u32[]{:S(2)}, u32[]{:S(2)}) %all-to-all-start.3) | async-done | bytes 163872 | tf_op jit(solution)/shard_map/all_to_all | solution.py:18
  188.3 7.9 %all_to_all.37 = f32[8,2,2,128]{3,2,1,0:T(2,128)S(1)} all-to-all(f32[8,2,2,128]{3,2,1,0:T(2,128)S(1)} %broadcast_in_dim.14), channel_id=1, replica_groups=mesh['y'=4,'c'=2,'z'=8,'x'=4] {'y','c'}, dimensions={0} | all-to-all | bytes 32768 | tf_op jit(solution)/shard_map/all_to_all | solution.py:18
  196.2 5.6 %all-to-all-start.5 = ((bf16[4,1280,256]{2,1,0:T(8,128)(2,1)}), bf16[4,1280,256]{2,1,0:T(8,128)(2,1)S(1)}, u32[]{:S(2)}, u32[]{:S(2)}) async-start(bf16[4,1280,256]{2,1,0:T(8,128)(2,1)} %get-tuple-element.13), calls=%async_computation.5 | async-start | bytes 5242880 | tf_op jit(solution)/shard_map/all_to_all | solution.py:151
  201.8 0.6 slice_reduce_fusion.1
  202.6 29.3 %all-to-all-done.5 = bf16[4,1280,256]{2,1,0:T(8,128)(2,1)S(1)} async-done(((bf16[4,1280,256]{2,1,0:T(8,128)(2,1)}), bf16[4,1280,256]{2,1,0:T(8,128)(2,1)S(1)}, u32[]{:S(2)}, u32[]{:S(2)}) %all-to-all-start.5) | async-done | bytes 2621472 | tf_op jit(solution)/shard_map/all_to_all | solution.py:151
  231.9 1.5 multiply_reduce_fusion
  233.4 3.5 %all-to-all-start.6 = ((bf16[8,160,256]{2,1,0:T(8,128)(2,1)}), bf16[8,160,256]{2,1,0:T(8,128)(2,1)S(1)}, u32[]{:S(2)}, u32[]{:S(2)}) async-start(bf16[8,160,256]{2,1,0:T(8,128)(2,1)} %bitcast.21), calls=%async_computation.6 | async-start | bytes 1310720 | tf_op jit(solution)/shard_map/all_to_all | solution.py:168
  237.0 0.8 fusion.21
  239.8 3.5 %multiply_convert_fusion = bf16[256,2432]{1,0:T(8,128)(2,1)} fusion(f32[256,2432]{1,0:T(8,128)} %get-tuple-element.12, s32[2432]{0:T(1024)S(1)} %iota_add_fusion, f32[256]{0:T(256)S(1)} %get-tuple-element.40, f32[256]{0:T(256)S(1)} %get-tuple-element.37, s32[256]{0:T(256)S(1)} %bitcast.86), kind=kLoop, calls=%fused_computation.8 | loop fusion | flops 3735552 | bytes 3748352 | tf_op jit(solution)/shard_map/convert_element_type | solution.py:201
  243.3 13.2 %all-to-all-done.6 = bf16[8,160,256]{2,1,0:T(8,128)(2,1)S(1)} async-done(((bf16[8,160,256]{2,1,0:T(8,128)(2,1)}), bf16[8,160,256]{2,1,0:T(8,128)(2,1)S(1)}, u32[]{:S(2)}, u32[]{:S(2)}) %all-to-all-start.6) | async-done | bytes 655392 | tf_op jit(solution)/shard_map/all_to_all | solution.py:168
  256.6 0.7 copy_bitcast_fusion
  (38 shorter events, 1.4 us)
Async XLA Ops:
  7.2 9.4 %copy-start.1 = (bf16[640,2432]{1,0:T(8,128)(2,1)S(1)}, bf16[640,2432]{1,0:T(8,128)(2,1)}, u32[]{:S(2)}) copy-start(bf16[640,2432]{1,0:T(8,128)(2,1)} %param.8) | copy-start | bytes 9338884
  7.2 0.8 copy-start.2
  7.2 127.8 %all-gather.2.cloned.1.call-start = ((), (), s32[]{:S(2)}) async-start(), calls=%async_computation.7 | async-start | bytes 28016640 | tf_op jit(solution)/shard_map/all_gather | solution.py:136
  8.6 7.9 %all-to-all-start = ((s32[8,1,256]{2,1,0:T(1,128)}), s32[8,1,256]{2,1,0:T(1,128)S(1)}, u32[]{:S(2)}, u32[]{:S(2)}) async-start(s32[8,1,256]{2,1,0:T(1,128)} %broadcast_in_dim.11), calls=%async_computation | async-start | bytes 16384 | tf_op jit(solution)/shard_map/all_to_all | solution.py:18
  65.6 9.4 %copy-start = (bf16[2,128,2432]{2,1,0:T(8,128)(2,1)S(1)}, bf16[2,128,2432]{2,1,0:T(8,128)(2,1)}, u32[]{:S(2)}) copy-start(bf16[2,128,2432]{2,1,0:T(8,128)(2,1)} %param.9) | copy-start | bytes 3735556
  66.6 27.6 %all-to-all-start.2 = ((bf16[8,160,256]{2,1,0:T(8,128)(2,1)}), bf16[8,160,256]{2,1,0:T(8,128)(2,1)S(1)}, u32[]{:S(2)}, u32[]{:S(2)}) async-start(bf16[8,160,256]{2,1,0:T(8,128)(2,1)} %copy.36), calls=%async_computation.2 | async-start | bytes 1310720 | tf_op jit(solution)/shard_map/all_to_all | solution.py:121
  94.3 10.9 %collective-permute-start = (bf16[160,256]{1,0:T(8,128)(2,1)S(1)}, bf16[160,256]{1,0:T(8,128)(2,1)S(1)}, u32[]{:S(2)}, u32[]{:S(2)}) collective-permute-start(bf16[160,256]{1,0:T(8,128)(2,1)S(1)} %reduce_sum.133), channel_id=1, source_target_pairs={{0,0},{4,32},{8,64},{12,96},{16,128},{20,160},{24,192},{28,224},{3... | collective-permute-start | bytes 245768 | tf_op jit(solution)/shard_map/ppermute | solution.py:124
  135.0 53.2 %copy-start.4 = (s32[2,128]{1,0:T(2,128)S(1)}, s32[2,128]{1,0:T(2,128)}, u32[]{:S(2)}) copy-start(s32[2,128]{1,0:T(2,128)} %param.12) | copy-start | bytes 3076
  135.0 53.2 %copy-start.5 = (f32[2]{0:T(128)S(1)}, f32[2]{0:T(128)}, u32[]{:S(2)}) copy-start(f32[2]{0:T(128)} %param.13) | copy-start | bytes 28
  135.0 53.2 %copy-start.6 = (s32[2]{0:T(128)S(1)}, s32[2]{0:T(128)}, u32[]{:S(2)}) copy-start(s32[2]{0:T(128)} %param.11) | copy-start | bytes 28
  165.4 22.6 %all-to-all-start.3 = ((f32[32,5,256]{2,1,0:T(8,128)}), f32[32,5,256]{2,1,0:T(8,128)S(1)}, u32[]{:S(2)}, u32[]{:S(2)}) async-start(f32[32,5,256]{2,1,0:T(8,128)} %broadcast_in_dim.13), calls=%async_computation.3 | async-start | bytes 524288 | tf_op jit(solution)/shard_map/all_to_all | solution.py:18
  196.2 35.8 %all-to-all-start.5 = ((bf16[4,1280,256]{2,1,0:T(8,128)(2,1)}), bf16[4,1280,256]{2,1,0:T(8,128)(2,1)S(1)}, u32[]{:S(2)}, u32[]{:S(2)}) async-start(bf16[4,1280,256]{2,1,0:T(8,128)(2,1)} %get-tuple-element.13), calls=%async_computation.5 | async-start | bytes 5242880 | tf_op jit(solution)/shard_map/all_to_all | solution.py:151
  233.4 23.1 %all-to-all-start.6 = ((bf16[8,160,256]{2,1,0:T(8,128)(2,1)}), bf16[8,160,256]{2,1,0:T(8,128)(2,1)S(1)}, u32[]{:S(2)}, u32[]{:S(2)}) async-start(bf16[8,160,256]{2,1,0:T(8,128)(2,1)} %bitcast.21), calls=%async_computation.6 | async-start | bytes 1310720 | tf_op jit(solution)/shard_map/all_to_all | solution.py:168
  239.7 17.6 %copy-start.3 = (f32[1,2,128]{2,0,1:T(1,128)}, f32[1,2,128]{2,0,1:T(1,128)S(1)}, u32[]{:S(2)}) copy-start(f32[1,2,128]{2,0,1:T(1,128)S(1)} %subtract_divide_fusion) | copy-start | bytes 3076
Sparse Core Ops, SparseCore 0:
  9.8 125.0 all-gather.1

commit v3 on v2

--- a/solution.py
+++ b/solution.py
@@ -9,8 +9,9 @@
 
 SEQ = ("y", "c")
 VOC = ("z", "x")
-STRIP = 16
 TILE = 128
+SUB = 8
+WIDE = 8
 
 
 def spread(value, axes):
@@ -18,82 +19,115 @@
     return lax.all_to_all(jnp.broadcast_to(value[None], (count,) + value.shape), axes, 0, 0)
 
 
-def head_kernel(
-    blocks, state_ref, ref_ref, token_ref, head_hbm, logit_ref, stat_ref, back_ref, head, expo, turned, sems
-):
-    rows, columns = logit_ref.shape
-    depth = head.shape[0] // blocks
-    parts = back_ref.shape[0]
+def head_kernel(blocks, place_ref, state_hbm, ref_hbm, token_ref, lse_ref, head_hbm,
+                logit_hbm, stat_ref, back0, back1, back2, back3,
+                state, refs, head, logit, flipped, turned, result, sems, outsem):
+    rows, columns = logit.shape
+    width = head.shape[0]
+    depth = width // blocks
+    backs = (back0, back1, back2, back3)
+    parts = len(backs)
     piece = depth // parts
-
-    def fetch(block):
-        span = pl.ds(pl.multiple_of(block * depth, depth), depth)
-        return pltpu.make_async_copy(head_hbm.at[span], head.at[span], sems.at[block])
-
-    for block in range(blocks):
-        fetch(block).start()
-    logit_ref[...] = jnp.zeros_like(logit_ref)
-
-    @pl.loop(0, blocks)
-    def _(block):
-        fetch(block).wait()
-        span = pl.ds(pl.multiple_of(block * depth, depth), depth)
-        logit_ref[...] += jnp.dot(
-            state_ref[:, span], head[span, :], preferred_element_type=jnp.float32
+    wide = WIDE * TILE
+    tiles = columns // wide
+    tail = columns - tiles * wide
+
+    def fetch(tile, size):
+        span = pl.ds(pl.multiple_of(tile * wide, wide), size)
+        return pltpu.make_async_copy(head_hbm.at[:, span], head.at[:, span], sems.at[tile])
+
+    get_state = pltpu.make_async_copy(state_hbm, state, outsem.at[0])
+    get_refs = pltpu.make_async_copy(ref_hbm, refs, outsem.at[1])
+    get_state.start()
+    for tile in range(tiles):
+        fetch(tile, wide).start()
+    if tail:
+        fetch(tiles, tail).start()
+    get_refs.start()
+    get_state.wait()
+
+    def forward(tile, size, best):
+        fetch(tile, size).wait()
+        span = pl.ds(pl.multiple_of(tile * wide, wide), size)
+        values = jnp.dot(state[...], head[:, span], preferred_element_type=jnp.float32)
+        logit[:, span] = values
+        values = values.T
+        flipped[span, :] = values
+        return jnp.maximum(best, jnp.max(values.reshape(size // SUB, SUB, rows), axis=0))
+
+    best = jnp.full((SUB, rows), -jnp.inf, jnp.float32)
+    best = lax.fori_loop(0, tiles, lambda tile, best: forward(tile, wide, best), best)
+    if tail:
+        best = forward(tiles, tail, best)
+    top = jnp.max(best, axis=0, keepdims=True)
+    put_logit = pltpu.make_async_copy(logit, logit_hbm, outsem.at[0])
+    put_logit.start()
+    get_refs.wait()
+
+    column = lax.broadcasted_iota(jnp.int32, (TILE, rows), 0)
+
+    def fold(terms):
+        return jnp.sum(terms.reshape(TILE // SUB, SUB, rows), axis=0)
+
+    def strip(tile, sums):
+        span = pl.ds(pl.multiple_of(tile * TILE, TILE), TILE)
+        values = flipped[span, :]
+        powers = jnp.exp(values - top)
+        gap = values - refs[span, :].astype(jnp.float32)
+        hit = column == token_ref[...] - tile * TILE
+        turned[span, :] = jnp.where(hit, 0.0, powers).astype(jnp.bfloat16)
+        return (
+            sums[0] + fold(powers),
+            sums[1] + fold(powers * gap),
+            sums[2] + fold(jnp.where(hit, values, 0.0)),
         )
 
-    column = lax.broadcasted_iota(jnp.int32, (STRIP, columns), 1)
-    lane = lax.broadcasted_iota(jnp.int32, (STRIP, TILE), 1)
-
-    @pl.loop(0, rows // STRIP)
-    def _(strip):
-        span = pl.ds(pl.multiple_of(strip * STRIP, STRIP), STRIP)
-        values = logit_ref[span, :]
-        top = jnp.max(values, axis=1, keepdims=True)
-        powers = jnp.exp(values - top)
-        total = jnp.sum(powers, axis=1, keepdims=True)
-        gap = values - ref_ref[span, :].astype(jnp.float32)
-        weighted = jnp.sum(powers * gap, axis=1, keepdims=True)
-        hit = column == token_ref[span, :]
-        own = jnp.sum(jnp.where(hit, values, 0.0), axis=1, keepdims=True)
-        expo[span, :] = jnp.where(hit, 0.0, powers)
-        stat_ref[span, :] = jnp.where(
-            lane == 0, top, jnp.where(lane == 1, total, jnp.where(lane == 2, weighted, own))
-        )
-
-    @pl.loop(0, columns // TILE)
-    def _(tile):
-        span = pl.ds(pl.multiple_of(tile * TILE, TILE), TILE)
-        turned[span, :] = expo[:, span].T.astype(jnp.bfloat16)
+    zero = jnp.zeros((SUB, rows), jnp.float32)
+    sums = lax.fori_loop(0, columns // TILE, strip, (zero, zero, zero))
+    total, weighted, own = (jnp.sum(term, axis=0, keepdims=True) for term in sums)
+    stats = jnp.concatenate([top, total, weighted, own, lse_ref[...], zero[:3]], axis=0)
+    for device in range(stat_ref.shape[0]):
+        stat_ref[device] = stats
+
+    place = place_ref[0]
 
     @pl.loop(0, blocks)
     def _(block):
         span = pl.ds(pl.multiple_of(block * depth, depth), depth)
-        result = jnp.dot(head[span, :], turned[...], preferred_element_type=jnp.float32)
-        result = result.astype(jnp.bfloat16)
+        result[...] = jnp.dot(
+            head[span, :], turned[...], preferred_element_type=jnp.float32
+        ).astype(jnp.bfloat16)
         target = pl.ds(pl.multiple_of(block * piece, piece), piece)
-        for part in range(parts):
-            back_ref[part, target, :] = result[part * piece : (part + 1) * piece]
-
-
-def run_head(states, refs, tokens, head, blocks, parts):
+        for step, back in enumerate(backs):
+            source = lax.rem(place + step, parts) * piece
+            back[target, :] = result[pl.ds(pl.multiple_of(source, piece), piece), :]
+
+    put_logit.wait()
+
+def run_head(states, refs, tokens, ref_lse, place, head, blocks, parts, peers):
     rows, width = states.shape
     columns = head.shape[1]
     vmem = pl.BlockSpec(memory_space=pltpu.VMEM)
+    hbm = pl.BlockSpec(memory_space=pl.ANY)
+    back = jax.ShapeDtypeStruct((width // parts, rows), jnp.bfloat16)
     return pl.pallas_call(
         functools.partial(head_kernel, blocks),
         out_shape=(
             jax.ShapeDtypeStruct((rows, columns), jnp.float32),
-            jax.ShapeDtypeStruct((rows, TILE), jnp.float32),
-            jax.ShapeDtypeStruct((parts, width // parts, rows), jnp.bfloat16),
-        ),
-        in_specs=[vmem, vmem, vmem, pl.BlockSpec(memory_space=pl.ANY)],
-        out_specs=(vmem, vmem, vmem),
+            jax.ShapeDtypeStruct((peers, SUB, rows), jnp.float32),
+        ) + (back,) * parts,
+        in_specs=[pl.BlockSpec(memory_space=pltpu.SMEM), hbm, hbm, vmem, vmem, hbm],
+        out_specs=(hbm,) + (vmem,) * (1 + parts),
         scratch_shapes=[
+            pltpu.VMEM((rows, width), jnp.bfloat16),
+            pltpu.VMEM((columns, rows), jnp.bfloat16),
             pltpu.VMEM((width, columns), jnp.bfloat16),
             pltpu.VMEM((rows, columns), jnp.float32),
+            pltpu.VMEM((columns, rows), jnp.float32),
             pltpu.VMEM((columns, rows), jnp.bfloat16),
-            pltpu.SemaphoreType.DMA((blocks,)),
+            pltpu.VMEM((width // blocks, rows), jnp.bfloat16),
+            pltpu.SemaphoreType.DMA((-(-columns // (WIDE * TILE)),)),
+            pltpu.SemaphoreType.DMA((2,)),
         ],
         compiler_params=pltpu.CompilerParams(vmem_limit_bytes=56 << 20),
         cost_estimate=pl.CostEstimate(
@@ -102,7 +136,7 @@
             transcendentals=rows * columns,
         ),
         name="head",
-    )(states, refs, tokens, head)
+    )(place, states, refs, tokens, ref_lse, head)
 
 
 def token_columns(head_weight, token_ids, vocab_start):
@@ -140,15 +174,28 @@
     wide = refs.astype(jnp.float32)
     ref_top = jnp.max(wide, axis=1)
     ref_lse = ref_top + jnp.log(jnp.sum(jnp.exp(wide - ref_top[:, None]), axis=1))
-    states, own_columns, ref_lse = lax.optimization_barrier(
-        (hidden.reshape(rows, width), own_columns, ref_lse)
+    turned_refs = refs.T
+    states, turned_refs, own_columns, ref_lse = lax.optimization_barrier(
+        (hidden.reshape(rows, width), turned_refs, own_columns, ref_lse)
     )
     tokens = token_ids.reshape(rows, 1)
-    logits, local, back = run_head(states, refs, tokens - vocab_start, whole_head, seqs, xs)
-
-    stats = jnp.concatenate([local[:, :4].T, ref_lse[None]], axis=0)
-    stats = spread(stats, VOC)
-    back = lax.all_to_all(back, "x", 0, 0)
+    x_index = lax.axis_index("x")
+    logits, stats, *backs = run_head(
+        states,
+        turned_refs,
+        (tokens - vocab_start).reshape(1, rows),
+        ref_lse[None],
+        x_index.reshape(1),
+        whole_head,
+        seqs,
+        xs,
+        lax.axis_size(VOC),
+    )
+    backs = [
+        part if step == 0 else lax.ppermute(part, "x", [(i, (i + step) % xs) for i in range(xs)])
+        for step, part in enumerate(backs)
+    ]
+    stats = lax.all_to_all(stats, VOC, 0, 0)
 
     tops = stats[:, 0]
     top_policy = jnp.max(tops, axis=0)
@@ -162,9 +209,12 @@
     kl_value = (weighted / total - lse_policy + lse_ref).reshape(batch, segment)
 
     z_start = lax.axis_index("z") * xs
-    share = lax.dynamic_slice_in_dim(scale, z_start, xs, 0) / total[None]
-    back = back.reshape(xs, seqs, -1, rows)
-    back = jnp.sum(back.astype(jnp.float32) * share[:, None, None, :], axis=0).astype(jnp.bfloat16)
+    back = 0.0
+    for step, part in enumerate(backs):
+        sender = z_start + lax.rem(x_index + xs - step, xs)
+        share = lax.dynamic_index_in_dim(scale, sender, 0, keepdims=True) / total[None]
+        back = back + part.astype(jnp.float32) * share
+    back = back.astype(jnp.bfloat16).reshape(seqs, -1, rows)
     back = lax.all_to_all(back, "z", 0, 0)
     back = jnp.sum(back.astype(jnp.float32), axis=0)
 

time: 268 us -> 244 us (0.910)
  waiting for transfers between devices: 112 us -> 95.5 us
  blocking collectives: 42.4 us -> 34.6 us
  starting transfers between devices: 37.1 us -> 41.5 us
  Pallas kernels: 28.6 us -> 24.6 us
  other arithmetic: 8.53 us -> 11.3 us
    all_to_all x1, waiting for transfers between devices: 29.3 us -> 8.74 us  [per_device(): stats = lax.all_to_all(stats, VOC, 0, 0)]
    ppermute x0 -> x3, waiting for transfers between devices: none -> 13.1 us  [per_device(): lax.ppermute(part, 'x', [(i, (i + step) % xs) for i in range(xs)])]
    all_to_all x2, waiting for transfers between devices: 14.9 us -> 6.51 us  [spread(): lax.all_to_all(jnp.broadcast_to(value[None], (count,) + value.shape), axe...]
    all_to_all x1 -> x0, blocking collectives: 7.9 us -> none  [spread(): lax.all_to_all(jnp.broadcast_to(value[None], (count,) + value.shape), axe...]
    all_to_all x2, starting transfers between devices: 15.6 us -> 9.5 us  [spread(): lax.all_to_all(jnp.broadcast_to(value[None], (count,) + value.shape), axe...]
    all_to_all x1, starting transfers between devices: 5.63 us -> 10.9 us  [per_device(): stats = lax.all_to_all(stats, VOC, 0, 0)]
    pallas_call x1, Pallas kernels: 28.6 us -> 24.6 us  [run_head(): pl.pallas_call(functools.partial(head_kernel, blocks), out_shape=(jax.Sha...]
    ppermute x0 -> x3, starting transfers between devices: none -> 3 us  [per_device(): lax.ppermute(part, 'x', [(i, (i + step) % xs) for i in range(xs)])]
  transfers between devices with their start and end apart: 7 -> 10, of which waited for: 7 -> 9; matrix products, arithmetic and copies ran while one was open for 9% -> 11% of each run, Pallas kernels for 0% -> 0%
where the time goes in v3:
time: 244 us; the launch traced here: 242 us
  waiting for transfers between devices  95.5 us (39%)
  starting transfers between devices  41.5 us (17%)
  blocking collectives  34.6 us (14%)
  Pallas kernels  24.6 us (10%)
  between operations  16.3 us (7%)
  other arithmetic  11.3 us (5%)
  matrix products  10.2 us (4%)
  local copies, waits for them, and re-layouts  8.08 us (3%)
    all_to_all x1, blocking collectives, token_columns(): found = lax.all_to_all(found, 'x', 0, 0)  34.6 us
    all_gather x1, waiting for transfers between devices, per_device(): whole_head = lax.all_gather(head_weight, SEQ, axis=0, tiled=True)  27.8 us
    pallas_call x1, Pallas kernels, run_head(): pl.pallas_call(functools.partial(head_kernel, blocks), out_shape=(jax.Sha...  24.6 us
    all_to_all x1, waiting for transfers between devices, token_columns(): found = lax.all_to_all(found, 'z', 0, 0)  17.8 us
    all_to_all x1, waiting for transfers between devices, per_device(): back = lax.all_to_all(back, 'z', 0, 0)  15.9 us
    ppermute x3, waiting for transfers between devices, per_device(): lax.ppermute(part, 'x', [(i, (i + step) % xs) for i in range(xs)])  13.1 us
    all_to_all x1, starting transfers between devices, per_device(): stats = lax.all_to_all(stats, VOC, 0, 0)  10.9 us
    all_to_all x2, starting transfers between devices, spread(): lax.all_to_all(jnp.broadcast_to(value[None], (count,) + value.shape), axe...  9.5 us
  transfers between devices with their start and end apart: 10, of which 9 were waited for; matrix products, arithmetic and copies ran while one was open for 11% of the time, Pallas kernels for 0%

profile of v3, /device:TPU:30, one launch (start us, length us, event | category | flops | bytes accessed | tf_op | source)
XLA Modules:
  0.0 242.0 jit_solution(9945067844251278847)
XLA Ops:
  7.2 0.7 all-gather.2.cloned.1.call-update
  8.0 0.6 broadcast_in_dim.11
  8.6 4.7 %all-to-all-start = ((s32[8,1,256]{2,1,0:T(1,128)}), s32[8,1,256]{2,1,0:T(1,128)S(1)}, u32[]{:S(2)}, u32[]{:S(2)}) async-start(s32[8,1,256]{2,1,0:T(1,128)} %broadcast_in_dim.11), calls=%async_computation | async-start | bytes 16384 | tf_op jit(solution)/shard_map/all_to_all | solution.py:19
  13.3 3.2 %all-to-all-done = s32[8,1,256]{2,1,0:T(1,128)S(1)} async-done(((s32[8,1,256]{2,1,0:T(1,128)}), s32[8,1,256]{2,1,0:T(1,128)S(1)}, u32[]{:S(2)}, u32[]{:S(2)}) %all-to-all-start) | async-done | bytes 8224 | tf_op jit(solution)/shard_map/all_to_all | solution.py:19
  16.5 9.5 %fusion.7 = bf16[640,2048]{0,1:T(8,128)(2,1)} fusion(bf16[640,2432]{1,0:T(8,128)(2,1)S(1)} %copy-done.1, s32[2432]{0:T(1024)S(1)} %iota_add_fusion, s32[2048]{0:T(1024)S(1)} %bitcast.94), kind=kOutput, calls=%fused_computation.5 | convolution fusion | flops 6381633536 | bytes 5752320 | tf_op jit(solution)/shard_map/dot_general | solution.py:149
  26.0 3.2 %copy.36 = bf16[640,2048]{1,0:T(8,128)(2,1)S(1)} copy(bf16[640,2048]{0,1:T(8,128)(2,1)} %fusion.7) | data formatting | bytes 5242880 | tf_op jit(solution)/shard_map/convert_element_type | solution.py:151
  29.3 0.9 copy.54
  30.3 34.6 %all_to_all.31 = bf16[4,8,160,256]{3,1,2,0:T(8,128)(2,1)} all-to-all(bf16[4,8,160,256]{3,1,2,0:T(8,128)(2,1)S(1)} %bitcast_bitcast_fusion), channel_id=1, replica_groups=mesh['y'=4,'c'=2,'z'=8,'x'=4] {'x'}, dimensions={0} | all-to-all | bytes 5242880 | tf_op jit(solution)/shard_map/all_to_all | solution.py:153
  64.9 2.8 %reduce_sum.123 = bf16[8,160,256]{2,0,1:T(8,128)(2,1)S(1)} reduce(bf16[4,8,160,256]{3,1,2,0:T(8,128)(2,1)} %all_to_all.31, bf16[]{:T(256)} %constant.72.clone.1), dimensions={0}, to_apply=%region_0.0 | reduce | flops 983040 | bytes 3276802 | tf_op jit(solution)/shard_map/reduce_sum | solution.py:154
  67.7 1.0 copy.37
  68.6 8.3 %all-to-all-start.2 = ((bf16[8,160,256]{2,1,0:T(8,128)(2,1)}), bf16[8,160,256]{2,1,0:T(8,128)(2,1)S(1)}, u32[]{:S(2)}, u32[]{:S(2)}) async-start(bf16[8,160,256]{2,1,0:T(8,128)(2,1)} %copy.37), calls=%async_computation.2 | async-start | bytes 1310720 | tf_op jit(solution)/shard_map/all_to_all | solution.py:155
  77.7 0.6 add_bitcast_fusion
  78.3 17.8 %all-to-all-done.2 = bf16[8,160,256]{2,1,0:T(8,128)(2,1)S(1)} async-done(((bf16[8,160,256]{2,1,0:T(8,128)(2,1)}), bf16[8,160,256]{2,1,0:T(8,128)(2,1)S(1)}, u32[]{:S(2)}, u32[]{:S(2)}) %all-to-all-start.2) | async-done | bytes 655392 | tf_op jit(solution)/shard_map/all_to_all | solution.py:155
  96.2 4.0 %collective-permute-start = (bf16[160,256]{1,0:T(8,128)(2,1)S(1)}, bf16[160,256]{1,0:T(8,128)(2,1)S(1)}, u32[]{:S(2)}, u32[]{:S(2)}) collective-permute-start(bf16[160,256]{1,0:T(8,128)(2,1)S(1)} %reduce_sum.124), channel_id=1, source_target_pairs={{0,0},{4,32},{8,64},{12,96},{16,128},{20,160},{24,192},{28,224},{3... | collective-permute-start | bytes 245768 | tf_op jit(solution)/shard_map/ppermute | solution.py:158
  100.8 1.4 copy.43
  102.2 4.9 %collective-permute-done = bf16[160,256]{1,0:T(8,128)(2,1)S(1)} collective-permute-done((bf16[160,256]{1,0:T(8,128)(2,1)S(1)}, bf16[160,256]{1,0:T(8,128)(2,1)S(1)}, u32[]{:S(2)}, u32[]{:S(2)}) %collective-permute-start) | collective-permute-done | bytes 81952 | tf_op jit(solution)/shard_map/ppermute | solution.py:158
  107.2 27.8 %all-gather.2.cloned.1.call-done.head_hbm = bf16[5120,2432]{1,0:T(8,128)(2,1)} async-done(((bf16[640,2432]{1,0:T(8,128)(2,1)}), bf16[5120,2432]{1,0:T(8,128)(2,1)}) %all-gather.2.cloned.1.call-update) | async-done | bytes 24903696 | tf_op jit(solution)/shard_map/all_gather | solution.py:170
  135.0 24.6 %head.1 = (f32[256,2432]{1,0:T(8,128)}, f32[32,8,256]{2,1,0:T(8,128)}, bf16[1280,256]{1,0:T(8,128)(2,1)}, bf16[1280,256]{1,0:T(8,128)(2,1)}, bf16[1280,256]{1,0:T(8,128)(2,1)}, /*index=5*/bf16[1280,256]{1,0:T(8,128)(2,1)}) custom-call(s32[1]{0:T(128)} %bitcast.place_ref, bf16[256,5120]{1,0:T(8,128)(2,1)} %bitcast.103, bf16[2432,256]{1,0:T(8,128)(2,1)} %bitcast.90, ...), custom_call_target="tpu_custom_call" | custom-call | flops 12750684160 | bytes 29884416 | tf_op jit(solution)/shard_map/head/pallas_call | solution.py:113
  159.6 10.9 %all-to-all-start.3 = ((f32[32,8,256]{2,1,0:T(8,128)}), f32[32,8,256]{2,1,0:T(8,128)S(1)}, u32[]{:S(2)}, u32[]{:S(2)}) async-start(f32[32,8,256]{2,1,0:T(8,128)} %get-tuple-element.16), calls=%async_computation.3 | async-start | bytes 524288 | tf_op jit(solution)/shard_map/all_to_all | solution.py:198
  170.9 2.7 %collective-permute-start.2 = (bf16[1280,256]{1,0:T(8,128)(2,1)}, bf16[1280,256]{1,0:T(8,128)(2,1)}, u32[]{:S(2)}, u32[]{:S(2)}) collective-permute-start(bf16[1280,256]{1,0:T(8,128)(2,1)} %get-tuple-element.20), channel_id=1, source_target_pairs={{0,2},{1,3},{2,0},{3,1},{4,6},{5,7},{6,4},{7,5},{8,10},{9,11},{10,... | collective-permute-start | bytes 1966088 | tf_op jit(solution)/shard_map/ppermute | solution.py:195
  173.6 8.7 %all-to-all-done.3 = f32[32,8,256]{2,1,0:T(8,128)S(1)} async-done(((f32[32,8,256]{2,1,0:T(8,128)}), f32[32,8,256]{2,1,0:T(8,128)S(1)}, u32[]{:S(2)}, u32[]{:S(2)}) %all-to-all-start.3) | async-done | bytes 262176 | tf_op jit(solution)/shard_map/all_to_all | solution.py:198
  182.6 0.6 broadcast_in_dim.13
  183.2 4.8 %all-to-all-start.4 = ((f32[8,2,2,128]{3,2,1,0:T(2,128)}), f32[8,2,2,128]{3,2,1,0:T(2,128)S(1)}, u32[]{:S(2)}, u32[]{:S(2)}) async-start(f32[8,2,2,128]{3,2,1,0:T(2,128)} %broadcast_in_dim.13), calls=%async_computation.4 | async-start | bytes 32768 | tf_op jit(solution)/shard_map/all_to_all | solution.py:19
  188.1 3.3 %all-to-all-done.4 = f32[8,2,2,128]{3,2,1,0:T(2,128)S(1)} async-done(((f32[8,2,2,128]{3,2,1,0:T(2,128)}), f32[8,2,2,128]{3,2,1,0:T(2,128)S(1)}, u32[]{:S(2)}, u32[]{:S(2)}) %all-to-all-start.4) | async-done | bytes 16416 | tf_op jit(solution)/shard_map/all_to_all | solution.py:19
  191.3 0.6 slice_reduce_fusion.1
  192.2 13.0 %collective-permute-done.3 = bf16[1280,256]{1,0:T(8,128)(2,1)} collective-permute-done((bf16[1280,256]{1,0:T(8,128)(2,1)}, bf16[1280,256]{1,0:T(8,128)(2,1)}, u32[]{:S(2)}, u32[]{:S(2)}) %collective-permute-start.3) | collective-permute-done | bytes 655392 | tf_op jit(solution)/shard_map/ppermute | solution.py:195
  205.2 2.8 %add_convert_fusion = bf16[1280,256]{1,0:T(8,128)(2,1)} fusion(bf16[1280,256]{1,0:T(8,128)(2,1)} %collective-permute-done.3, bf16[1280,256]{1,0:T(8,128)(2,1)} %collective-permute-done.2, bf16[1280,256]{1,0:T(8,128)(2,1)S(1)} %collective-permute-done.1, bf16[1280,256]{1,0:T(8,128)(2,1)} %get-tuple-element.18, f32[256]{0:T(256)S(1)} %bitcast.96, ...), kind=kLoop, calls=%fused_computation.10 | loop fusion | flops 3932160 | bytes 3280896 | tf_op jit(solution)/shard_map/convert_element_type | solution.py:217
  208.1 5.8 %all-to-all-start.5 = ((bf16[8,160,256]{2,1,0:T(8,128)(2,1)}), bf16[8,160,256]{2,1,0:T(8,128)(2,1)S(1)}, u32[]{:S(2)}, u32[]{:S(2)}) async-start(bf16[8,160,256]{2,1,0:T(8,128)(2,1)} %bitcast.27), calls=%async_computation.5 | async-start | bytes 1310720 | tf_op jit(solution)/shard_map/all_to_all | solution.py:218
  213.9 0.8 fusion.21
  216.7 1.8 multiply_convert_fusion
  218.5 15.9 %all-to-all-done.5 = bf16[8,160,256]{2,1,0:T(8,128)(2,1)S(1)} async-done(((bf16[8,160,256]{2,1,0:T(8,128)(2,1)}), bf16[8,160,256]{2,1,0:T(8,128)(2,1)S(1)}, u32[]{:S(2)}, u32[]{:S(2)}) %all-to-all-start.5) | async-done | bytes 655392 | tf_op jit(solution)/shard_map/all_to_all | solution.py:218
  234.5 0.7 copy_bitcast_fusion
  (41 shorter events, 2.8 us)
Async XLA Ops:
  7.2 9.4 %copy-start.1 = (bf16[640,2432]{1,0:T(8,128)(2,1)S(1)}, bf16[640,2432]{1,0:T(8,128)(2,1)}, u32[]{:S(2)}) copy-start(bf16[640,2432]{1,0:T(8,128)(2,1)} %param.8) | copy-start | bytes 9338884
  7.2 0.8 copy-start.3
  7.2 127.8 %all-gather.2.cloned.1.call-start = ((), (), s32[]{:S(2)}) async-start(), calls=%async_computation.6 | async-start | bytes 28016640 | tf_op jit(solution)/shard_map/all_gather | solution.py:170
  8.6 7.9 %all-to-all-start = ((s32[8,1,256]{2,1,0:T(1,128)}), s32[8,1,256]{2,1,0:T(1,128)S(1)}, u32[]{:S(2)}, u32[]{:S(2)}) async-start(s32[8,1,256]{2,1,0:T(1,128)} %broadcast_in_dim.11), calls=%async_computation | async-start | bytes 16384 | tf_op jit(solution)/shard_map/all_to_all | solution.py:19
  64.9 12.1 %copy-start = (bf16[2,128,2432]{2,1,0:T(8,128)(2,1)S(1)}, bf16[2,128,2432]{2,1,0:T(8,128)(2,1)}, u32[]{:S(2)}) copy-start(bf16[2,128,2432]{2,1,0:T(8,128)(2,1)} %param.9) | copy-start | bytes 3735556
  68.6 27.5 %all-to-all-start.2 = ((bf16[8,160,256]{2,1,0:T(8,128)(2,1)}), bf16[8,160,256]{2,1,0:T(8,128)(2,1)S(1)}, u32[]{:S(2)}, u32[]{:S(2)}) async-start(bf16[8,160,256]{2,1,0:T(8,128)(2,1)} %copy.37), calls=%async_computation.2 | async-start | bytes 1310720 | tf_op jit(solution)/shard_map/all_to_all | solution.py:155
  96.2 10.9 %collective-permute-start = (bf16[160,256]{1,0:T(8,128)(2,1)S(1)}, bf16[160,256]{1,0:T(8,128)(2,1)S(1)}, u32[]{:S(2)}, u32[]{:S(2)}) collective-permute-start(bf16[160,256]{1,0:T(8,128)(2,1)S(1)} %reduce_sum.124), channel_id=1, source_target_pairs={{0,0},{4,32},{8,64},{12,96},{16,128},{20,160},{24,192},{28,224},{3... | collective-permute-start | bytes 245768 | tf_op jit(solution)/shard_map/ppermute | solution.py:158
  135.0 47.5 %copy-start.5 = (s32[2,128]{1,0:T(2,128)S(1)}, s32[2,128]{1,0:T(2,128)}, u32[]{:S(2)}) copy-start(s32[2,128]{1,0:T(2,128)} %param.12) | copy-start | bytes 3076
  135.0 47.5 %copy-start.6 = (f32[2]{0:T(128)S(1)}, f32[2]{0:T(128)}, u32[]{:S(2)}) copy-start(f32[2]{0:T(128)} %param.13) | copy-start | bytes 28
  135.0 47.5 %copy-start.7 = (s32[2]{0:T(128)S(1)}, s32[2]{0:T(128)}, u32[]{:S(2)}) copy-start(s32[2]{0:T(128)} %param.11) | copy-start | bytes 28
  159.6 22.7 %all-to-all-start.3 = ((f32[32,8,256]{2,1,0:T(8,128)}), f32[32,8,256]{2,1,0:T(8,128)S(1)}, u32[]{:S(2)}, u32[]{:S(2)}) async-start(f32[32,8,256]{2,1,0:T(8,128)} %get-tuple-element.16), calls=%async_computation.3 | async-start | bytes 524288 | tf_op jit(solution)/shard_map/all_to_all | solution.py:198
  170.6 21.6 %collective-permute-start.1 = (bf16[1280,256]{1,0:T(8,128)(2,1)}, bf16[1280,256]{1,0:T(8,128)(2,1)S(1)}, u32[]{:S(2)}, u32[]{:S(2)}) collective-permute-start(bf16[1280,256]{1,0:T(8,128)(2,1)} %get-tuple-element.19), channel_id=1, source_target_pairs={{0,1},{1,2},{2,3},{3,0},{4,5},{5,6},{6,7},{7,4},{8,9},{9,10},{10,1... | collective-permute-start | bytes 1966088 | tf_op jit(solution)/shard_map/ppermute | solution.py:195
  170.9 21.3 %collective-permute-start.2 = (bf16[1280,256]{1,0:T(8,128)(2,1)}, bf16[1280,256]{1,0:T(8,128)(2,1)}, u32[]{:S(2)}, u32[]{:S(2)}) collective-permute-start(bf16[1280,256]{1,0:T(8,128)(2,1)} %get-tuple-element.20), channel_id=1, source_target_pairs={{0,2},{1,3},{2,0},{3,1},{4,6},{5,7},{6,4},{7,5},{8,10},{9,11},{10,... | collective-permute-start | bytes 1966088 | tf_op jit(solution)/shard_map/ppermute | solution.py:195
  173.6 31.7 %collective-permute-start.3 = (bf16[1280,256]{1,0:T(8,128)(2,1)}, bf16[1280,256]{1,0:T(8,128)(2,1)}, u32[]{:S(2)}, u32[]{:S(2)}) collective-permute-start(bf16[1280,256]{1,0:T(8,128)(2,1)} %get-tuple-element.21), channel_id=1, source_target_pairs={{0,3},{1,0},{2,1},{3,2},{4,7},{5,4},{6,5},{7,6},{8,11},{9,8},{10,9... | collective-permute-start | bytes 1966088 | tf_op jit(solution)/shard_map/ppermute | solution.py:195
  182.4 34.2 %copy-start.2 = (f32[256,2432]{1,0:T(8,128)S(1)}, f32[256,2432]{1,0:T(8,128)}, u32[]{:S(2)}) copy-start(f32[256,2432]{1,0:T(8,128)} %get-tuple-element.17) | copy-start | bytes 7471108
  183.2 8.1 %all-to-all-start.4 = ((f32[8,2,2,128]{3,2,1,0:T(2,128)}), f32[8,2,2,128]{3,2,1,0:T(2,128)S(1)}, u32[]{:S(2)}, u32[]{:S(2)}) async-start(f32[8,2,2,128]{3,2,1,0:T(2,128)} %broadcast_in_dim.13), calls=%async_computation.4 | async-start | bytes 32768 | tf_op jit(solution)/shard_map/all_to_all | solution.py:19
  208.1 26.3 %all-to-all-start.5 = ((bf16[8,160,256]{2,1,0:T(8,128)(2,1)}), bf16[8,160,256]{2,1,0:T(8,128)(2,1)S(1)}, u32[]{:S(2)}, u32[]{:S(2)}) async-start(bf16[8,160,256]{2,1,0:T(8,128)(2,1)} %bitcast.27), calls=%async_computation.5 | async-start | bytes 1310720 | tf_op jit(solution)/shard_map/all_to_all | solution.py:218
  216.7 18.5 %copy-start.4 = (f32[1,2,128]{2,0,1:T(1,128)}, f32[1,2,128]{2,0,1:T(1,128)S(1)}, u32[]{:S(2)}) copy-start(f32[1,2,128]{2,0,1:T(1,128)S(1)} %fusion.24) | copy-start | bytes 3076
Sparse Core Ops, SparseCore 0:
  9.8 125.0 all-gather.1

commit v4 on v3

--- a/solution.py
+++ b/solution.py
@@ -12,6 +12,7 @@
 TILE = 128
 SUB = 8
 WIDE = 8
+FIRST = 48
 
 
 def spread(value, axes):
@@ -19,14 +20,20 @@
     return lax.all_to_all(jnp.broadcast_to(value[None], (count,) + value.shape), axes, 0, 0)
 
 
-def head_kernel(blocks, place_ref, state_hbm, ref_hbm, token_ref, lse_ref, head_hbm,
-                logit_hbm, stat_ref, back0, back1, back2, back3,
-                state, refs, head, logit, flipped, turned, result, sems, outsem):
+def rotate(value, axis, by):
+    count = lax.axis_size(axis)
+    return lax.ppermute(value, axis, [(i, (i + by) % count) for i in range(count)])
+
+
+def head_kernel(blocks, pieces, first, place_ref, state_hbm, ref_hbm, token_ref, lse_ref, *rest):
+    heads, rest = rest[:pieces], rest[pieces:]
+    logit_hbm, stat_ref = rest[:2]
+    parts = (len(rest) - 11) // 2
+    early, late = rest[2 : 2 + parts], rest[2 + parts : 2 + 2 * parts]
+    state, refs, head, logit, flipped, turned, result, sems, outsem = rest[2 + 2 * parts :]
     rows, columns = logit.shape
     width = head.shape[0]
     depth = width // blocks
-    backs = (back0, back1, back2, back3)
-    parts = len(backs)
     piece = depth // parts
     wide = WIDE * TILE
     tiles = columns // wide
@@ -34,20 +41,30 @@
 
     def fetch(tile, size):
         span = pl.ds(pl.multiple_of(tile * wide, wide), size)
-        return pltpu.make_async_copy(head_hbm.at[:, span], head.at[:, span], sems.at[tile])
+        copies = []
+        for index, part in enumerate(heads):
+            start = pl.multiple_of(place_ref[1 + index], SUB * 4)
+            place = pl.ds(start, part.shape[0])
+            copies.append(
+                pltpu.make_async_copy(part.at[:, span], head.at[place, span], sems.at[tile, index])
+            )
+        return copies
 
     get_state = pltpu.make_async_copy(state_hbm, state, outsem.at[0])
     get_refs = pltpu.make_async_copy(ref_hbm, refs, outsem.at[1])
     get_state.start()
     for tile in range(tiles):
-        fetch(tile, wide).start()
+        for copy in fetch(tile, wide):
+            copy.start()
     if tail:
-        fetch(tiles, tail).start()
+        for copy in fetch(tiles, tail):
+            copy.start()
     get_refs.start()
     get_state.wait()
 
     def forward(tile, size, best):
-        fetch(tile, size).wait()
+        for copy in fetch(tile, size):
+            copy.wait()
         span = pl.ds(pl.multiple_of(tile * wide, wide), size)
         values = jnp.dot(state[...], head[:, span], preferred_element_type=jnp.float32)
         logit[:, span] = values
@@ -97,27 +114,30 @@
         result[...] = jnp.dot(
             head[span, :], turned[...], preferred_element_type=jnp.float32
         ).astype(jnp.bfloat16)
-        target = pl.ds(pl.multiple_of(block * piece, piece), piece)
-        for step, back in enumerate(backs):
+        for step in range(parts):
             source = lax.rem(place + step, parts) * piece
-            back[target, :] = result[pl.ds(pl.multiple_of(source, piece), piece), :]
+            for backs, offset, size in ((early, 0, first), (late, first, piece - first)):
+                target = pl.ds(pl.multiple_of(block * size, SUB * 2), size)
+                origin = pl.ds(pl.multiple_of(source + offset, SUB * 2), size)
+                backs[step][target, :] = result[origin, :]
 
     put_logit.wait()
 
-def run_head(states, refs, tokens, ref_lse, place, head, blocks, parts, peers):
+def run_head(states, refs, tokens, ref_lse, place, heads, blocks, parts, first, peers):
     rows, width = states.shape
-    columns = head.shape[1]
+    columns = heads[0].shape[1]
     vmem = pl.BlockSpec(memory_space=pltpu.VMEM)
     hbm = pl.BlockSpec(memory_space=pl.ANY)
-    back = jax.ShapeDtypeStruct((width // parts, rows), jnp.bfloat16)
+    early = jax.ShapeDtypeStruct((blocks * first, rows), jnp.bfloat16)
+    late = jax.ShapeDtypeStruct((width // parts - blocks * first, rows), jnp.bfloat16)
     return pl.pallas_call(
-        functools.partial(head_kernel, blocks),
+        functools.partial(head_kernel, blocks, len(heads), first),
         out_shape=(
             jax.ShapeDtypeStruct((rows, columns), jnp.float32),
             jax.ShapeDtypeStruct((peers, SUB, rows), jnp.float32),
-        ) + (back,) * parts,
-        in_specs=[pl.BlockSpec(memory_space=pltpu.SMEM), hbm, hbm, vmem, vmem, hbm],
-        out_specs=(hbm,) + (vmem,) * (1 + parts),
+        ) + (early,) * parts + (late,) * parts,
+        in_specs=[pl.BlockSpec(memory_space=pltpu.SMEM), hbm, hbm, vmem, vmem] + [hbm] * len(heads),
+        out_specs=(hbm,) + (vmem,) * (1 + 2 * parts),
         scratch_shapes=[
             pltpu.VMEM((rows, width), jnp.bfloat16),
             pltpu.VMEM((columns, rows), jnp.bfloat16),
@@ -126,7 +146,7 @@
             pltpu.VMEM((columns, rows), jnp.float32),
             pltpu.VMEM((columns, rows), jnp.bfloat16),
             pltpu.VMEM((width // blocks, rows), jnp.bfloat16),
-            pltpu.SemaphoreType.DMA((-(-columns // (WIDE * TILE)),)),
+            pltpu.SemaphoreType.DMA((-(-columns // (WIDE * TILE)), len(heads))),
             pltpu.SemaphoreType.DMA((2,)),
         ],
         compiler_params=pltpu.CompilerParams(vmem_limit_bytes=56 << 20),
@@ -136,10 +156,43 @@
             transcendentals=rows * columns,
         ),
         name="head",
-    )(place, states, refs, tokens, ref_lse, head)
-
-
-def token_columns(head_weight, token_ids, vocab_start):
+    )(place, states, refs, tokens, ref_lse, *heads)
+
+
+def merge(stats):
+    top = jnp.max(stats[:, 0], axis=0)
+    scale = jnp.exp(stats[:, 0] - top[None])
+    total = jnp.sum(stats[:, 1] * scale, axis=0)
+    weighted = jnp.sum(stats[:, 2] * scale, axis=0)
+    own = jnp.sum(stats[:, 3], axis=0)
+    ref_top = jnp.max(stats[:, 4], axis=0)
+    ref_lse = ref_top + jnp.log(jnp.sum(jnp.exp(stats[:, 4] - ref_top[None]), axis=0))
+    return top, total, weighted, own, ref_lse
+
+
+def gather_head(head_weight):
+    depth = head_weight.shape[0]
+    half = depth // 2
+    ys, cores = lax.axis_size("y"), lax.axis_size("c")
+    y, core = lax.axis_index("y"), lax.axis_index("c")
+    upper, lower = head_weight[:half], head_weight[half:]
+    near = [rotate(upper, "y", 1), rotate(lower, "y", -1)]
+    late = [rotate(lower, "y", 1), rotate(upper, "y", -1)]
+    far = [rotate(near[0], "y", 1), rotate(near[1], "y", -1)]
+    found = [(head_weight, 0, 0)]
+    found += [(near[0], -1, 0), (near[1], 1, half), (late[0], -1, half), (late[1], 1, 0)]
+    found += [(far[0], -2, 0), (far[1], 2, half)]
+    pieces, starts = [], []
+    for piece, step, row in found:
+        chip = lax.rem(y + step + ys, ys)
+        for other in (0, 1):
+            owner = chip * cores + (core if other == 0 else 1 - core)
+            pieces.append(piece if other == 0 else rotate(piece, "c", 1))
+            starts.append(owner * depth + row)
+    return pieces, starts, near
+
+
+def token_columns(head_weight, token_ids, vocab_start, near):
     depth, vocab_dev = head_weight.shape
     seqs, zs, xs = lax.axis_size(SEQ), lax.axis_size("z"), lax.axis_size("x")
     rows = token_ids.size
@@ -150,6 +203,7 @@
         head_weight, onehot, (((1,), (1,)), ((), ())), preferred_element_type=jnp.float32
     ).astype(jnp.bfloat16)
     found = found.reshape(xs, depth // xs, seqs, rows).transpose(0, 2, 1, 3)
+    found, near = lax.optimization_barrier((found, near))
     found = lax.all_to_all(found, "x", 0, 0)
     found = jnp.sum(found.astype(jnp.float32), axis=0).astype(jnp.bfloat16)
     found = lax.all_to_all(found, "z", 0, 0)
@@ -167,8 +221,8 @@
     seq_start = seq_index * segment
     vocab_start = lax.axis_index(VOC) * vocab_dev
 
-    whole_head = lax.all_gather(head_weight, SEQ, axis=0, tiled=True)
-    own_columns = token_columns(head_weight, token_ids, vocab_start)
+    heads, starts, near = gather_head(head_weight)
+    own_columns = token_columns(head_weight, token_ids, vocab_start, near)
 
     refs = ref_logits.reshape(rows, vocab_dev)
     wide = refs.astype(jnp.float32)
@@ -185,38 +239,36 @@
         turned_refs,
         (tokens - vocab_start).reshape(1, rows),
         ref_lse[None],
-        x_index.reshape(1),
-        whole_head,
+        jnp.stack([x_index] + starts),
+        heads,
         seqs,
         xs,
-        lax.axis_size(VOC),
-    )
-    backs = [
-        part if step == 0 else lax.ppermute(part, "x", [(i, (i + step) % xs) for i in range(xs)])
-        for step, part in enumerate(backs)
-    ]
-    stats = lax.all_to_all(stats, VOC, 0, 0)
-
+        FIRST,
+        xs,
+    )
+    early, late = (
+        [part if step == 0 else rotate(part, "x", step) for step, part in enumerate(group)]
+        for group in (backs[:xs], backs[xs:])
+    )
+    stats = lax.all_to_all(stats, "x", 0, 0)
     tops = stats[:, 0]
-    top_policy = jnp.max(tops, axis=0)
-    scale = jnp.exp(tops - top_policy[None])
-    total = jnp.sum(stats[:, 1] * scale, axis=0)
-    weighted = jnp.sum(stats[:, 2] * scale, axis=0)
-    own_logit = jnp.sum(stats[:, 3], axis=0)
-    top_ref = jnp.max(stats[:, 4], axis=0)
-    lse_ref = top_ref + jnp.log(jnp.sum(jnp.exp(stats[:, 4] - top_ref[None]), axis=0))
+    merged, early = lax.optimization_barrier((jnp.stack(merge(stats)), early))
+    stats = spread(merged, "z")
+    top_policy, total, weighted, own_logit, lse_ref = merge(stats)
     lse_policy = top_policy + jnp.log(total)
     kl_value = (weighted / total - lse_policy + lse_ref).reshape(batch, segment)
 
-    z_start = lax.axis_index("z") * xs
-    back = 0.0
-    for step, part in enumerate(backs):
-        sender = z_start + lax.rem(x_index + xs - step, xs)
-        share = lax.dynamic_index_in_dim(scale, sender, 0, keepdims=True) / total[None]
-        back = back + part.astype(jnp.float32) * share
-    back = back.astype(jnp.bfloat16).reshape(seqs, -1, rows)
-    back = lax.all_to_all(back, "z", 0, 0)
-    back = jnp.sum(back.astype(jnp.float32), axis=0)
+    share = jnp.exp(tops - top_policy[None]) / total[None]
+    gathered = []
+    for group in (early, late):
+        back = 0.0
+        for step, part in enumerate(group):
+            sender = lax.rem(x_index + xs - step, xs)
+            back = back + part.astype(jnp.float32) * lax.dynamic_slice_in_dim(share, sender, 1, 0)
+        back = back.astype(jnp.bfloat16).reshape(seqs, -1, rows)
+        back = lax.all_to_all(back, "z", 0, 0)
+        gathered.append(jnp.sum(back.astype(jnp.float32), axis=0))
+    back = jnp.concatenate(gathered, axis=0)
 
     position = seq_start + lax.broadcasted_iota(jnp.int32, (1, segment), 1)
     live = ((loss_mask == 1) & (position <= end_pos[:, None])).astype(jnp.float32)

time: 244 us -> 257 us (1.053)
  between operations: 16.3 us -> 2.98 us
  starting transfers between devices: 41.5 us -> 53.3 us
  local copies, waits for them, and re-layouts: 8.08 us -> 17.5 us
  other arithmetic: 11.3 us -> 17.2 us
  blocking collectives: 34.6 us -> 29.4 us
  Pallas kernels: 24.6 us -> 29 us
    ppermute x3 -> x19, waiting for transfers between devices: 13.1 us -> 66 us  [rotate(): lax.ppermute(value, axis, [(i, (i + by) % count) for i in range(count)])]
    all_gather x1 -> x0, waiting for transfers between devices: 27.8 us -> none  [per_device(): whole_head = lax.all_gather(head_weight, SEQ, axis=0, tiled=True)]
    all_to_all x2, waiting for transfers between devices: 26.6 us -> 0.01 us  [the longest x1 0.01 us: per_device(): stats = lax.all_to_all(stats, 'x', 0, 0)]
    ppermute x3 -> x19, starting transfers between devices: 3 us -> 13 us  [rotate(): lax.ppermute(value, axis, [(i, (i + by) % count) for i in range(count)])]
    all_to_all x2, starting transfers between devices: 19.2 us -> 9.68 us  [the longest x1 4.91 us: per_device(): stats = lax.all_to_all(stats, 'x', 0, 0)]
    all_to_all x2 -> x3, starting transfers between devices: 9.5 us -> 16.3 us  [spread(): lax.all_to_all(jnp.broadcast_to(value[None], (count,) + value.shape), axe...]
    all_to_all x1, blocking collectives: 34.6 us -> 29.4 us  [token_columns(): found = lax.all_to_all(found, 'z', 0, 0)]
    pallas_call x1, Pallas kernels: 24.6 us -> 29 us  [run_head(): pl.pallas_call(functools.partial(head_kernel, blocks, len(heads), first),...]
  transfers between devices with their start and end apart: 10 -> 27, of which waited for: 9 -> 13; matrix products, arithmetic and copies ran while one was open for 11% -> 15% of each run, Pallas kernels for 0% -> 0%
where the time goes in v4:
time: 257 us; the launch traced here: 253 us
  waiting for transfers between devices  93.5 us (36%)
  starting transfers between devices  53.3 us (21%)
  blocking collectives  29.4 us (11%)
  Pallas kernels  29 us (11%)
  local copies, waits for them, and re-layouts  17.5 us (7%)
  other arithmetic  17.2 us (7%)
  matrix products  10.3 us (4%)
  between operations  2.98 us (1%)
    ppermute x19, waiting for transfers between devices, rotate(): lax.ppermute(value, axis, [(i, (i + by) % count) for i in range(count)])  66 us
    all_to_all x1, blocking collectives, token_columns(): found = lax.all_to_all(found, 'z', 0, 0)  29.4 us
    pallas_call x1, Pallas kernels, run_head(): pl.pallas_call(functools.partial(head_kernel, blocks, len(heads), first),...  29 us
    all_to_all x2, waiting for transfers between devices, per_device(): back = lax.all_to_all(back, 'z', 0, 0)  18.2 us
    all_to_all x3, starting transfers between devices, spread(): lax.all_to_all(jnp.broadcast_to(value[None], (count,) + value.shape), axe...  16.3 us
    ppermute x19, starting transfers between devices, rotate(): lax.ppermute(value, axis, [(i, (i + by) % count) for i in range(count)])  13 us
    dot_general x1, matrix products, token_columns(): lax.dot_general(head_weight, onehot, (((1,), (1,)), ((), ())), preferred_...  9.54 us
    ppermute x1, starting transfers between devices, token_columns(): return lax.ppermute(found, SEQ + ('z',), pairs)  7.44 us
  transfers between devices with their start and end apart: 27, of which 13 were waited for; matrix products, arithmetic and copies ran while one was open for 15% of the time, Pallas kernels for 0%

profile of v4, /device:TPU:30, one launch (start us, length us, event | category | flops | bytes accessed | tf_op | source)
XLA Modules:
  0.0 253.1 jit_solution(2392609840816193115)
XLA Ops:
  1.9 4.7 %all-to-all-start = ((s32[8,1,256]{2,1,0:T(1,128)}), s32[8,1,256]{2,1,0:T(1,128)S(1)}, u32[]{:S(2)}, u32[]{:S(2)}) async-start(s32[8,1,256]{2,1,0:T(1,128)} %broadcast_in_dim.11), calls=%async_computation | async-start | bytes 16384 | tf_op jit(solution)/shard_map/all_to_all | solution.py:20
  6.6 3.9 %fusion.35 = (bf16[320,2432]{1,0:T(8,128)(2,1)}, bf16[320,2432]{1,0:T(8,128)(2,1)}) fusion(bf16[640,2432]{1,0:T(8,128)(2,1)} %rest_0_.1), kind=kLoop, calls=%fused_computation.82 | loop fusion | bytes 6225920 | tf_op jit(solution)/shard_map/slice | solution.py:178
  10.5 2.0 collective-permute-start.1
  12.5 9.5 %fusion.7 = bf16[640,2048]{0,1:T(8,128)(2,1)} fusion(bf16[640,2432]{1,0:T(8,128)(2,1)S(1)} %copy-done.1, s32[2432]{0:T(1024)S(1)} %iota_add_fusion, s32[2048]{0:T(1024)S(1)} %bitcast.150), kind=kOutput, calls=%fused_computation.5 | convolution fusion | flops 6381633536 | bytes 5752320 | tf_op jit(solution)/shard_map/dot_general | solution.py:202
  22.1 3.0 %copy.52 = bf16[640,2048]{1,0:T(8,128)(2,1)S(1)} copy(bf16[640,2048]{0,1:T(8,128)(2,1)} %fusion.7) | data formatting | bytes 5242880 | tf_op jit(solution)/shard_map/convert_element_type | solution.py:204
  25.9 1.7 bitcast_bitcast_fusion
  27.6 19.3 %collective-permute-done.rest_2_ = bf16[320,2432]{1,0:T(8,128)(2,1)} collective-permute-done((bf16[320,2432]{1,0:T(8,128)(2,1)}, bf16[320,2432]{1,0:T(8,128)(2,1)}, u32[]{:S(2)}, u32[]{:S(2)}) %collective-permute-start) | collective-permute-done | bytes 1556512 | tf_op jit(solution)/shard_map/ppermute | solution.py:25
  48.2 4.8 %all-to-all-start.1 = ((bf16[4,8,160,256]{3,1,2,0:T(8,128)(2,1)}), bf16[4,8,160,256]{3,1,2,0:T(8,128)(2,1)S(1)}, u32[]{:S(2)}, u32[]{:S(2)}) async-start(bf16[4,8,160,256]{3,1,2,0:T(8,128)(2,1)} %bitcast_bitcast_fusion), calls=%async_computation.1 | async-start | bytes 5242880 | tf_op jit(solution)/shard_map/all_to_all | solution.py:207
  53.4 1.6 collective-permute-start.8
  55.0 1.7 collective-permute-start.10
  57.0 33.1 %collective-permute-done.6.rest_6_ = bf16[320,2432]{1,0:T(8,128)(2,1)S(1)} collective-permute-done((bf16[320,2432]{1,0:T(8,128)(2,1)}, bf16[320,2432]{1,0:T(8,128)(2,1)S(1)}, u32[]{:S(2)}, u32[]{:S(2)}) %collective-permute-start.6) | collective-permute-done | bytes 1556512 | tf_op jit(solution)/shard_map/ppermute | solution.py:25
  90.1 1.7 collective-permute-done.8.rest_8_
  93.9 29.4 %all_to_all.41 = bf16[8,160,256]{2,1,0:T(8,128)(2,1)S(1)} all-to-all(bf16[8,160,256]{2,1,0:T(8,128)(2,1)S(1)} %copy.53), channel_id=1, replica_groups=mesh['y'=4,'c'=2,'z'=8,'x'=4] {'z'}, dimensions={0} | all-to-all | bytes 1310720 | tf_op jit(solution)/shard_map/all_to_all | solution.py:209
  123.4 7.4 %collective-permute-start.2 = (bf16[160,256]{1,0:T(8,128)(2,1)S(1)}, bf16[160,256]{1,0:T(8,128)(2,1)}, u32[]{:S(2)}, u32[]{:S(2)}) collective-permute-start(bf16[160,256]{1,0:T(8,128)(2,1)S(1)} %reduce_sum.169), channel_id=1, source_target_pairs={{0,0},{4,32},{8,64},{12,96},{16,128},{20,160},{24,192},{28,224},{3... | collective-permute-start | bytes 245768 | tf_op jit(solution)/shard_map/ppermute | solution.py:212
  131.6 4.7 %collective-permute-done.2 = bf16[160,256]{1,0:T(8,128)(2,1)} collective-permute-done((bf16[160,256]{1,0:T(8,128)(2,1)S(1)}, bf16[160,256]{1,0:T(8,128)(2,1)}, u32[]{:S(2)}, u32[]{:S(2)}) %collective-permute-start.2) | collective-permute-done | bytes 81952 | tf_op jit(solution)/shard_map/ppermute | solution.py:212
  141.5 29.0 %head.1 = (f32[256,2432]{1,0:T(8,128)}, f32[4,8,256]{2,1,0:T(8,128)}, bf16[384,256]{1,0:T(8,128)(2,1)}, bf16[384,256]{1,0:T(8,128)(2,1)}, bf16[384,256]{1,0:T(8,...) custom-call(s32[15]{0:T(128)} %stack.91.place_ref, ...), custom_call_target="tpu_custom_call" | custom-call | flops 12750684160 | bytes 29884416 | tf_op jit(solution)/shard_map/head/pallas_call | solution.py:133
  170.5 4.9 %all-to-all-start.3 = ((f32[4,8,256]{2,1,0:T(8,128)}), f32[4,8,256]{2,1,0:T(8,128)S(1)}, u32[]{:S(2)}, u32[]{:S(2)}) async-start(f32[4,8,256]{2,1,0:T(8,128)} %get-tuple-element.27), calls=%async_computation.3 | async-start | bytes 65536 | tf_op jit(solution)/shard_map/all_to_all | solution.py:253
  176.0 2.9 %collective-permute-start.15 = (bf16[384,256]{1,0:T(8,128)(2,1)}, bf16[384,256]{1,0:T(8,128)(2,1)S(1)}, u32[]{:S(2)}, u32[]{:S(2)}) collective-permute-start(bf16[384,256]{1,0:T(8,128)(2,1)} %get-tuple-element.30), channel_id=1, source_target_pairs={{0,2},{1,3},{2,0},{3,1},{4,6},{5,7},{6,4},{7,5},{8,10},{9,11},{10,... | collective-permute-start | bytes 589832 | tf_op jit(solution)/shard_map/ppermute | solution.py:25
  179.1 5.0 %collective-permute-done.14 = bf16[384,256]{1,0:T(8,128)(2,1)S(1)} collective-permute-done((bf16[384,256]{1,0:T(8,128)(2,1)}, bf16[384,256]{1,0:T(8,128)(2,1)S(1)}, u32[]{:S(2)}, u32[]{:S(2)}) %collective-permute-start.14) | collective-permute-done | bytes 196640 | tf_op jit(solution)/shard_map/ppermute | solution.py:25
  185.5 3.1 %collective-permute-done.16 = bf16[384,256]{1,0:T(8,128)(2,1)S(1)} collective-permute-done((bf16[384,256]{1,0:T(8,128)(2,1)}, bf16[384,256]{1,0:T(8,128)(2,1)S(1)}, u32[]{:S(2)}, u32[]{:S(2)}) %collective-permute-start.16) | collective-permute-done | bytes 196640 | tf_op jit(solution)/shard_map/ppermute | solution.py:25
  189.3 4.0 %all-to-all-start.4 = ((f32[8,5,256]{2,1,0:T(8,128)}), f32[8,5,256]{2,1,0:T(8,128)}, u32[]{:S(2)}, u32[]{:S(2)}) async-start(f32[8,5,256]{2,1,0:T(8,128)} %broadcast_in_dim.13), calls=%async_computation.4 | async-start | bytes 131072 | tf_op jit(solution)/shard_map/all_to_all | solution.py:20
  195.0 2.1 collective-permute-start.18
  197.1 4.6 %all-to-all-done.4 = f32[8,5,256]{2,1,0:T(8,128)} async-done(((f32[8,5,256]{2,1,0:T(8,128)}), f32[8,5,256]{2,1,0:T(8,128)}, u32[]{:S(2)}, u32[]{:S(2)}) %all-to-all-start.4) | async-done | bytes 40992 | tf_op jit(solution)/shard_map/all_to_all | solution.py:20
  201.7 1.6 fusion.36
  206.3 7.6 %all-to-all-start.5 = ((f32[8,2,2,128]{3,2,1,0:T(2,128)}), f32[8,2,2,128]{3,2,1,0:T(2,128)S(1)}, u32[]{:S(2)}, u32[]{:S(2)}) async-start(f32[8,2,2,128]{3,2,1,0:T(2,128)} %broadcast_in_dim.14), calls=%async_computation.5 | async-start | bytes 32768 | tf_op jit(solution)/shard_map/all_to_all | solution.py:20
  215.3 1.8 add_convert_fusion.1
  217.1 3.4 %all-to-all-start.6 = ((bf16[8,48,256]{2,1,0:T(8,128)(2,1)}), bf16[8,48,256]{2,1,0:T(8,128)(2,1)S(1)}, u32[]{:S(2)}, u32[]{:S(2)}) async-start(bf16[8,48,256]{2,1,0:T(8,128)(2,1)} %bitcast.47), calls=%async_computation.6 | async-start | bytes 393216 | tf_op jit(solution)/shard_map/all_to_all | solution.py:269
  225.5 2.4 add_convert_fusion
  227.9 3.7 %all-to-all-done.6 = bf16[8,48,256]{2,1,0:T(8,128)(2,1)S(1)} async-done(((bf16[8,48,256]{2,1,0:T(8,128)(2,1)}), bf16[8,48,256]{2,1,0:T(8,128)(2,1)S(1)}, u32[]{:S(2)}, u32[]{:S(2)}) %all-to-all-start.6) | async-done | bytes 196640 | tf_op jit(solution)/shard_map/all_to_all | solution.py:269
  231.6 3.5 %all-to-all-start.7 = ((bf16[8,112,256]{2,1,0:T(8,128)(2,1)}), bf16[8,112,256]{2,1,0:T(8,128)(2,1)S(1)}, u32[]{:S(2)}, u32[]{:S(2)}) async-start(bf16[8,112,256]{2,1,0:T(8,128)(2,1)} %bitcast.48), calls=%async_computation.7 | async-start | bytes 917504 | tf_op jit(solution)/shard_map/all_to_all | solution.py:269
  235.1 1.8 multiply_convert_fusion
  237.0 14.5 %all-to-all-done.7 = bf16[8,112,256]{2,1,0:T(8,128)(2,1)S(1)} async-done(((bf16[8,112,256]{2,1,0:T(8,128)(2,1)}), bf16[8,112,256]{2,1,0:T(8,128)(2,1)S(1)}, u32[]{:S(2)}, u32[]{:S(2)}) %all-to-all-start.7) | async-done | bytes 458784 | tf_op jit(solution)/shard_map/all_to_all | solution.py:269
  (111 shorter events, 26.0 us)
Async XLA Ops:
  1.9 10.6 %all-to-all-start = ((s32[8,1,256]{2,1,0:T(1,128)}), s32[8,1,256]{2,1,0:T(1,128)S(1)}, u32[]{:S(2)}, u32[]{:S(2)}) async-start(s32[8,1,256]{2,1,0:T(1,128)} %broadcast_in_dim.11), calls=%async_computation | async-start | bytes 16384 | tf_op jit(solution)/shard_map/all_to_all | solution.py:20
  10.5 36.4 %collective-permute-start = (bf16[320,2432]{1,0:T(8,128)(2,1)}, bf16[320,2432]{1,0:T(8,128)(2,1)}, u32[]{:S(2)}, u32[]{:S(2)}) collective-permute-start(bf16[320,2432]{1,0:T(8,128)(2,1)} %get-tuple-element.78), channel_id=1, source_target_pairs={{0,64},{64,128},{128,192},{192,0},{1,65},{65,129},{129,193},{193,1... | collective-permute-start | bytes 4669448 | tf_op jit(solution)/shard_map/ppermute | solution.py:25
  10.5 37.7 %collective-permute-start.1 = (bf16[320,2432]{1,0:T(8,128)(2,1)}, bf16[320,2432]{1,0:T(8,128)(2,1)}, u32[]{:S(2)}, u32[]{:S(2)}) collective-permute-start(bf16[320,2432]{1,0:T(8,128)(2,1)} %get-tuple-element.77), channel_id=1, source_target_pairs={{0,192},{64,0},{128,64},{192,128},{1,193},{65,1},{129,65},{193,129... | collective-permute-start | bytes 4669448 | tf_op jit(solution)/shard_map/ppermute | solution.py:25
  48.2 44.8 %all-to-all-start.1 = ((bf16[4,8,160,256]{3,1,2,0:T(8,128)(2,1)}), bf16[4,8,160,256]{3,1,2,0:T(8,128)(2,1)S(1)}, u32[]{:S(2)}, u32[]{:S(2)}) async-start(bf16[4,8,160,256]{3,1,2,0:T(8,128)(2,1)} %bitcast_bitcast_fusion), calls=%async_computation.1 | async-start | bytes 5242880 | tf_op jit(solution)/shard_map/all_to_all | solution.py:207
  52.9 37.2 %collective-permute-start.6 = (bf16[320,2432]{1,0:T(8,128)(2,1)}, bf16[320,2432]{1,0:T(8,128)(2,1)S(1)}, u32[]{:S(2)}, u32[]{:S(2)}) collective-permute-start(bf16[320,2432]{1,0:T(8,128)(2,1)} %get-tuple-element.77), channel_id=1, source_target_pairs={{0,64},{64,128},{128,192},{192,0},{1,65},{65,129},{129,193},{193,1... | collective-permute-start | bytes 4669448 | tf_op jit(solution)/shard_map/ppermute | solution.py:25
  53.4 38.4 %collective-permute-start.8 = (bf16[320,2432]{1,0:T(8,128)(2,1)}, bf16[320,2432]{1,0:T(8,128)(2,1)S(1)}, u32[]{:S(2)}, u32[]{:S(2)}) collective-permute-start(bf16[320,2432]{1,0:T(8,128)(2,1)} %get-tuple-element.78), channel_id=1, source_target_pairs={{0,192},{64,0},{128,64},{192,128},{1,193},{65,1},{129,65},{193,129... | collective-permute-start | bytes 4669448 | tf_op jit(solution)/shard_map/ppermute | solution.py:25
  55.0 68.4 %collective-permute-start.10 = (bf16[320,2432]{1,0:T(8,128)(2,1)}, bf16[320,2432]{1,0:T(8,128)(2,1)}, u32[]{:S(2)}, u32[]{:S(2)}) collective-permute-start(bf16[320,2432]{1,0:T(8,128)(2,1)} %collective-permute-done.rest_2_), channel_id=1, source_target_pairs={{0,64},{64,128},{128,192},{192,0},{1,65},{65,129},{129,193},{193,1... | collective-permute-start | bytes 4669448 | tf_op jit(solution)/shard_map/ppermute | solution.py:25
  56.6 74.2 %collective-permute-start.12 = (bf16[320,2432]{1,0:T(8,128)(2,1)}, bf16[320,2432]{1,0:T(8,128)(2,1)}, u32[]{:S(2)}, u32[]{:S(2)}) collective-permute-start(bf16[320,2432]{1,0:T(8,128)(2,1)} %collective-permute-done.1.rest_4_), channel_id=1, source_target_pairs={{0,192},{64,0},{128,64},{192,128},{1,193},{65,1},{129,65},{193,129... | collective-permute-start | bytes 4669448 | tf_op jit(solution)/shard_map/ppermute | solution.py:25
  57.0 74.0 %collective-permute-start.4 = (bf16[320,2432]{1,0:T(8,128)(2,1)}, bf16[320,2432]{1,0:T(8,128)(2,1)}, u32[]{:S(2)}, u32[]{:S(2)}) collective-permute-start(bf16[320,2432]{1,0:T(8,128)(2,1)} %collective-permute-done.rest_2_), channel_id=1, source_target_pairs={{0,32},{32,0},{1,33},{33,1},{2,34},{34,2},{3,35},{35,3},{4,36},{36... | collective-permute-start | bytes 4669448 | tf_op jit(solution)/shard_map/ppermute | solution.py:25
  90.1 41.3 %collective-permute-start.5 = (bf16[320,2432]{1,0:T(8,128)(2,1)}, bf16[320,2432]{1,0:T(8,128)(2,1)}, u32[]{:S(2)}, u32[]{:S(2)}) collective-permute-start(bf16[320,2432]{1,0:T(8,128)(2,1)} %collective-permute-done.1.rest_4_), channel_id=1, source_target_pairs={{0,32},{32,0},{1,33},{33,1},{2,34},{34,2},{3,35},{35,3},{4,36},{36... | collective-permute-start | bytes 4669448 | tf_op jit(solution)/shard_map/ppermute | solution.py:25
  92.9 47.4 %collective-permute-start.3 = (bf16[640,2432]{1,0:T(8,128)(2,1)}, bf16[640,2432]{1,0:T(8,128)(2,1)}, u32[]{:S(2)}, u32[]{:S(2)}) collective-permute-start(bf16[640,2432]{1,0:T(8,128)(2,1)} %rest_0_.1), channel_id=1, source_target_pairs={{0,32},{32,0},{1,33},{33,1},{2,34},{34,2},{3,35},{35,3},{4,36},{36... | collective-permute-start | bytes 9338888 | tf_op jit(solution)/shard_map/ppermute | solution.py:25
  93.8 42.5 %copy-start = (bf16[2,128,2432]{2,1,0:T(8,128)(2,1)S(1)}, bf16[2,128,2432]{2,1,0:T(8,128)(2,1)}, u32[]{:S(2)}) copy-start(bf16[2,128,2432]{2,1,0:T(8,128)(2,1)} %param.9) | copy-start | bytes 3735556
  123.4 12.8 %collective-permute-start.2 = (bf16[160,256]{1,0:T(8,128)(2,1)S(1)}, bf16[160,256]{1,0:T(8,128)(2,1)}, u32[]{:S(2)}, u32[]{:S(2)}) collective-permute-start(bf16[160,256]{1,0:T(8,128)(2,1)S(1)} %reduce_sum.169), channel_id=1, source_target_pairs={{0,0},{4,32},{8,64},{12,96},{16,128},{20,160},{24,192},{28,224},{3... | collective-permute-start | bytes 245768 | tf_op jit(solution)/shard_map/ppermute | solution.py:212
  130.9 9.4 %collective-permute-start.7 = (bf16[320,2432]{1,0:T(8,128)(2,1)}, bf16[320,2432]{1,0:T(8,128)(2,1)S(1)}, u32[]{:S(2)}, u32[]{:S(2)}) collective-permute-start(bf16[320,2432]{1,0:T(8,128)(2,1)} %copy-done.18), channel_id=1, source_target_pairs={{0,32},{32,0},{1,33},{33,1},{2,34},{34,2},{3,35},{35,3},{4,36},{36... | collective-permute-start | bytes 4669448 | tf_op jit(solution)/shard_map/ppermute | solution.py:25
  131.0 9.3 %collective-permute-start.9 = (bf16[320,2432]{1,0:T(8,128)(2,1)}, bf16[320,2432]{1,0:T(8,128)(2,1)}, u32[]{:S(2)}, u32[]{:S(2)}) collective-permute-start(bf16[320,2432]{1,0:T(8,128)(2,1)} %copy-done.19), channel_id=1, source_target_pairs={{0,32},{32,0},{1,33},{33,1},{2,34},{34,2},{3,35},{35,3},{4,36},{36... | collective-permute-start | bytes 4669448 | tf_op jit(solution)/shard_map/ppermute | solution.py:25
  131.5 8.8 %collective-permute-start.11 = (bf16[320,2432]{1,0:T(8,128)(2,1)}, bf16[320,2432]{1,0:T(8,128)(2,1)}, u32[]{:S(2)}, u32[]{:S(2)}) collective-permute-start(bf16[320,2432]{1,0:T(8,128)(2,1)} %collective-permute-done.10.rest_10_), channel_id=1, source_target_pairs={{0,32},{32,0},{1,33},{33,1},{2,34},{34,2},{3,35},{35,3},{4,36},{36... | collective-permute-start | bytes 4669448 | tf_op jit(solution)/shard_map/ppermute | solution.py:25
  136.2 5.1 %collective-permute-start.13 = (bf16[320,2432]{1,0:T(8,128)(2,1)}, bf16[320,2432]{1,0:T(8,128)(2,1)}, u32[]{:S(2)}, u32[]{:S(2)}) collective-permute-start(bf16[320,2432]{1,0:T(8,128)(2,1)} %collective-permute-done.12.rest_12_), channel_id=1, source_target_pairs={{0,32},{32,0},{1,33},{33,1},{2,34},{34,2},{3,35},{35,3},{4,36},{36... | collective-permute-start | bytes 4669448 | tf_op jit(solution)/shard_map/ppermute | solution.py:25
  141.5 62.4 %copy-start.15 = (s32[2,128]{1,0:T(2,128)S(1)}, s32[2,128]{1,0:T(2,128)}, u32[]{:S(2)}) copy-start(s32[2,128]{1,0:T(2,128)} %param.12) | copy-start | bytes 3076
  141.5 62.4 %copy-start.16 = (f32[2]{0:T(128)S(1)}, f32[2]{0:T(128)}, u32[]{:S(2)}) copy-start(f32[2]{0:T(128)} %param.13) | copy-start | bytes 28
  141.5 62.4 %copy-start.17 = (s32[2]{0:T(128)S(1)}, s32[2]{0:T(128)}, u32[]{:S(2)}) copy-start(s32[2]{0:T(128)} %param.11) | copy-start | bytes 28
  170.5 55.0 %copy-start.3 = (bf16[896,256]{1,0:T(8,128)(2,1)S(1)}, bf16[896,256]{1,0:T(8,128)(2,1)}, u32[]{:S(2)}) copy-start(bf16[896,256]{1,0:T(8,128)(2,1)} %get-tuple-element.38) | copy-start | bytes 1376260
  170.5 8.4 %all-to-all-start.3 = ((f32[4,8,256]{2,1,0:T(8,128)}), f32[4,8,256]{2,1,0:T(8,128)S(1)}, u32[]{:S(2)}, u32[]{:S(2)}) async-start(f32[4,8,256]{2,1,0:T(8,128)} %get-tuple-element.27), calls=%async_computation.3 | async-start | bytes 65536 | tf_op jit(solution)/shard_map/all_to_all | solution.py:253
  176.0 8.0 %collective-permute-start.14 = (bf16[384,256]{1,0:T(8,128)(2,1)}, bf16[384,256]{1,0:T(8,128)(2,1)S(1)}, u32[]{:S(2)}, u32[]{:S(2)}) collective-permute-start(bf16[384,256]{1,0:T(8,128)(2,1)} %get-tuple-element.29), channel_id=1, source_target_pairs={{0,1},{1,2},{2,3},{3,0},{4,5},{5,6},{6,7},{7,4},{8,9},{9,10},{10,1... | collective-permute-start | bytes 589832 | tf_op jit(solution)/shard_map/ppermute | solution.py:25
  176.0 9.5 %collective-permute-start.15 = (bf16[384,256]{1,0:T(8,128)(2,1)}, bf16[384,256]{1,0:T(8,128)(2,1)S(1)}, u32[]{:S(2)}, u32[]{:S(2)}) collective-permute-start(bf16[384,256]{1,0:T(8,128)(2,1)} %get-tuple-element.30), channel_id=1, source_target_pairs={{0,2},{1,3},{2,0},{3,1},{4,6},{5,7},{6,4},{7,5},{8,10},{9,11},{10,... | collective-permute-start | bytes 589832 | tf_op jit(solution)/shard_map/ppermute | solution.py:25
  179.0 9.7 %collective-permute-start.16 = (bf16[384,256]{1,0:T(8,128)(2,1)}, bf16[384,256]{1,0:T(8,128)(2,1)S(1)}, u32[]{:S(2)}, u32[]{:S(2)}) collective-permute-start(bf16[384,256]{1,0:T(8,128)(2,1)} %get-tuple-element.31), channel_id=1, source_target_pairs={{0,3},{1,0},{2,1},{3,2},{4,7},{5,4},{6,5},{7,6},{8,11},{9,8},{10,9... | collective-permute-start | bytes 589832 | tf_op jit(solution)/shard_map/ppermute | solution.py:25
  189.3 12.4 %all-to-all-start.4 = ((f32[8,5,256]{2,1,0:T(8,128)}), f32[8,5,256]{2,1,0:T(8,128)}, u32[]{:S(2)}, u32[]{:S(2)}) async-start(f32[8,5,256]{2,1,0:T(8,128)} %broadcast_in_dim.13), calls=%async_computation.4 | async-start | bytes 131072 | tf_op jit(solution)/shard_map/all_to_all | solution.py:20
  193.8 31.7 %collective-permute-start.17 = (bf16[896,256]{1,0:T(8,128)(2,1)}, bf16[896,256]{1,0:T(8,128)(2,1)}, u32[]{:S(2)}, u32[]{:S(2)}) collective-permute-start(bf16[896,256]{1,0:T(8,128)(2,1)} %get-tuple-element.39), channel_id=1, source_target_pairs={{0,1},{1,2},{2,3},{3,0},{4,5},{5,6},{6,7},{7,4},{8,9},{9,10},{10,1... | collective-permute-start | bytes 1376264 | tf_op jit(solution)/shard_map/ppermute | solution.py:25
  195.0 30.5 %collective-permute-start.18 = (bf16[896,256]{1,0:T(8,128)(2,1)}, bf16[896,256]{1,0:T(8,128)(2,1)}, u32[]{:S(2)}, u32[]{:S(2)}) collective-permute-start(bf16[896,256]{1,0:T(8,128)(2,1)} %get-tuple-element.40), channel_id=1, source_target_pairs={{0,2},{1,3},{2,0},{3,1},{4,6},{5,7},{6,4},{7,5},{8,10},{9,11},{10,... | collective-permute-start | bytes 1376264 | tf_op jit(solution)/shard_map/ppermute | solution.py:25
  197.1 28.4 %collective-permute-start.19 = (bf16[896,256]{1,0:T(8,128)(2,1)}, bf16[896,256]{1,0:T(8,128)(2,1)}, u32[]{:S(2)}, u32[]{:S(2)}) collective-permute-start(bf16[896,256]{1,0:T(8,128)(2,1)} %get-tuple-element.41), channel_id=1, source_target_pairs={{0,3},{1,0},{2,1},{3,2},{4,7},{5,4},{6,5},{7,6},{8,11},{9,8},{10,9... | collective-permute-start | bytes 1376264 | tf_op jit(solution)/shard_map/ppermute | solution.py:25
  206.3 10.9 %all-to-all-start.5 = ((f32[8,2,2,128]{3,2,1,0:T(2,128)}), f32[8,2,2,128]{3,2,1,0:T(2,128)S(1)}, u32[]{:S(2)}, u32[]{:S(2)}) async-start(f32[8,2,2,128]{3,2,1,0:T(2,128)} %broadcast_in_dim.14), calls=%async_computation.5 | async-start | bytes 32768 | tf_op jit(solution)/shard_map/all_to_all | solution.py:20
  217.1 14.5 %all-to-all-start.6 = ((bf16[8,48,256]{2,1,0:T(8,128)(2,1)}), bf16[8,48,256]{2,1,0:T(8,128)(2,1)S(1)}, u32[]{:S(2)}, u32[]{:S(2)}) async-start(bf16[8,48,256]{2,1,0:T(8,128)(2,1)} %bitcast.47), calls=%async_computation.6 | async-start | bytes 393216 | tf_op jit(solution)/shard_map/all_to_all | solution.py:269
  231.6 19.9 %all-to-all-start.7 = ((bf16[8,112,256]{2,1,0:T(8,128)(2,1)}), bf16[8,112,256]{2,1,0:T(8,128)(2,1)S(1)}, u32[]{:S(2)}, u32[]{:S(2)}) async-start(bf16[8,112,256]{2,1,0:T(8,128)(2,1)} %bitcast.48), calls=%async_computation.7 | async-start | bytes 917504 | tf_op jit(solution)/shard_map/all_to_all | solution.py:269
  (16 other events, 129.5 us)

commit v5 on v3

--- a/solution.py
+++ b/solution.py
@@ -12,6 +12,7 @@
 TILE = 128
 SUB = 8
 WIDE = 8
+FIRST = 112
 
 
 def spread(value, axes):
@@ -19,8 +20,18 @@
     return lax.all_to_all(jnp.broadcast_to(value[None], (count,) + value.shape), axes, 0, 0)
 
 
+def share_out(value, axes):
+    slots = lax.broadcasted_iota(jnp.int32, (lax.axis_size(axes),) + (1,) * value.ndim, 0)
+    return lax.psum(jnp.where(slots == lax.axis_index(axes), value[None], 0.0), axes)
+
+
+def rotate(value, axis, by):
+    count = lax.axis_size(axis)
+    return lax.ppermute(value, axis, [(i, (i + by) % count) for i in range(count)])
+
+
 def head_kernel(blocks, place_ref, state_hbm, ref_hbm, token_ref, lse_ref, head_hbm,
-                logit_hbm, stat_ref, back0, back1, back2, back3,
+                logit_hbm, stat_ref, back0, back1, back2, back3, by_block,
                 state, refs, head, logit, flipped, turned, result, sems, outsem):
     rows, columns = logit.shape
     width = head.shape[0]
@@ -28,6 +39,7 @@
     backs = (back0, back1, back2, back3)
     parts = len(backs)
     piece = depth // parts
+    first = back0.shape[0] // blocks
     wide = WIDE * TILE
     tiles = columns // wide
     tail = columns - tiles * wide
@@ -97,27 +109,31 @@
         result[...] = jnp.dot(
             head[span, :], turned[...], preferred_element_type=jnp.float32
         ).astype(jnp.bfloat16)
-        target = pl.ds(pl.multiple_of(block * piece, piece), piece)
-        for step, back in enumerate(backs):
-            source = lax.rem(place + step, parts) * piece
-            back[target, :] = result[pl.ds(pl.multiple_of(source, piece), piece), :]
+        target = pl.ds(pl.multiple_of(block * first, SUB * 2), first)
+        for part, back in enumerate(backs):
+            source = lax.rem(place + part, parts) * piece
+            back[target, :] = result[pl.ds(pl.multiple_of(source, SUB * 4), first), :]
+            by_block[block, part * (piece - first) : (part + 1) * (piece - first), :] = result[
+                part * piece + first : (part + 1) * piece, :
+            ]
 
     put_logit.wait()
 
-def run_head(states, refs, tokens, ref_lse, place, head, blocks, parts, peers):
+def run_head(states, refs, tokens, ref_lse, place, head, blocks, parts, first, peers):
     rows, width = states.shape
     columns = head.shape[1]
     vmem = pl.BlockSpec(memory_space=pltpu.VMEM)
     hbm = pl.BlockSpec(memory_space=pl.ANY)
-    back = jax.ShapeDtypeStruct((width // parts, rows), jnp.bfloat16)
+    back = jax.ShapeDtypeStruct((blocks * first, rows), jnp.bfloat16)
+    rest = width // blocks - parts * first
     return pl.pallas_call(
         functools.partial(head_kernel, blocks),
         out_shape=(
             jax.ShapeDtypeStruct((rows, columns), jnp.float32),
             jax.ShapeDtypeStruct((peers, SUB, rows), jnp.float32),
-        ) + (back,) * parts,
+        ) + (back,) * parts + (jax.ShapeDtypeStruct((blocks, rest, rows), jnp.bfloat16),),
         in_specs=[pl.BlockSpec(memory_space=pltpu.SMEM), hbm, hbm, vmem, vmem, hbm],
-        out_specs=(hbm,) + (vmem,) * (1 + parts),
+        out_specs=(hbm,) + (vmem,) * (2 + parts),
         scratch_shapes=[
             pltpu.VMEM((rows, width), jnp.bfloat16),
             pltpu.VMEM((columns, rows), jnp.bfloat16),
@@ -180,7 +196,7 @@
     )
     tokens = token_ids.reshape(rows, 1)
     x_index = lax.axis_index("x")
-    logits, stats, *backs = run_head(
+    logits, stats, *backs, other = run_head(
         states,
         turned_refs,
         (tokens - vocab_start).reshape(1, rows),
@@ -189,13 +205,13 @@
         whole_head,
         seqs,
         xs,
+        FIRST,
         lax.axis_size(VOC),
     )
-    backs = [
-        part if step == 0 else lax.ppermute(part, "x", [(i, (i + step) % xs) for i in range(xs)])
-        for step, part in enumerate(backs)
-    ]
+    backs = [part if step == 0 else rotate(part, "x", step) for step, part in enumerate(backs)]
     stats = lax.all_to_all(stats, VOC, 0, 0)
+    stats, other = lax.optimization_barrier((stats, other))
+    other = lax.all_to_all(other, "z", 0, 0)
 
     tops = stats[:, 0]
     top_policy = jnp.max(tops, axis=0)
@@ -208,21 +224,31 @@
     lse_policy = top_policy + jnp.log(total)
     kl_value = (weighted / total - lse_policy + lse_ref).reshape(batch, segment)
 
-    z_start = lax.axis_index("z") * xs
+    zs, z_index = lax.axis_size("z"), lax.axis_index("z")
+    share = (scale / total[None]).reshape(zs, xs, rows)
+    here = lax.dynamic_index_in_dim(share, z_index, 0, keepdims=False)
     back = 0.0
     for step, part in enumerate(backs):
-        sender = z_start + lax.rem(x_index + xs - step, xs)
-        share = lax.dynamic_index_in_dim(scale, sender, 0, keepdims=True) / total[None]
-        back = back + part.astype(jnp.float32) * share
-    back = back.astype(jnp.bfloat16).reshape(seqs, -1, rows)
+        sender = lax.rem(x_index + xs - step, xs)
+        back = back + part.astype(jnp.float32) * lax.dynamic_slice_in_dim(here, sender, 1, 0)
+    back = back.astype(jnp.bfloat16).reshape(zs, -1, rows)
     back = lax.all_to_all(back, "z", 0, 0)
     back = jnp.sum(back.astype(jnp.float32), axis=0)
+
+    here = lax.dynamic_index_in_dim(share, x_index, 1, keepdims=True)
+    other = jnp.sum(other.astype(jnp.float32) * here, axis=0).astype(jnp.bfloat16)
+    other = other.reshape(xs, -1, rows)
+    mine = 0.0
+    for step in range(xs):
+        part = lax.dynamic_index_in_dim(other, lax.rem(x_index + step, xs), 0, keepdims=False)
+        mine = mine + (part if step == 0 else rotate(part, "x", step)).astype(jnp.float32)
+    back = jnp.concatenate([back, mine], axis=0)
 
     position = seq_start + lax.broadcasted_iota(jnp.int32, (1, segment), 1)
     live = ((loss_mask == 1) & (position <= end_pos[:, None])).astype(jnp.float32)
     at_end = (position == end_pos[:, None]).astype(jnp.float32)
     reward = -0.01 * kl_value * live + scores[:, None] * at_end
-    both = spread(jnp.stack([reward, live]), SEQ)
+    both = share_out(jnp.stack([reward, live]), SEQ)
     rewards, lives = both[:, 0], both[:, 1]
     upper = (
         lax.broadcasted_iota(jnp.int32, (segment, segment), 0)

time: 244 us -> 255 us (1.045)
  waiting for transfers between devices: 95.5 us -> 73.6 us
  blocking collectives: 34.6 us -> 55.8 us
  other arithmetic: 11.3 us -> 20.1 us
    psum x0 -> x1, blocking collectives: none -> 21.2 us  [share_out(): lax.psum(jnp.where(slots == lax.axis_index(axes), value[None], 0.0), axes)]
    ppermute x3 -> x6, waiting for transfers between devices: 13.1 us -> 0.02 us  [rotate(): lax.ppermute(value, axis, [(i, (i + by) % count) for i in range(count)])]
    all_to_all x2 -> x1, starting transfers between devices: 9.5 us -> 4.69 us  [spread(): lax.all_to_all(jnp.broadcast_to(value[None], (count,) + value.shape), axe...]
    all_to_all x1, waiting for transfers between devices: 15.9 us -> 12 us  [per_device(): back = lax.all_to_all(back, 'z', 0, 0)]
    all_to_all x0 -> x1, starting transfers between devices: none -> 3.68 us  [per_device(): other = lax.all_to_all(other, 'z', 0, 0)]
    all_to_all x2 -> x1, waiting for transfers between devices: 6.51 us -> 3.24 us  [spread(): lax.all_to_all(jnp.broadcast_to(value[None], (count,) + value.shape), axe...]
    ppermute x3 -> x6, starting transfers between devices: 3 us -> 5.8 us  [rotate(): lax.ppermute(value, axis, [(i, (i + by) % count) for i in range(count)])]
  transfers between devices with their start and end apart: 10 -> 13, of which waited for: 9 -> 6; matrix products, arithmetic and copies ran while one was open for 11% -> 15% of each run, Pallas kernels for 0% -> 0%
where the time goes in v5:
time: 255 us; the launch traced here: 253 us
  waiting for transfers between devices  73.6 us (29%)
  blocking collectives  55.8 us (22%)
  starting transfers between devices  44 us (17%)
  Pallas kernels  24.3 us (10%)
  other arithmetic  20.1 us (8%)
  between operations  16.3 us (6%)
  matrix products  10.3 us (4%)
  local copies, waits for them, and re-layouts  8.14 us (3%)
    all_to_all x1, blocking collectives, token_columns(): found = lax.all_to_all(found, 'x', 0, 0)  34.6 us
    all_gather x1, waiting for transfers between devices, per_device(): whole_head = lax.all_gather(head_weight, SEQ, axis=0, tiled=True)  27.8 us
    pallas_call x1, Pallas kernels, run_head(): pl.pallas_call(functools.partial(head_kernel, blocks), out_shape=(jax.Sha...  24.3 us
    psum x1, blocking collectives, share_out(): lax.psum(jnp.where(slots == lax.axis_index(axes), value[None], 0.0), axes)  21.2 us
    all_to_all x1, waiting for transfers between devices, token_columns(): found = lax.all_to_all(found, 'z', 0, 0)  17.8 us
    all_to_all x1, waiting for transfers between devices, per_device(): back = lax.all_to_all(back, 'z', 0, 0)  12 us
    all_to_all x1, starting transfers between devices, per_device(): stats = lax.all_to_all(stats, VOC, 0, 0)  11 us
    dot_general x1, matrix products, token_columns(): lax.dot_general(head_weight, onehot, (((1,), (1,)), ((), ())), preferred_...  9.46 us
  transfers between devices with their start and end apart: 13, of which 6 were waited for; matrix products, arithmetic and copies ran while one was open for 15% of the time, Pallas kernels for 0%

profile of v5, /device:TPU:30, one launch (start us, length us, event | category | flops | bytes accessed | tf_op | source)
XLA Modules:
  0.0 252.5 jit_solution(7293210003011492298)
XLA Ops:
  8.6 4.7 %all-to-all-start = ((s32[8,1,256]{2,1,0:T(1,128)}), s32[8,1,256]{2,1,0:T(1,128)S(1)}, u32[]{:S(2)}, u32[]{:S(2)}) async-start(s32[8,1,256]{2,1,0:T(1,128)} %broadcast_in_dim.28), calls=%async_computation | async-start | bytes 16384 | tf_op jit(solution)/shard_map/all_to_all | solution.py:20
  13.3 3.2 %all-to-all-done = s32[8,1,256]{2,1,0:T(1,128)S(1)} async-done(((s32[8,1,256]{2,1,0:T(1,128)}), s32[8,1,256]{2,1,0:T(1,128)S(1)}, u32[]{:S(2)}, u32[]{:S(2)}) %all-to-all-start) | async-done | bytes 8224 | tf_op jit(solution)/shard_map/all_to_all | solution.py:20
  16.5 9.5 %fusion.7 = bf16[640,2048]{0,1:T(8,128)(2,1)} fusion(bf16[640,2432]{1,0:T(8,128)(2,1)S(1)} %copy-done.1, s32[2432]{0:T(1024)S(1)} %iota_add_fusion, s32[2048]{0:T(1024)S(1)} %bitcast.110), kind=kOutput, calls=%fused_computation.5 | convolution fusion | flops 6381633536 | bytes 5752320 | tf_op jit(solution)/shard_map/dot_general | solution.py:165
  26.0 3.2 %copy.32 = bf16[640,2048]{1,0:T(8,128)(2,1)S(1)} copy(bf16[640,2048]{0,1:T(8,128)(2,1)} %fusion.7) | data formatting | bytes 5242880 | tf_op jit(solution)/shard_map/convert_element_type | solution.py:167
  29.3 0.9 copy.42
  30.3 34.6 %all_to_all.31 = bf16[4,8,160,256]{3,1,2,0:T(8,128)(2,1)} all-to-all(bf16[4,8,160,256]{3,1,2,0:T(8,128)(2,1)S(1)} %bitcast_bitcast_fusion), channel_id=1, replica_groups=mesh['y'=4,'c'=2,'z'=8,'x'=4] {'x'}, dimensions={0} | all-to-all | bytes 5242880 | tf_op jit(solution)/shard_map/all_to_all | solution.py:169
  64.9 2.8 %reduce_sum.132 = bf16[8,160,256]{2,0,1:T(8,128)(2,1)S(1)} reduce(bf16[4,8,160,256]{3,1,2,0:T(8,128)(2,1)} %all_to_all.31, bf16[]{:T(256)} %constant.153.clone.1), dimensions={0}, to_apply=%region_0.0 | reduce | flops 983040 | bytes 3276802 | tf_op jit(solution)/shard_map/reduce_sum | solution.py:170
  67.7 1.0 copy.33
  68.6 8.3 %all-to-all-start.2 = ((bf16[8,160,256]{2,1,0:T(8,128)(2,1)}), bf16[8,160,256]{2,1,0:T(8,128)(2,1)S(1)}, u32[]{:S(2)}, u32[]{:S(2)}) async-start(bf16[8,160,256]{2,1,0:T(8,128)(2,1)} %copy.33), calls=%async_computation.2 | async-start | bytes 1310720 | tf_op jit(solution)/shard_map/all_to_all | solution.py:171
  78.4 17.8 %all-to-all-done.2 = bf16[8,160,256]{2,1,0:T(8,128)(2,1)S(1)} async-done(((bf16[8,160,256]{2,1,0:T(8,128)(2,1)}), bf16[8,160,256]{2,1,0:T(8,128)(2,1)S(1)}, u32[]{:S(2)}, u32[]{:S(2)}) %all-to-all-start.2) | async-done | bytes 655392 | tf_op jit(solution)/shard_map/all_to_all | solution.py:171
  96.2 4.0 %collective-permute-start = (bf16[160,256]{1,0:T(8,128)(2,1)S(1)}, bf16[160,256]{1,0:T(8,128)(2,1)S(1)}, u32[]{:S(2)}, u32[]{:S(2)}) collective-permute-start(bf16[160,256]{1,0:T(8,128)(2,1)S(1)} %reduce_sum.133), channel_id=1, source_target_pairs={{0,0},{4,32},{8,64},{12,96},{16,128},{20,160},{24,192},{28,224},{3... | collective-permute-start | bytes 245768 | tf_op jit(solution)/shard_map/ppermute | solution.py:174
  100.8 1.4 copy.37
  102.2 4.9 %collective-permute-done = bf16[160,256]{1,0:T(8,128)(2,1)S(1)} collective-permute-done((bf16[160,256]{1,0:T(8,128)(2,1)S(1)}, bf16[160,256]{1,0:T(8,128)(2,1)S(1)}, u32[]{:S(2)}, u32[]{:S(2)}) %collective-permute-start) | collective-permute-done | bytes 81952 | tf_op jit(solution)/shard_map/ppermute | solution.py:174
  107.2 27.8 %all-gather.2.cloned.1.call-done.head_hbm = bf16[5120,2432]{1,0:T(8,128)(2,1)} async-done(((bf16[640,2432]{1,0:T(8,128)(2,1)}), bf16[5120,2432]{1,0:T(8,128)(2,1)}) %all-gather.2.cloned.1.call-update) | async-done | bytes 24903696 | tf_op jit(solution)/shard_map/all_gather | solution.py:186
  135.0 24.3 %head.1 = (f32[256,2432]{1,0:T(8,128)}, f32[32,8,256]{2,1,0:T(8,128)}, bf16[896,256]{1,0:T(8,128)(2,1)}, bf16[896,256]{1,0:T(8,128)(2,1)}, bf16[896,256]{1,0:T(8...) custom-call(s32[1]{0:T(128)} %bitcast.place_ref, bf16[256,5120]{1,0:T(8,128)(2,1)} %bitcast.119, ...), custom_call_target="tpu_custom_call" | custom-call | flops 12750684160 | bytes 29884416 | tf_op jit(solution)/shard_map/head/pallas_call | solution.py:129
  159.3 11.0 %all-to-all-start.3 = ((f32[32,8,256]{2,1,0:T(8,128)}), f32[32,8,256]{2,1,0:T(8,128)S(1)}, u32[]{:S(2)}, u32[]{:S(2)}) async-start(f32[32,8,256]{2,1,0:T(8,128)} %get-tuple-element.19), calls=%async_computation.3 | async-start | bytes 524288 | tf_op jit(solution)/shard_map/all_to_all | solution.py:212
  172.3 2.7 %collective-permute-start.2 = (bf16[896,256]{1,0:T(8,128)(2,1)}, bf16[896,256]{1,0:T(8,128)(2,1)}, u32[]{:S(2)}, u32[]{:S(2)}) collective-permute-start(bf16[896,256]{1,0:T(8,128)(2,1)} %get-tuple-element.25), channel_id=1, source_target_pairs={{0,2},{1,3},{2,0},{3,1},{4,6},{5,7},{6,4},{7,5},{8,10},{9,11},{10,... | collective-permute-start | bytes 1376264 | tf_op jit(solution)/shard_map/ppermute | solution.py:30
  175.0 7.1 %all-to-all-done.3 = f32[32,8,256]{2,1,0:T(8,128)S(1)} async-done(((f32[32,8,256]{2,1,0:T(8,128)}), f32[32,8,256]{2,1,0:T(8,128)S(1)}, u32[]{:S(2)}, u32[]{:S(2)}) %all-to-all-start.3) | async-done | bytes 262176 | tf_op jit(solution)/shard_map/all_to_all | solution.py:212
  182.2 1.3 fusion.33
  184.1 3.7 %all-to-all-start.5 = ((bf16[8,192,256]{2,1,0:T(8,128)(2,1)}), bf16[8,192,256]{2,1,0:T(8,128)(2,1)S(1)}, u32[]{:S(2)}, u32[]{:S(2)}) async-start(bf16[8,192,256]{2,1,0:T(8,128)(2,1)} %get-tuple-element.27), calls=%async_computation.5 | async-start | bytes 1572864 | tf_op jit(solution)/shard_map/all_to_all | solution.py:214
  187.8 0.8 fusion.18
  188.6 0.8 fusion.28
  190.2 21.2 %psum.7 = f32[8,2,2,128]{3,0,2,1:T(8,128)S(1)} all-reduce(f32[8,2,2,128]{3,0,2,1:T(8,128)S(1)} %broadcast_select_fusion), channel_id=1, replica_groups=mesh['y'=4,'c'=2,'z'=8,'x'=4] {'y','c'}, use_global_device_ids=true, to_apply=%region_9.0 | all-reduce | flops 4096 | bytes 32768 | tf_op jit(solution)/shard_map/psum | solution.py:25
  212.7 0.8 fusion.24
  213.5 0.8 exponential_divide_fusion
  217.0 2.6 %add_convert_fusion = bf16[896,256]{1,0:T(8,128)(2,1)} fusion(bf16[896,256]{1,0:T(8,128)(2,1)} %collective-permute-done.3, bf16[896,256]{1,0:T(8,128)(2,1)} %collective-permute-done.2, bf16[896,256]{1,0:T(8,128)(2,1)} %collective-permute-done.1, bf16[896,256]{1,0:T(8,128)(2,1)} %get-tuple-element.23, f32[256]{0:T(256)S(1)} %bitcast.112, ...), kind=kLoop, calls=%fused_computation.12 | loop fusion | flops 2752512 | bytes 2297856 | tf_op jit(solution)/shard_map/convert_element_type | solution.py:234
  219.6 6.5 %all-to-all-start.4 = ((bf16[8,112,256]{2,1,0:T(8,128)(2,1)}), bf16[8,112,256]{2,1,0:T(8,128)(2,1)}, u32[]{:S(2)}, u32[]{:S(2)}) async-start(bf16[8,112,256]{2,1,0:T(8,128)(2,1)} %bitcast.102), calls=%async_computation.4 | async-start | bytes 917504 | tf_op jit(solution)/shard_map/all_to_all | solution.py:235
  226.2 2.5 multiply_convert_fusion
  228.9 1.7 collective-permute-start.4
  230.6 1.2 collective-permute-start.5
  231.8 12.0 %all-to-all-done.4 = bf16[8,112,256]{2,1,0:T(8,128)(2,1)} async-done(((bf16[8,112,256]{2,1,0:T(8,128)(2,1)}), bf16[8,112,256]{2,1,0:T(8,128)(2,1)}, u32[]{:S(2)}, u32[]{:S(2)}) %all-to-all-start.4) | async-done | bytes 458784 | tf_op jit(solution)/shard_map/all_to_all | solution.py:235
  243.8 1.1 convert_reduce_fusion
  (57 shorter events, 10.0 us)
Async XLA Ops:
  7.2 9.4 %copy-start.1 = (bf16[640,2432]{1,0:T(8,128)(2,1)S(1)}, bf16[640,2432]{1,0:T(8,128)(2,1)}, u32[]{:S(2)}) copy-start(bf16[640,2432]{1,0:T(8,128)(2,1)} %param.8) | copy-start | bytes 9338884
  7.2 0.8 copy-start.6
  7.2 127.8 %all-gather.2.cloned.1.call-start = ((), (), s32[]{:S(2)}) async-start(), calls=%async_computation.6 | async-start | bytes 28016640 | tf_op jit(solution)/shard_map/all_gather | solution.py:186
  8.6 7.9 %all-to-all-start = ((s32[8,1,256]{2,1,0:T(1,128)}), s32[8,1,256]{2,1,0:T(1,128)S(1)}, u32[]{:S(2)}, u32[]{:S(2)}) async-start(s32[8,1,256]{2,1,0:T(1,128)} %broadcast_in_dim.28), calls=%async_computation | async-start | bytes 16384 | tf_op jit(solution)/shard_map/all_to_all | solution.py:20
  64.9 12.1 %copy-start = (bf16[2,128,2432]{2,1,0:T(8,128)(2,1)S(1)}, bf16[2,128,2432]{2,1,0:T(8,128)(2,1)}, u32[]{:S(2)}) copy-start(bf16[2,128,2432]{2,1,0:T(8,128)(2,1)} %param.9) | copy-start | bytes 3735556
  68.6 27.5 %all-to-all-start.2 = ((bf16[8,160,256]{2,1,0:T(8,128)(2,1)}), bf16[8,160,256]{2,1,0:T(8,128)(2,1)S(1)}, u32[]{:S(2)}, u32[]{:S(2)}) async-start(bf16[8,160,256]{2,1,0:T(8,128)(2,1)} %copy.33), calls=%async_computation.2 | async-start | bytes 1310720 | tf_op jit(solution)/shard_map/all_to_all | solution.py:171
  96.2 10.9 %collective-permute-start = (bf16[160,256]{1,0:T(8,128)(2,1)S(1)}, bf16[160,256]{1,0:T(8,128)(2,1)S(1)}, u32[]{:S(2)}, u32[]{:S(2)}) collective-permute-start(bf16[160,256]{1,0:T(8,128)(2,1)S(1)} %reduce_sum.133), channel_id=1, source_target_pairs={{0,0},{4,32},{8,64},{12,96},{16,128},{20,160},{24,192},{28,224},{3... | collective-permute-start | bytes 245768 | tf_op jit(solution)/shard_map/ppermute | solution.py:174
  107.2 52.2 %copy-start.3 = (bf16[160,256]{1,0:T(8,128)(2,1)}, bf16[160,256]{1,0:T(8,128)(2,1)S(1)}, u32[]{:S(2)}) copy-start(bf16[160,256]{1,0:T(8,128)(2,1)S(1)} %collective-permute-done) | copy-start | bytes 245764
  159.3 22.8 %all-to-all-start.3 = ((f32[32,8,256]{2,1,0:T(8,128)}), f32[32,8,256]{2,1,0:T(8,128)S(1)}, u32[]{:S(2)}, u32[]{:S(2)}) async-start(f32[32,8,256]{2,1,0:T(8,128)} %get-tuple-element.19), calls=%async_computation.3 | async-start | bytes 524288 | tf_op jit(solution)/shard_map/all_to_all | solution.py:212
  172.1 45.0 %collective-permute-start.1 = (bf16[896,256]{1,0:T(8,128)(2,1)}, bf16[896,256]{1,0:T(8,128)(2,1)}, u32[]{:S(2)}, u32[]{:S(2)}) collective-permute-start(bf16[896,256]{1,0:T(8,128)(2,1)} %get-tuple-element.24), channel_id=1, source_target_pairs={{0,1},{1,2},{2,3},{3,0},{4,5},{5,6},{6,7},{7,4},{8,9},{9,10},{10,1... | collective-permute-start | bytes 1376264 | tf_op jit(solution)/shard_map/ppermute | solution.py:30
  172.3 44.7 %collective-permute-start.2 = (bf16[896,256]{1,0:T(8,128)(2,1)}, bf16[896,256]{1,0:T(8,128)(2,1)}, u32[]{:S(2)}, u32[]{:S(2)}) collective-permute-start(bf16[896,256]{1,0:T(8,128)(2,1)} %get-tuple-element.25), channel_id=1, source_target_pairs={{0,2},{1,3},{2,0},{3,1},{4,6},{5,7},{6,4},{7,5},{8,10},{9,11},{10,... | collective-permute-start | bytes 1376264 | tf_op jit(solution)/shard_map/ppermute | solution.py:30
  175.0 42.1 %collective-permute-start.3 = (bf16[896,256]{1,0:T(8,128)(2,1)}, bf16[896,256]{1,0:T(8,128)(2,1)}, u32[]{:S(2)}, u32[]{:S(2)}) collective-permute-start(bf16[896,256]{1,0:T(8,128)(2,1)} %get-tuple-element.26), channel_id=1, source_target_pairs={{0,3},{1,0},{2,1},{3,2},{4,7},{5,4},{6,5},{7,6},{8,11},{9,8},{10,9... | collective-permute-start | bytes 1376264 | tf_op jit(solution)/shard_map/ppermute | solution.py:30
  184.1 42.1 %copy-start.2 = (f32[256,2432]{1,0:T(8,128)S(1)}, f32[256,2432]{1,0:T(8,128)}, u32[]{:S(2)}) copy-start(f32[256,2432]{1,0:T(8,128)} %get-tuple-element.22) | copy-start | bytes 7471108
  184.1 35.5 %all-to-all-start.5 = ((bf16[8,192,256]{2,1,0:T(8,128)(2,1)}), bf16[8,192,256]{2,1,0:T(8,128)(2,1)S(1)}, u32[]{:S(2)}, u32[]{:S(2)}) async-start(bf16[8,192,256]{2,1,0:T(8,128)(2,1)} %get-tuple-element.27), calls=%async_computation.5 | async-start | bytes 1572864 | tf_op jit(solution)/shard_map/all_to_all | solution.py:214
  188.6 0.8 copy-start.5
  216.3 12.4 %copy-start.7 = (f32[1,2,128]{2,0,1:T(1,128)}, f32[1,2,128]{2,0,1:T(1,128)S(1)}, u32[]{:S(2)}) copy-start(f32[1,2,128]{2,0,1:T(1,128)S(1)} %fusion.30) | copy-start | bytes 3076
  219.6 24.2 %all-to-all-start.4 = ((bf16[8,112,256]{2,1,0:T(8,128)(2,1)}), bf16[8,112,256]{2,1,0:T(8,128)(2,1)}, u32[]{:S(2)}, u32[]{:S(2)}) async-start(bf16[8,112,256]{2,1,0:T(8,128)(2,1)} %bitcast.102), calls=%async_computation.4 | async-start | bytes 917504 | tf_op jit(solution)/shard_map/all_to_all | solution.py:235
  226.2 18.8 %copy-start.4 = (bf16[160,256]{1,0:T(8,128)(2,1)S(1)}, bf16[160,256]{1,0:T(8,128)(2,1)}, u32[]{:S(2)}) copy-start(bf16[160,256]{1,0:T(8,128)(2,1)} %copy-done.3) | copy-start | bytes 245764
  228.9 16.0 %collective-permute-start.4 = (bf16[48,256]{1,0:T(8,128)(2,1)S(1)}, bf16[48,256]{1,0:T(8,128)(2,1)S(1)}, u32[]{:S(2)}, u32[]{:S(2)}) collective-permute-start(bf16[48,256]{1,0:T(8,128)(2,1)S(1)} %get-tuple-element.60), channel_id=1, source_target_pairs={{0,1},{1,2},{2,3},{3,0},{4,5},{5,6},{6,7},{7,4},{8,9},{9,10},{10,1... | collective-permute-start | bytes 73736 | tf_op jit(solution)/shard_map/ppermute | solution.py:30
  230.6 14.3 %collective-permute-start.5 = (bf16[48,256]{1,0:T(8,128)(2,1)S(1)}, bf16[48,256]{1,0:T(8,128)(2,1)S(1)}, u32[]{:S(2)}, u32[]{:S(2)}) collective-permute-start(bf16[48,256]{1,0:T(8,128)(2,1)S(1)} %get-tuple-element.62), channel_id=1, source_target_pairs={{0,2},{1,3},{2,0},{3,1},{4,6},{5,7},{6,4},{7,5},{8,10},{9,11},{10,... | collective-permute-start | bytes 73736 | tf_op jit(solution)/shard_map/ppermute | solution.py:30
  231.8 13.2 %collective-permute-start.6 = (bf16[48,256]{1,0:T(8,128)(2,1)S(1)}, bf16[48,256]{1,0:T(8,128)(2,1)S(1)}, u32[]{:S(2)}, u32[]{:S(2)}) collective-permute-start(bf16[48,256]{1,0:T(8,128)(2,1)S(1)} %get-tuple-element.61), channel_id=1, source_target_pairs={{0,3},{1,0},{2,1},{3,2},{4,7},{5,4},{6,5},{7,6},{8,11},{9,8},{10,9... | collective-permute-start | bytes 73736 | tf_op jit(solution)/shard_map/ppermute | solution.py:30
Sparse Core Ops, SparseCore 0:
  9.9 125.0 all-gather.1

commit v6 on v5

--- a/solution.py
+++ b/solution.py
@@ -11,7 +11,6 @@
 VOC = ("z", "x")
 TILE = 128
 SUB = 8
-WIDE = 8
 FIRST = 112
 
 
@@ -20,19 +19,16 @@
     return lax.all_to_all(jnp.broadcast_to(value[None], (count,) + value.shape), axes, 0, 0)
 
 
-def share_out(value, axes):
-    slots = lax.broadcasted_iota(jnp.int32, (lax.axis_size(axes),) + (1,) * value.ndim, 0)
-    return lax.psum(jnp.where(slots == lax.axis_index(axes), value[None], 0.0), axes)
-
-
 def rotate(value, axis, by):
     count = lax.axis_size(axis)
     return lax.ppermute(value, axis, [(i, (i + by) % count) for i in range(count)])
 
 
-def head_kernel(blocks, place_ref, state_hbm, ref_hbm, token_ref, lse_ref, head_hbm,
-                logit_hbm, stat_ref, back0, back1, back2, back3, by_block,
-                state, refs, head, logit, flipped, turned, result, sems, outsem):
+def head_kernel(sizes, place_ref, state_hbm, ref_hbm, token_ref, lse_ref, *rest):
+    count, blocks = sum(sizes), len(sizes)
+    heads, rest = rest[:count], rest[count:]
+    logit_hbm, stat_ref, back0, back1, back2, back3, by_block = rest[:7]
+    state, refs, head, logit, flipped, turned, result, sems, outsem = rest[7:]
     rows, columns = logit.shape
     width = head.shape[0]
     depth = width // blocks
@@ -40,40 +36,42 @@
     parts = len(backs)
     piece = depth // parts
     first = back0.shape[0] // blocks
-    wide = WIDE * TILE
-    tiles = columns // wide
-    tail = columns - tiles * wide
-
-    def fetch(tile, size):
-        span = pl.ds(pl.multiple_of(tile * wide, wide), size)
-        return pltpu.make_async_copy(head_hbm.at[:, span], head.at[:, span], sems.at[tile])
 
     get_state = pltpu.make_async_copy(state_hbm, state, outsem.at[0])
     get_refs = pltpu.make_async_copy(ref_hbm, refs, outsem.at[1])
     get_state.start()
-    for tile in range(tiles):
-        fetch(tile, wide).start()
-    if tail:
-        fetch(tiles, tail).start()
+    fetches, at = [], 0
+    for block, size in enumerate(sizes):
+        start = pl.multiple_of(place_ref[1 + block] * depth, depth)
+        copies = []
+        for part in heads[at : at + size]:
+            span = pl.ds(start, part.shape[0])
+            copies.append(pltpu.make_async_copy(part, head.at[span], sems.at[at]))
+            copies[-1].start()
+            start = pl.multiple_of(start + part.shape[0], SUB * 4)
+            at += 1
+        fetches.append(copies)
     get_refs.start()
     get_state.wait()
 
-    def forward(tile, size, best):
-        fetch(tile, size).wait()
-        span = pl.ds(pl.multiple_of(tile * wide, wide), size)
-        values = jnp.dot(state[...], head[:, span], preferred_element_type=jnp.float32)
-        logit[:, span] = values
-        values = values.T
-        flipped[span, :] = values
-        return jnp.maximum(best, jnp.max(values.reshape(size // SUB, SUB, rows), axis=0))
-
-    best = jnp.full((SUB, rows), -jnp.inf, jnp.float32)
-    best = lax.fori_loop(0, tiles, lambda tile, best: forward(tile, wide, best), best)
-    if tail:
-        best = forward(tiles, tail, best)
-    top = jnp.max(best, axis=0, keepdims=True)
+    for block, copies in enumerate(fetches):
+        for copy in copies:
+            copy.wait()
+        span = pl.ds(pl.multiple_of(place_ref[1 + block] * depth, depth), depth)
+        term = jnp.dot(state[:, span], head[span, :], preferred_element_type=jnp.float32)
+        logit[...] = term if block == 0 else logit[...] + term
     put_logit = pltpu.make_async_copy(logit, logit_hbm, outsem.at[0])
     put_logit.start()
+
+    def flip(tile, best):
+        span = pl.ds(pl.multiple_of(tile * TILE, TILE), TILE)
+        values = logit[:, span].T
+        flipped[span, :] = values
+        return jnp.maximum(best, jnp.max(values.reshape(TILE // SUB, SUB, rows), axis=0))
+
+    best = jnp.full((SUB, rows), -jnp.inf, jnp.float32)
+    best = lax.fori_loop(0, columns // TILE, flip, best)
+    top = jnp.max(best, axis=0, keepdims=True)
     get_refs.wait()
 
     column = lax.broadcasted_iota(jnp.int32, (TILE, rows), 0)
@@ -119,20 +117,22 @@
 
     put_logit.wait()
 
-def run_head(states, refs, tokens, ref_lse, place, head, blocks, parts, first, peers):
+def run_head(states, refs, tokens, ref_lse, place, shards, parts, first, peers):
+    heads = [part for shard in shards for part in shard]
+    blocks = len(shards)
     rows, width = states.shape
-    columns = head.shape[1]
+    columns = heads[0].shape[1]
     vmem = pl.BlockSpec(memory_space=pltpu.VMEM)
     hbm = pl.BlockSpec(memory_space=pl.ANY)
     back = jax.ShapeDtypeStruct((blocks * first, rows), jnp.bfloat16)
     rest = width // blocks - parts * first
     return pl.pallas_call(
-        functools.partial(head_kernel, blocks),
+        functools.partial(head_kernel, tuple(len(shard) for shard in shards)),
         out_shape=(
             jax.ShapeDtypeStruct((rows, columns), jnp.float32),
             jax.ShapeDtypeStruct((peers, SUB, rows), jnp.float32),
         ) + (back,) * parts + (jax.ShapeDtypeStruct((blocks, rest, rows), jnp.bfloat16),),
-        in_specs=[pl.BlockSpec(memory_space=pltpu.SMEM), hbm, hbm, vmem, vmem, hbm],
+        in_specs=[pl.BlockSpec(memory_space=pltpu.SMEM), hbm, hbm, vmem, vmem] + [hbm] * len(heads),
         out_specs=(hbm,) + (vmem,) * (2 + parts),
         scratch_shapes=[
             pltpu.VMEM((rows, width), jnp.bfloat16),
@@ -142,7 +142,7 @@
             pltpu.VMEM((columns, rows), jnp.float32),
             pltpu.VMEM((columns, rows), jnp.bfloat16),
             pltpu.VMEM((width // blocks, rows), jnp.bfloat16),
-            pltpu.SemaphoreType.DMA((-(-columns // (WIDE * TILE)),)),
+            pltpu.SemaphoreType.DMA((len(heads),)),
             pltpu.SemaphoreType.DMA((2,)),
         ],
         compiler_params=pltpu.CompilerParams(vmem_limit_bytes=56 << 20),
@@ -152,12 +152,36 @@
             transcendentals=rows * columns,
         ),
         name="head",
-    )(place, states, refs, tokens, ref_lse, head)
+    )(place, states, refs, tokens, ref_lse, *heads)
+
+
+def gather_rows(head_weight):
+    half = head_weight.shape[0] // 2
+    near = [rotate(head_weight, "y", 1), rotate(head_weight, "y", -1)]
+    far = [rotate(near[0][:half], "y", 1), rotate(near[1][half:], "y", -1)]
+    return near, far
+
+
+def swap_cores(head_weight, near, far, after):
+    ys, cores = lax.axis_size("y"), lax.axis_size("c")
+    y, core = lax.axis_index("y"), lax.axis_index("c")
+    late, _ = lax.optimization_barrier((far, after))
+    shards, owners = [], []
+    for shard, sent, step in (
+        ([head_weight], [head_weight], 0),
+        (near[:1], near[:1], -1),
+        (near[1:], near[1:], 1),
+        (far, late, 2),
+    ):
+        chip = lax.rem(y + step + ys, ys) * cores
+        shards += [shard, [rotate(part, "c", 1) for part in sent]]
+        owners += [chip + core, chip + 1 - core]
+    return shards, owners
 
 
 def token_columns(head_weight, token_ids, vocab_start):
     depth, vocab_dev = head_weight.shape
-    seqs, zs, xs = lax.axis_size(SEQ), lax.axis_size("z"), lax.axis_size("x")
+    seqs, xs = lax.axis_size(SEQ), lax.axis_size("x")
     rows = token_ids.size
     ids = spread(token_ids.reshape(rows), SEQ).reshape(seqs * rows, 1)
     column = vocab_start + lax.broadcasted_iota(jnp.int32, (1, vocab_dev), 1)
@@ -170,21 +194,21 @@
     found = jnp.sum(found.astype(jnp.float32), axis=0).astype(jnp.bfloat16)
     found = lax.all_to_all(found, "z", 0, 0)
     found = jnp.sum(found.astype(jnp.float32), axis=0).astype(jnp.bfloat16)
-    pairs = [(i * zs + j, j * zs + i) for i in range(seqs) for j in range(zs)]
-    return lax.ppermute(found, SEQ + ("z",), pairs)
+    return found
 
 
 def per_device(hidden, head_weight, ref_logits, token_ids, end_pos, loss_mask, scores):
     batch, segment, width = hidden.shape
     rows = batch * segment
     vocab_dev = head_weight.shape[1]
-    seqs, xs = lax.axis_size(SEQ), lax.axis_size("x")
+    seqs, zs, xs = lax.axis_size(SEQ), lax.axis_size("z"), lax.axis_size("x")
     seq_index = lax.axis_index(SEQ)
     seq_start = seq_index * segment
     vocab_start = lax.axis_index(VOC) * vocab_dev
 
-    whole_head = lax.all_gather(head_weight, SEQ, axis=0, tiled=True)
+    near, far = gather_rows(head_weight)
     own_columns = token_columns(head_weight, token_ids, vocab_start)
+    shards, owners = swap_cores(head_weight, near, far, own_columns)
 
     refs = ref_logits.reshape(rows, vocab_dev)
     wide = refs.astype(jnp.float32)
@@ -194,6 +218,8 @@
     states, turned_refs, own_columns, ref_lse = lax.optimization_barrier(
         (hidden.reshape(rows, width), turned_refs, own_columns, ref_lse)
     )
+    pairs = [(i * zs + j, j * zs + i) for i in range(seqs) for j in range(zs)]
+    own_columns = lax.ppermute(own_columns, SEQ + ("z",), pairs)
     tokens = token_ids.reshape(rows, 1)
     x_index = lax.axis_index("x")
     logits, stats, *backs, other = run_head(
@@ -201,9 +227,8 @@
         turned_refs,
         (tokens - vocab_start).reshape(1, rows),
         ref_lse[None],
-        x_index.reshape(1),
-        whole_head,
-        seqs,
+        jnp.stack([x_index] + owners),
+        shards,
         xs,
         FIRST,
         lax.axis_size(VOC),
@@ -224,7 +249,7 @@
     lse_policy = top_policy + jnp.log(total)
     kl_value = (weighted / total - lse_policy + lse_ref).reshape(batch, segment)
 
-    zs, z_index = lax.axis_size("z"), lax.axis_index("z")
+    z_index = lax.axis_index("z")
     share = (scale / total[None]).reshape(zs, xs, rows)
     here = lax.dynamic_index_in_dim(share, z_index, 0, keepdims=False)
     back = 0.0
@@ -248,8 +273,19 @@
     live = ((loss_mask == 1) & (position <= end_pos[:, None])).astype(jnp.float32)
     at_end = (position == end_pos[:, None]).astype(jnp.float32)
     reward = -0.01 * kl_value * live + scores[:, None] * at_end
-    both = share_out(jnp.stack([reward, live]), SEQ)
+    y, core = lax.axis_index("y"), lax.axis_index("c")
+    ys = lax.axis_size("y")
+    both = jnp.stack([reward, live])
+    both = jnp.stack([both, rotate(both, "c", 1)])
+    both = jnp.stack([both] + [rotate(both, "y", step) for step in range(1, ys)])
+    both = both.reshape((seqs,) + both.shape[2:])
     rewards, lives = both[:, 0], both[:, 1]
+    step = lax.broadcasted_iota(jnp.int32, (seqs, seqs), 0)
+    behind = lax.broadcasted_iota(jnp.int32, (seqs, seqs), 1)
+    owner, owner_behind = (
+        lax.rem(y + ys - at // 2, ys) * 2 + jnp.where(at % 2 == 0, core, 1 - core)
+        for at in (step, behind)
+    )
     upper = (
         lax.broadcasted_iota(jnp.int32, (segment, segment), 0)
         >= lax.broadcasted_iota(jnp.int32, (segment, segment), 1)
@@ -258,16 +294,13 @@
         rewards.reshape(seqs * batch, segment), upper, precision=lax.Precision.HIGHEST
     ).reshape(seqs, batch, segment)
     totals = jnp.sum(rewards, axis=2)
-    later = (
-        lax.broadcasted_iota(jnp.int32, (seqs, seqs, 1), 1)
-        > lax.broadcasted_iota(jnp.int32, (seqs, seqs, 1), 0)
-    ).astype(jnp.float32)
+    later = (owner_behind > owner).astype(jnp.float32)[:, :, None]
     carried = jnp.sum(later * totals[None], axis=1)
     returns_all = suffix + carried[:, :, None]
     count = jnp.maximum(jnp.sum(lives), 1.0)
     mean = jnp.sum(lives * returns_all) / count
     var = jnp.sum(lives * returns_all * returns_all) / count - mean * mean
-    returns = lax.dynamic_index_in_dim(returns_all, seq_index, 0, keepdims=False)
+    returns = returns_all[0]
     advantages = (returns - mean) / jnp.sqrt(var + 1e-05)
     factor = (live * advantages / count).reshape(rows)
 

time: 255 us -> 265 us (1.039)
  waiting for transfers between devices: 73.6 us -> 113 us
  blocking collectives: 55.8 us -> 27.8 us
  between operations: 16.3 us -> 2.96 us
  Pallas kernels: 24.3 us -> 31.5 us
  local copies, waits for them, and re-layouts: 8.14 us -> 15.3 us
  other arithmetic: 20.1 us -> 17.1 us
    all_to_all x1, waiting for transfers between devices: 3.24 us -> 62.8 us  [spread(): lax.all_to_all(jnp.broadcast_to(value[None], (count,) + value.shape), axe...]
    all_gather x1 -> x0, waiting for transfers between devices: 27.8 us -> none  [per_device(): whole_head = lax.all_gather(head_weight, SEQ, axis=0, tiled=True)]
    psum x1 -> x0, blocking collectives: 21.2 us -> none  [share_out(): lax.psum(jnp.where(slots == lax.axis_index(axes), value[None], 0.0), axes)]
    ppermute x6 -> x19, waiting for transfers between devices: 0.02 us -> 16.4 us  [rotate(): lax.ppermute(value, axis, [(i, (i + by) % count) for i in range(count)])]
    ppermute x6 -> x19, starting transfers between devices: 5.8 us -> 16.1 us  [rotate(): lax.ppermute(value, axis, [(i, (i + by) % count) for i in range(count)])]
    pallas_call x1, Pallas kernels: 24.3 us -> 31.5 us  [run_head(): pl.pallas_call(functools.partial(head_kernel, tuple((len(shard) for shard...]
    all_to_all x1, blocking collectives: 34.6 us -> 27.8 us  [token_columns(): found = lax.all_to_all(found, 'z', 0, 0)]
    all_to_all x1, starting transfers between devices: 11 us -> 5.58 us  [per_device(): stats = lax.all_to_all(stats, VOC, 0, 0)]
  transfers between devices with their start and end apart: 13 -> 25, of which waited for: 6 -> 11; matrix products, arithmetic and copies ran while one was open for 15% -> 16% of each run, Pallas kernels for 0% -> 0%
where the time goes in v6:
time: 265 us; the launch traced here: 264 us
  waiting for transfers between devices  113 us (43%)
  starting transfers between devices  44.7 us (17%)
  Pallas kernels  31.5 us (12%)
  blocking collectives  27.8 us (10%)
  other arithmetic  17.1 us (6%)
  local copies, waits for them, and re-layouts  15.3 us (6%)
  matrix products  12.2 us (5%)
  between operations  2.96 us (1%)
    all_to_all x1, waiting for transfers between devices, spread(): lax.all_to_all(jnp.broadcast_to(value[None], (count,) + value.shape), axe...  62.8 us
    pallas_call x1, Pallas kernels, run_head(): pl.pallas_call(functools.partial(head_kernel, tuple((len(shard) for shard...  31.5 us
    all_to_all x1, blocking collectives, token_columns(): found = lax.all_to_all(found, 'z', 0, 0)  27.8 us
    all_to_all x1, waiting for transfers between devices, token_columns(): found = lax.all_to_all(found, 'x', 0, 0)  22.3 us
    ppermute x19, waiting for transfers between devices, rotate(): lax.ppermute(value, axis, [(i, (i + by) % count) for i in range(count)])  16.4 us
    ppermute x19, starting transfers between devices, rotate(): lax.ppermute(value, axis, [(i, (i + by) % count) for i in range(count)])  16.1 us
    dot_general x1, matrix products, token_columns(): lax.dot_general(head_weight, onehot, (((1,), (1,)), ((), ())), preferred_...  11.5 us
    all_to_all x1, waiting for transfers between devices, per_device(): back = lax.all_to_all(back, 'z', 0, 0)  8.89 us
  transfers between devices with their start and end apart: 25, of which 11 were waited for; matrix products, arithmetic and copies ran while one was open for 16% of the time, Pallas kernels for 0%

profile of v6, /device:TPU:30, one launch (start us, length us, event | category | flops | bytes accessed | tf_op | source)
XLA Modules:
  0.0 264.3 jit_solution(13526734369852142634)
XLA Ops:
  0.9 1.8 collective-permute-start.3
  2.7 1.3 broadcast_in_dim.17
  4.0 4.7 %all-to-all-start = ((s32[8,1,256]{2,1,0:T(1,128)}), s32[8,1,256]{2,1,0:T(1,128)S(1)}, u32[]{:S(2)}, u32[]{:S(2)}) async-start(s32[8,1,256]{2,1,0:T(1,128)} %broadcast_in_dim.17), calls=%async_computation | async-start | bytes 16384 | tf_op jit(solution)/shard_map/all_to_all | solution.py:19
  8.7 62.8 %all-to-all-done = s32[8,1,256]{2,1,0:T(1,128)S(1)} async-done(((s32[8,1,256]{2,1,0:T(1,128)}), s32[8,1,256]{2,1,0:T(1,128)S(1)}, u32[]{:S(2)}, u32[]{:S(2)}) %all-to-all-start) | async-done | bytes 8224 | tf_op jit(solution)/shard_map/all_to_all | solution.py:19
  71.5 11.5 %fusion.7 = bf16[640,2048]{0,1:T(8,128)(2,1)} fusion(bf16[640,2432]{1,0:T(8,128)(2,1)} %rest_0_.1, s32[2432]{0:T(1024)S(1)} %iota_add_fusion, s32[2048]{0:T(1024)S(1)} %bitcast.129), kind=kOutput, calls=%fused_computation.5 | convolution fusion | flops 6381633536 | bytes 5752320 | tf_op jit(solution)/shard_map/dot_general | solution.py:189
  83.0 3.0 %copy.36 = bf16[640,2048]{1,0:T(8,128)(2,1)S(1)} copy(bf16[640,2048]{0,1:T(8,128)(2,1)} %fusion.7) | data formatting | bytes 5242880 | tf_op jit(solution)/shard_map/convert_element_type | solution.py:191
  86.9 1.7 bitcast_bitcast_fusion
  88.6 4.8 %all-to-all-start.1 = ((bf16[4,8,160,256]{3,1,2,0:T(8,128)(2,1)}), bf16[4,8,160,256]{3,1,2,0:T(8,128)(2,1)S(1)}, u32[]{:S(2)}, u32[]{:S(2)}) async-start(bf16[4,8,160,256]{3,1,2,0:T(8,128)(2,1)} %bitcast_bitcast_fusion), calls=%async_computation.1 | async-start | bytes 5242880 | tf_op jit(solution)/shard_map/all_to_all | solution.py:193
  93.3 2.7 %slice.41 = bf16[320,2432]{1,0:T(8,128)(2,1)} slice(bf16[640,2432]{1,0:T(8,128)(2,1)} %collective-permute-done.1.rest_2_), slice={[0:320], [0:2432]} | slice | bytes 3112960 | tf_op jit(solution)/shard_map/slice | solution.py:161
  96.0 1.3 collective-permute-start.5
  97.3 2.7 %slice.42 = bf16[320,2432]{1,0:T(8,128)(2,1)} slice(bf16[640,2432]{1,0:T(8,128)(2,1)} %collective-permute-done.3.rest_4_), slice={[320:640], [0:2432]} | slice | bytes 3112960 | tf_op jit(solution)/shard_map/slice | solution.py:161
  101.2 22.3 %all-to-all-done.1 = bf16[4,8,160,256]{3,1,2,0:T(8,128)(2,1)S(1)} async-done(((bf16[4,8,160,256]{3,1,2,0:T(8,128)(2,1)}), bf16[4,8,160,256]{3,1,2,0:T(8,128)(2,1)S(1)}, u32[]{:S(2)}, u32[]{:S(2)}) %all-to-all-start.1) | async-done | bytes 2621472 | tf_op jit(solution)/shard_map/all_to_all | solution.py:193
  124.5 27.8 %all_to_all.31 = bf16[8,160,256]{2,1,0:T(8,128)(2,1)S(1)} all-to-all(bf16[8,160,256]{2,1,0:T(8,128)(2,1)S(1)} %copy.37), channel_id=1, replica_groups=mesh['y'=4,'c'=2,'z'=8,'x'=4] {'z'}, dimensions={0} | all-to-all | bytes 1310720 | tf_op jit(solution)/shard_map/all_to_all | solution.py:195
  153.8 1.4 copy.42
  159.1 31.5 %head.1 = (f32[256,2432]{1,0:T(8,128)}, f32[32,8,256]{2,1,0:T(8,128)}, bf16[896,256]{1,0:T(8,128)(2,1)}, bf16[896,256]{1,0:T(8,128)(2,1)}, bf16[896,256]{1,0:T(8...) custom-call(s32[9]{0:T(128)} %stack.75.place_ref, bf16[256,5120]{1,0:T(8,128)(2,1)} %bitcast.142, ...), custom_call_target="tpu_custom_call" | custom-call | flops 12750684160 | bytes 29884416 | tf_op jit(solution)/shard_map/head/pallas_call | solution.py:129
  190.6 5.6 %all-to-all-start.3 = ((f32[32,8,256]{2,1,0:T(8,128)}), f32[32,8,256]{2,1,0:T(8,128)S(1)}, u32[]{:S(2)}, u32[]{:S(2)}) async-start(f32[32,8,256]{2,1,0:T(8,128)} %get-tuple-element.23), calls=%async_computation.3 | async-start | bytes 524288 | tf_op jit(solution)/shard_map/all_to_all | solution.py:237
  197.5 5.7 %collective-permute-start.19 = (bf16[160,256]{1,0:T(8,128)(2,1)}, bf16[160,256]{1,0:T(8,128)(2,1)}, u32[]{:S(2)}, u32[]{:S(2)}) collective-permute-start(bf16[160,256]{1,0:T(8,128)(2,1)} %reduce_sum.133), channel_id=1, source_target_pairs={{0,0},{4,32},{8,64},{12,96},{16,128},{20,160},{24,192},{28,224},{3... | collective-permute-start | bytes 245768 | tf_op jit(solution)/shard_map/ppermute | solution.py:222
  203.8 2.4 collective-permute-start.14
  206.2 2.4 all-to-all-done.3
  208.6 1.3 fusion.41
  210.5 3.7 %all-to-all-start.5 = ((bf16[8,192,256]{2,1,0:T(8,128)(2,1)}), bf16[8,192,256]{2,1,0:T(8,128)(2,1)S(1)}, u32[]{:S(2)}, u32[]{:S(2)}) async-start(bf16[8,192,256]{2,1,0:T(8,128)(2,1)} %get-tuple-element.31), calls=%async_computation.5 | async-start | bytes 1572864 | tf_op jit(solution)/shard_map/all_to_all | solution.py:239
  217.0 2.1 collective-permute-done.14
  219.1 7.8 %collective-permute-done.15 = bf16[896,256]{1,0:T(8,128)(2,1)} collective-permute-done((bf16[896,256]{1,0:T(8,128)(2,1)}, bf16[896,256]{1,0:T(8,128)(2,1)}, u32[]{:S(2)}, u32[]{:S(2)}) %collective-permute-start.15) | collective-permute-done | bytes 458784 | tf_op jit(solution)/shard_map/ppermute | solution.py:24
  226.9 2.6 add_convert_fusion
  229.6 4.6 %collective-permute-start.11 = (f32[2,2,2,128]{3,2,1,0:T(2,128)S(1)}, f32[2,2,2,128]{3,2,1,0:T(2,128)S(1)}, u32[]{:S(2)}, u32[]{:S(2)}) collective-permute-start(f32[2,2,2,128]{3,2,1,0:T(2,128)S(1)} %get-tuple-element.72), channel_id=1, source_target_pairs={{0,128},{64,192},{128,0},{192,64},{1,129},{65,193},{129,1},{193,65... | collective-permute-start | bytes 12296 | tf_op jit(solution)/shard_map/ppermute | solution.py:24
  234.2 1.5 collective-permute-done.11
  235.8 3.2 %collective-permute-done.12 = f32[2,2,2,128]{3,2,1,0:T(2,128)S(1)} collective-permute-done((f32[2,2,2,128]{3,2,1,0:T(2,128)S(1)}, f32[2,2,2,128]{3,2,1,0:T(2,128)S(1)}, u32[]{:S(2)}, u32[]{:S(2)}) %collective-permute-start.12) | collective-permute-done | bytes 4128 | tf_op jit(solution)/shard_map/ppermute | solution.py:24
  242.6 4.1 %all-to-all-start.4 = ((bf16[8,112,256]{2,1,0:T(8,128)(2,1)}), bf16[8,112,256]{2,1,0:T(8,128)(2,1)}, u32[]{:S(2)}, u32[]{:S(2)}) async-start(bf16[8,112,256]{2,1,0:T(8,128)(2,1)} %bitcast.119), calls=%async_computation.4 | async-start | bytes 917504 | tf_op jit(solution)/shard_map/all_to_all | solution.py:260
  246.7 2.5 multiply_convert_fusion
  250.4 2.1 collective-permute-start.17
  252.6 8.9 %all-to-all-done.4 = bf16[8,112,256]{2,1,0:T(8,128)(2,1)} async-done(((bf16[8,112,256]{2,1,0:T(8,128)(2,1)}), bf16[8,112,256]{2,1,0:T(8,128)(2,1)}, u32[]{:S(2)}, u32[]{:S(2)}) %all-to-all-start.4) | async-done | bytes 458784 | tf_op jit(solution)/shard_map/all_to_all | solution.py:260
  262.7 1.6 copy_bitcast_fusion
  (84 shorter events, 18.2 us)
Async XLA Ops:
  0.6 92.7 %collective-permute-start.1 = (bf16[640,2432]{1,0:T(8,128)(2,1)}, bf16[640,2432]{1,0:T(8,128)(2,1)}, u32[]{:S(2)}, u32[]{:S(2)}) collective-permute-start(bf16[640,2432]{1,0:T(8,128)(2,1)} %rest_0_.1), channel_id=1, source_target_pairs={{0,64},{64,128},{128,192},{192,0},{1,65},{65,129},{129,193},{193,1... | collective-permute-start | bytes 9338888 | tf_op jit(solution)/shard_map/ppermute | solution.py:24
  0.9 96.4 %collective-permute-start.3 = (bf16[640,2432]{1,0:T(8,128)(2,1)}, bf16[640,2432]{1,0:T(8,128)(2,1)}, u32[]{:S(2)}, u32[]{:S(2)}) collective-permute-start(bf16[640,2432]{1,0:T(8,128)(2,1)} %rest_0_.1), channel_id=1, source_target_pairs={{0,192},{64,0},{128,64},{192,128},{1,193},{65,1},{129,65},{193,129... | collective-permute-start | bytes 9338888 | tf_op jit(solution)/shard_map/ppermute | solution.py:24
  4.0 67.5 %all-to-all-start = ((s32[8,1,256]{2,1,0:T(1,128)}), s32[8,1,256]{2,1,0:T(1,128)S(1)}, u32[]{:S(2)}, u32[]{:S(2)}) async-start(s32[8,1,256]{2,1,0:T(1,128)} %broadcast_in_dim.17), calls=%async_computation | async-start | bytes 16384 | tf_op jit(solution)/shard_map/all_to_all | solution.py:19
  88.6 34.9 %all-to-all-start.1 = ((bf16[4,8,160,256]{3,1,2,0:T(8,128)(2,1)}), bf16[4,8,160,256]{3,1,2,0:T(8,128)(2,1)S(1)}, u32[]{:S(2)}, u32[]{:S(2)}) async-start(bf16[4,8,160,256]{3,1,2,0:T(8,128)(2,1)} %bitcast_bitcast_fusion), calls=%async_computation.1 | async-start | bytes 5242880 | tf_op jit(solution)/shard_map/all_to_all | solution.py:193
  96.0 57.0 %collective-permute-start.5 = (bf16[320,2432]{1,0:T(8,128)(2,1)}, bf16[320,2432]{1,0:T(8,128)(2,1)}, u32[]{:S(2)}, u32[]{:S(2)}) collective-permute-start(bf16[320,2432]{1,0:T(8,128)(2,1)} %slice.41), channel_id=1, source_target_pairs={{0,64},{64,128},{128,192},{192,0},{1,65},{65,129},{129,193},{193,1... | collective-permute-start | bytes 4669448 | tf_op jit(solution)/shard_map/ppermute | solution.py:24
  100.0 53.1 %collective-permute-start.6 = (bf16[320,2432]{1,0:T(8,128)(2,1)}, bf16[320,2432]{1,0:T(8,128)(2,1)}, u32[]{:S(2)}, u32[]{:S(2)}) collective-permute-start(bf16[320,2432]{1,0:T(8,128)(2,1)} %slice.42), channel_id=1, source_target_pairs={{0,192},{64,0},{128,64},{192,128},{1,193},{65,1},{129,65},{193,129... | collective-permute-start | bytes 4669448 | tf_op jit(solution)/shard_map/ppermute | solution.py:24
  100.7 56.8 %collective-permute-start = (bf16[640,2432]{1,0:T(8,128)(2,1)}, bf16[640,2432]{1,0:T(8,128)(2,1)}, u32[]{:S(2)}, u32[]{:S(2)}) collective-permute-start(bf16[640,2432]{1,0:T(8,128)(2,1)} %rest_0_.1), channel_id=1, source_target_pairs={{0,32},{32,0},{1,33},{33,1},{2,34},{34,2},{3,35},{35,3},{4,36},{36... | collective-permute-start | bytes 9338888 | tf_op jit(solution)/shard_map/ppermute | solution.py:24
  100.7 58.3 %collective-permute-start.2 = (bf16[640,2432]{1,0:T(8,128)(2,1)}, bf16[640,2432]{1,0:T(8,128)(2,1)}, u32[]{:S(2)}, u32[]{:S(2)}) collective-permute-start(bf16[640,2432]{1,0:T(8,128)(2,1)} %collective-permute-done.1.rest_2_), channel_id=1, source_target_pairs={{0,32},{32,0},{1,33},{33,1},{2,34},{34,2},{3,35},{35,3},{4,36},{36... | collective-permute-start | bytes 9338888 | tf_op jit(solution)/shard_map/ppermute | solution.py:24
  101.2 57.8 %collective-permute-start.4 = (bf16[640,2432]{1,0:T(8,128)(2,1)}, bf16[640,2432]{1,0:T(8,128)(2,1)}, u32[]{:S(2)}, u32[]{:S(2)}) collective-permute-start(bf16[640,2432]{1,0:T(8,128)(2,1)} %collective-permute-done.3.rest_4_), channel_id=1, source_target_pairs={{0,32},{32,0},{1,33},{33,1},{2,34},{34,2},{3,35},{35,3},{4,36},{36... | collective-permute-start | bytes 9338888 | tf_op jit(solution)/shard_map/ppermute | solution.py:24
  124.3 29.2 %copy-start = (bf16[2,128,2432]{2,1,0:T(8,128)(2,1)S(1)}, bf16[2,128,2432]{2,1,0:T(8,128)(2,1)}, u32[]{:S(2)}) copy-start(bf16[2,128,2432]{2,1,0:T(8,128)(2,1)} %param.9) | copy-start | bytes 3735556
  153.0 4.9 %collective-permute-start.7 = (bf16[320,2432]{1,0:T(8,128)(2,1)}, bf16[320,2432]{1,0:T(8,128)(2,1)S(1)}, u32[]{:S(2)}, u32[]{:S(2)}) collective-permute-start(bf16[320,2432]{1,0:T(8,128)(2,1)} %collective-permute-done.5.rest_6_), channel_id=1, source_target_pairs={{0,32},{32,0},{1,33},{33,1},{2,34},{34,2},{3,35},{35,3},{4,36},{36... | collective-permute-start | bytes 4669448 | tf_op jit(solution)/shard_map/ppermute | solution.py:24
  153.1 5.9 %collective-permute-start.8 = (bf16[320,2432]{1,0:T(8,128)(2,1)}, bf16[320,2432]{1,0:T(8,128)(2,1)}, u32[]{:S(2)}, u32[]{:S(2)}) collective-permute-start(bf16[320,2432]{1,0:T(8,128)(2,1)} %collective-permute-done.6.rest_7_), channel_id=1, source_target_pairs={{0,32},{32,0},{1,33},{33,1},{2,34},{34,2},{3,35},{35,3},{4,36},{36... | collective-permute-start | bytes 4669448 | tf_op jit(solution)/shard_map/ppermute | solution.py:24
  153.6 2.9 %copy-start.3 = (s32[2,128]{1,0:T(2,128)S(1)}, s32[2,128]{1,0:T(2,128)}, u32[]{:S(2)}) copy-start(s32[2,128]{1,0:T(2,128)} %param.10) | copy-start | bytes 3076
  157.9 1.2 copy-start.6
  190.6 17.9 %all-to-all-start.3 = ((f32[32,8,256]{2,1,0:T(8,128)}), f32[32,8,256]{2,1,0:T(8,128)S(1)}, u32[]{:S(2)}, u32[]{:S(2)}) async-start(f32[32,8,256]{2,1,0:T(8,128)} %get-tuple-element.23), calls=%async_computation.3 | async-start | bytes 524288 | tf_op jit(solution)/shard_map/all_to_all | solution.py:237
  197.5 65.2 %collective-permute-start.19 = (bf16[160,256]{1,0:T(8,128)(2,1)}, bf16[160,256]{1,0:T(8,128)(2,1)}, u32[]{:S(2)}, u32[]{:S(2)}) collective-permute-start(bf16[160,256]{1,0:T(8,128)(2,1)} %reduce_sum.133), channel_id=1, source_target_pairs={{0,0},{4,32},{8,64},{12,96},{16,128},{20,160},{24,192},{28,224},{3... | collective-permute-start | bytes 245768 | tf_op jit(solution)/shard_map/ppermute | solution.py:222
  203.2 13.8 %collective-permute-start.13 = (bf16[896,256]{1,0:T(8,128)(2,1)}, bf16[896,256]{1,0:T(8,128)(2,1)}, u32[]{:S(2)}, u32[]{:S(2)}) collective-permute-start(bf16[896,256]{1,0:T(8,128)(2,1)} %get-tuple-element.28), channel_id=1, source_target_pairs={{0,1},{1,2},{2,3},{3,0},{4,5},{5,6},{6,7},{7,4},{8,9},{9,10},{10,1... | collective-permute-start | bytes 1376264 | tf_op jit(solution)/shard_map/ppermute | solution.py:24
  203.8 15.3 %collective-permute-start.14 = (bf16[896,256]{1,0:T(8,128)(2,1)}, bf16[896,256]{1,0:T(8,128)(2,1)}, u32[]{:S(2)}, u32[]{:S(2)}) collective-permute-start(bf16[896,256]{1,0:T(8,128)(2,1)} %get-tuple-element.29), channel_id=1, source_target_pairs={{0,2},{1,3},{2,0},{3,1},{4,6},{5,7},{6,4},{7,5},{8,10},{9,11},{10,... | collective-permute-start | bytes 1376264 | tf_op jit(solution)/shard_map/ppermute | solution.py:24
  206.2 20.8 %collective-permute-start.15 = (bf16[896,256]{1,0:T(8,128)(2,1)}, bf16[896,256]{1,0:T(8,128)(2,1)}, u32[]{:S(2)}, u32[]{:S(2)}) collective-permute-start(bf16[896,256]{1,0:T(8,128)(2,1)} %get-tuple-element.30), channel_id=1, source_target_pairs={{0,3},{1,0},{2,1},{3,2},{4,7},{5,4},{6,5},{7,6},{8,11},{9,8},{10,9... | collective-permute-start | bytes 1376264 | tf_op jit(solution)/shard_map/ppermute | solution.py:24
  210.5 36.2 %copy-start.1 = (f32[256,2432]{1,0:T(8,128)S(1)}, f32[256,2432]{1,0:T(8,128)}, u32[]{:S(2)}) copy-start(f32[256,2432]{1,0:T(8,128)} %get-tuple-element.26) | copy-start | bytes 7471108
  210.5 32.0 %all-to-all-start.5 = ((bf16[8,192,256]{2,1,0:T(8,128)(2,1)}), bf16[8,192,256]{2,1,0:T(8,128)(2,1)S(1)}, u32[]{:S(2)}, u32[]{:S(2)}) async-start(bf16[8,192,256]{2,1,0:T(8,128)(2,1)} %get-tuple-element.31), calls=%async_computation.5 | async-start | bytes 1572864 | tf_op jit(solution)/shard_map/all_to_all | solution.py:239
  215.1 25.2 %copy-start.2 = (f32[8,8]{1,0:T(8,128)S(1)}, f32[8,8]{1,0:T(8,128)}, u32[]{:S(2)}) copy-start(f32[8,8]{1,0:T(8,128)} %fusion.33) | copy-start | bytes 772
  215.1 27.5 %copy-start.5 = (f32[256]{0:T(256)S(1)}, f32[256]{0:T(256)}, u32[]{:S(2)}) copy-start(f32[256]{0:T(256)} %get-tuple-element.63) | copy-start | bytes 3076
  215.9 13.6 %collective-permute-start.9 = (f32[2,2,128]{2,1,0:T(2,128)S(1)}, f32[2,2,128]{2,1,0:T(2,128)S(1)}, u32[]{:S(2)}, u32[]{:S(2)}) collective-permute-start(f32[2,2,128]{2,1,0:T(2,128)S(1)} %get-tuple-element.74), channel_id=1, source_target_pairs={{0,32},{32,0},{1,33},{33,1},{2,34},{34,2},{3,35},{35,3},{4,36},{36... | collective-permute-start | bytes 6152 | tf_op jit(solution)/shard_map/ppermute | solution.py:24
  229.5 4.7 %collective-permute-start.10 = (f32[2,2,2,128]{3,2,1,0:T(2,128)S(1)}, f32[2,2,2,128]{3,2,1,0:T(2,128)S(1)}, u32[]{:S(2)}, u32[]{:S(2)}) collective-permute-start(f32[2,2,2,128]{3,2,1,0:T(2,128)S(1)} %get-tuple-element.72), channel_id=1, source_target_pairs={{0,64},{64,128},{128,192},{192,0},{1,65},{65,129},{129,193},{193,1... | collective-permute-start | bytes 12296 | tf_op jit(solution)/shard_map/ppermute | solution.py:24
  229.6 6.1 %collective-permute-start.11 = (f32[2,2,2,128]{3,2,1,0:T(2,128)S(1)}, f32[2,2,2,128]{3,2,1,0:T(2,128)S(1)}, u32[]{:S(2)}, u32[]{:S(2)}) collective-permute-start(f32[2,2,2,128]{3,2,1,0:T(2,128)S(1)} %get-tuple-element.72), channel_id=1, source_target_pairs={{0,128},{64,192},{128,0},{192,64},{1,129},{65,193},{129,1},{193,65... | collective-permute-start | bytes 12296 | tf_op jit(solution)/shard_map/ppermute | solution.py:24
  234.2 4.8 %collective-permute-start.12 = (f32[2,2,2,128]{3,2,1,0:T(2,128)S(1)}, f32[2,2,2,128]{3,2,1,0:T(2,128)S(1)}, u32[]{:S(2)}, u32[]{:S(2)}) collective-permute-start(f32[2,2,2,128]{3,2,1,0:T(2,128)S(1)} %get-tuple-element.72), channel_id=1, source_target_pairs={{0,192},{64,0},{128,64},{192,128},{1,193},{65,1},{129,65},{193,129... | collective-permute-start | bytes 12296 | tf_op jit(solution)/shard_map/ppermute | solution.py:24
  242.5 6.8 %copy-start.4 = (f32[1,2,128]{2,0,1:T(1,128)}, f32[1,2,128]{2,0,1:T(1,128)S(1)}, u32[]{:S(2)}) copy-start(f32[1,2,128]{2,0,1:T(1,128)S(1)} %fusion.36) | copy-start | bytes 3076
  242.6 19.0 %all-to-all-start.4 = ((bf16[8,112,256]{2,1,0:T(8,128)(2,1)}), bf16[8,112,256]{2,1,0:T(8,128)(2,1)}, u32[]{:S(2)}, u32[]{:S(2)}) async-start(bf16[8,112,256]{2,1,0:T(8,128)(2,1)} %bitcast.119), calls=%async_computation.4 | async-start | bytes 917504 | tf_op jit(solution)/shard_map/all_to_all | solution.py:260
  249.4 13.2 %collective-permute-start.16 = (bf16[48,256]{1,0:T(8,128)(2,1)S(1)}, bf16[48,256]{1,0:T(8,128)(2,1)S(1)}, u32[]{:S(2)}, u32[]{:S(2)}) collective-permute-start(bf16[48,256]{1,0:T(8,128)(2,1)S(1)} %get-tuple-element.64), channel_id=1, source_target_pairs={{0,1},{1,2},{2,3},{3,0},{4,5},{5,6},{6,7},{7,4},{8,9},{9,10},{10,1... | collective-permute-start | bytes 73736 | tf_op jit(solution)/shard_map/ppermute | solution.py:24
  250.4 12.3 %collective-permute-start.17 = (bf16[48,256]{1,0:T(8,128)(2,1)S(1)}, bf16[48,256]{1,0:T(8,128)(2,1)S(1)}, u32[]{:S(2)}, u32[]{:S(2)}) collective-permute-start(bf16[48,256]{1,0:T(8,128)(2,1)S(1)} %get-tuple-element.66), channel_id=1, source_target_pairs={{0,2},{1,3},{2,0},{3,1},{4,6},{5,7},{6,4},{7,5},{8,10},{9,11},{10,... | collective-permute-start | bytes 73736 | tf_op jit(solution)/shard_map/ppermute | solution.py:24
  252.5 10.2 %collective-permute-start.18 = (bf16[48,256]{1,0:T(8,128)(2,1)S(1)}, bf16[48,256]{1,0:T(8,128)(2,1)S(1)}, u32[]{:S(2)}, u32[]{:S(2)}) collective-permute-start(bf16[48,256]{1,0:T(8,128)(2,1)S(1)} %get-tuple-element.65), channel_id=1, source_target_pairs={{0,3},{1,0},{2,1},{3,2},{4,7},{5,4},{6,5},{7,6},{8,11},{9,8},{10,9... | collective-permute-start | bytes 73736 | tf_op jit(solution)/shard_map/ppermute | solution.py:24

commit v7 on v6

--- a/solution.py
+++ b/solution.py
@@ -11,6 +11,7 @@
 VOC = ("z", "x")
 TILE = 128
 SUB = 8
+WIDE = 8
 FIRST = 112
 
 
@@ -24,8 +25,7 @@
     return lax.ppermute(value, axis, [(i, (i + by) % count) for i in range(count)])
 
 
-def head_kernel(sizes, place_ref, state_hbm, ref_hbm, token_ref, lse_ref, *rest):
-    count, blocks = sum(sizes), len(sizes)
+def head_kernel(count, blocks, place_ref, state_hbm, ref_hbm, token_ref, lse_ref, *rest):
     heads, rest = rest[:count], rest[count:]
     logit_hbm, stat_ref, back0, back1, back2, back3, by_block = rest[:7]
     state, refs, head, logit, flipped, turned, result, sems, outsem = rest[7:]
@@ -36,42 +36,43 @@
     parts = len(backs)
     piece = depth // parts
     first = back0.shape[0] // blocks
+    edges = list(range(0, columns, WIDE * TILE)) + [columns]
+    spans = [slice(low, high) for low, high in zip(edges, edges[1:])]
 
     get_state = pltpu.make_async_copy(state_hbm, state, outsem.at[0])
     get_refs = pltpu.make_async_copy(ref_hbm, refs, outsem.at[1])
+
+    def fetch(tile):
+        copies = []
+        for index, part in enumerate(heads):
+            place = pl.ds(pl.multiple_of(place_ref[1 + index], SUB * 4), part.shape[0])
+            copies.append(
+                pltpu.make_async_copy(
+                    part.at[:, spans[tile]], head.at[place, spans[tile]], sems.at[tile, index]
+                )
+            )
+            copies[-1].start()
+        return copies
+
     get_state.start()
-    fetches, at = [], 0
-    for block, size in enumerate(sizes):
-        start = pl.multiple_of(place_ref[1 + block] * depth, depth)
-        copies = []
-        for part in heads[at : at + size]:
-            span = pl.ds(start, part.shape[0])
-            copies.append(pltpu.make_async_copy(part, head.at[span], sems.at[at]))
-            copies[-1].start()
-            start = pl.multiple_of(start + part.shape[0], SUB * 4)
-            at += 1
-        fetches.append(copies)
-    get_refs.start()
+    copies = [fetch(0), fetch(1)]
     get_state.wait()
-
-    for block, copies in enumerate(fetches):
-        for copy in copies:
+    best = jnp.full((SUB, rows), -jnp.inf, jnp.float32)
+    for tile, span in enumerate(spans):
+        for copy in copies[tile]:
             copy.wait()
-        span = pl.ds(pl.multiple_of(place_ref[1 + block] * depth, depth), depth)
-        term = jnp.dot(state[:, span], head[span, :], preferred_element_type=jnp.float32)
-        logit[...] = term if block == 0 else logit[...] + term
+        if tile + 2 < len(spans):
+            copies.append(fetch(tile + 2))
+        if tile + 2 == len(spans):
+            get_refs.start()
+        values = jnp.dot(state[...], head[:, span], preferred_element_type=jnp.float32)
+        logit[:, span] = values
+        values = values.T
+        flipped[span, :] = values
+        best = jnp.maximum(best, jnp.max(values.reshape(-1, SUB, rows), axis=0))
+    top = jnp.max(best, axis=0, keepdims=True)
     put_logit = pltpu.make_async_copy(logit, logit_hbm, outsem.at[0])
     put_logit.start()
-
-    def flip(tile, best):
-        span = pl.ds(pl.multiple_of(tile * TILE, TILE), TILE)
-        values = logit[:, span].T
-        flipped[span, :] = values
-        return jnp.maximum(best, jnp.max(values.reshape(TILE // SUB, SUB, rows), axis=0))
-
-    best = jnp.full((SUB, rows), -jnp.inf, jnp.float32)
-    best = lax.fori_loop(0, columns // TILE, flip, best)
-    top = jnp.max(best, axis=0, keepdims=True)
     get_refs.wait()
 
     column = lax.broadcasted_iota(jnp.int32, (TILE, rows), 0)
@@ -117,9 +118,7 @@
 
     put_logit.wait()
 
-def run_head(states, refs, tokens, ref_lse, place, shards, parts, first, peers):
-    heads = [part for shard in shards for part in shard]
-    blocks = len(shards)
+def run_head(states, refs, tokens, ref_lse, place, heads, blocks, parts, first, peers):
     rows, width = states.shape
     columns = heads[0].shape[1]
     vmem = pl.BlockSpec(memory_space=pltpu.VMEM)
@@ -127,7 +126,7 @@
     back = jax.ShapeDtypeStruct((blocks * first, rows), jnp.bfloat16)
     rest = width // blocks - parts * first
     return pl.pallas_call(
-        functools.partial(head_kernel, tuple(len(shard) for shard in shards)),
+        functools.partial(head_kernel, len(heads), blocks),
         out_shape=(
             jax.ShapeDtypeStruct((rows, columns), jnp.float32),
             jax.ShapeDtypeStruct((peers, SUB, rows), jnp.float32),
@@ -142,7 +141,7 @@
             pltpu.VMEM((columns, rows), jnp.float32),
             pltpu.VMEM((columns, rows), jnp.bfloat16),
             pltpu.VMEM((width // blocks, rows), jnp.bfloat16),
-            pltpu.SemaphoreType.DMA((len(heads),)),
+            pltpu.SemaphoreType.DMA((-(-columns // (WIDE * TILE)), len(heads))),
             pltpu.SemaphoreType.DMA((2,)),
         ],
         compiler_params=pltpu.CompilerParams(vmem_limit_bytes=56 << 20),
@@ -157,39 +156,39 @@
 
 def gather_rows(head_weight):
     half = head_weight.shape[0] // 2
-    near = [rotate(head_weight, "y", 1), rotate(head_weight, "y", -1)]
-    far = [rotate(near[0][:half], "y", 1), rotate(near[1][half:], "y", -1)]
-    return near, far
-
-
-def swap_cores(head_weight, near, far, after):
+    upper, lower = head_weight[:half], head_weight[half:]
+    near = [rotate(upper, "y", 1), rotate(lower, "y", -1)]
+    late = [rotate(lower, "y", 1), rotate(upper, "y", -1)]
+    far = [rotate(near[0], "y", 1), rotate(near[1], "y", -1)]
+    own_swap = rotate(head_weight, "c", 1)
+    return own_swap, near, list(zip(near + late + far, (-1, 1, -1, 1, 2, 2), (0, half, half, 0, 0, half)))
+
+
+def swap_cores(head_weight, own_swap, gathered, after):
+    depth = head_weight.shape[0]
     ys, cores = lax.axis_size("y"), lax.axis_size("c")
     y, core = lax.axis_index("y"), lax.axis_index("c")
-    late, _ = lax.optimization_barrier((far, after))
-    shards, owners = [], []
-    for shard, sent, step in (
-        ([head_weight], [head_weight], 0),
-        (near[:1], near[:1], -1),
-        (near[1:], near[1:], 1),
-        (far, late, 2),
-    ):
+    pieces, starts = [], []
+    for piece, step, row in [(head_weight, 0, 0)] + gathered:
+        sent = lax.optimization_barrier((piece, after))[0] if step == 2 else piece
         chip = lax.rem(y + step + ys, ys) * cores
-        shards += [shard, [rotate(part, "c", 1) for part in sent]]
-        owners += [chip + core, chip + 1 - core]
-    return shards, owners
-
-
-def token_columns(head_weight, token_ids, vocab_start):
+        pieces += [piece, own_swap if step == 0 else rotate(sent, "c", 1)]
+        starts += [(chip + core) * depth + row, (chip + 1 - core) * depth + row]
+    return pieces, starts
+
+
+def token_columns(head_weight, ids, vocab_start, own_swap, near):
     depth, vocab_dev = head_weight.shape
     seqs, xs = lax.axis_size(SEQ), lax.axis_size("x")
-    rows = token_ids.size
-    ids = spread(token_ids.reshape(rows), SEQ).reshape(seqs * rows, 1)
+    rows = ids.size // seqs
     column = vocab_start + lax.broadcasted_iota(jnp.int32, (1, vocab_dev), 1)
     onehot = (column == ids).astype(jnp.bfloat16)
+    head_weight, _ = lax.optimization_barrier((head_weight, own_swap))
     found = lax.dot_general(
         head_weight, onehot, (((1,), (1,)), ((), ())), preferred_element_type=jnp.float32
     ).astype(jnp.bfloat16)
     found = found.reshape(xs, depth // xs, seqs, rows).transpose(0, 2, 1, 3)
+    found, _ = lax.optimization_barrier((found, near))
     found = lax.all_to_all(found, "x", 0, 0)
     found = jnp.sum(found.astype(jnp.float32), axis=0).astype(jnp.bfloat16)
     found = lax.all_to_all(found, "z", 0, 0)
@@ -206,9 +205,10 @@
     seq_start = seq_index * segment
     vocab_start = lax.axis_index(VOC) * vocab_dev
 
-    near, far = gather_rows(head_weight)
-    own_columns = token_columns(head_weight, token_ids, vocab_start)
-    shards, owners = swap_cores(head_weight, near, far, own_columns)
+    ids = spread(token_ids.reshape(rows), SEQ).reshape(seqs * rows, 1)
+    own_swap, near, gathered = gather_rows(head_weight)
+    own_columns = token_columns(head_weight, ids, vocab_start, own_swap, near)
+    pieces, starts = swap_cores(head_weight, own_swap, gathered, own_columns)
 
     refs = ref_logits.reshape(rows, vocab_dev)
     wide = refs.astype(jnp.float32)
@@ -227,8 +227,9 @@
         turned_refs,
         (tokens - vocab_start).reshape(1, rows),
         ref_lse[None],
-        jnp.stack([x_index] + owners),
-        shards,
+        jnp.stack([x_index] + starts),
+        pieces,
+        seqs,
         xs,
         FIRST,
         lax.axis_size(VOC),

time: 265 us -> 239 us (0.902)
  waiting for transfers between devices: 113 us -> 90.5 us
  starting transfers between devices: 44.7 us -> 53.9 us
  local copies, waits for them, and re-layouts: 15.3 us -> 10.7 us
  matrix products: 12.2 us -> 8.13 us
  Pallas kernels: 31.5 us -> 27.7 us
    all_to_all x1, waiting for transfers between devices: 62.8 us -> 0.01 us  [spread(): lax.all_to_all(jnp.broadcast_to(value[None], (count,) + value.shape), axe...]
    ppermute x19 -> x23, waiting for transfers between devices: 16.4 us -> 55 us  [rotate(): lax.ppermute(value, axis, [(i, (i + by) % count) for i in range(count)])]
    all_to_all x1, starting transfers between devices: 5.58 us -> 11.6 us  [per_device(): stats = lax.all_to_all(stats, VOC, 0, 0)]
    dot_general x1, matrix products: 11.5 us -> 7.37 us  [token_columns(): lax.dot_general(head_weight, onehot, (((1,), (1,)), ((), ())), preferred_...]
    pallas_call x1, Pallas kernels: 31.5 us -> 27.7 us  [run_head(): pl.pallas_call(functools.partial(head_kernel, len(heads), blocks), out_sh...]
    all_to_all x1, waiting for transfers between devices: 22.3 us -> 25.4 us  [token_columns(): found = lax.all_to_all(found, 'x', 0, 0)]
    convert_element_type x1 -> x0, local copies, waits for them, and re-layouts: 2.99 us -> none  [token_columns(): found = lax.dot_general(head_weight, onehot, (((1,), (1,)), ((), ())), pr...]
    ppermute x19 -> x23, starting transfers between devices: 16.1 us -> 18.2 us  [rotate(): lax.ppermute(value, axis, [(i, (i + by) % count) for i in range(count)])]
  transfers between devices with their start and end apart: 25 -> 29, of which waited for: 11 -> 13; matrix products, arithmetic and copies ran while one was open for 16% -> 14% of each run, Pallas kernels for 0% -> 0%
where the time goes in v7:
time: 239 us; the launch traced here: 238 us
  waiting for transfers between devices  90.5 us (38%)
  starting transfers between devices  53.9 us (23%)
  Pallas kernels  27.7 us (12%)
  blocking collectives  27.1 us (11%)
  other arithmetic  17.1 us (7%)
  local copies, waits for them, and re-layouts  10.7 us (4%)
  matrix products  8.13 us (3%)
  between operations  2.99 us (1%)
    ppermute x23, waiting for transfers between devices, rotate(): lax.ppermute(value, axis, [(i, (i + by) % count) for i in range(count)])  55 us
    pallas_call x1, Pallas kernels, run_head(): pl.pallas_call(functools.partial(head_kernel, len(heads), blocks), out_sh...  27.7 us
    all_to_all x1, blocking collectives, token_columns(): found = lax.all_to_all(found, 'z', 0, 0)  27.1 us
    all_to_all x1, waiting for transfers between devices, token_columns(): found = lax.all_to_all(found, 'x', 0, 0)  25.4 us
    ppermute x23, starting transfers between devices, rotate(): lax.ppermute(value, axis, [(i, (i + by) % count) for i in range(count)])  18.2 us
    all_to_all x1, starting transfers between devices, per_device(): stats = lax.all_to_all(stats, VOC, 0, 0)  11.6 us
    all_to_all x1, waiting for transfers between devices, per_device(): back = lax.all_to_all(back, 'z', 0, 0)  8.89 us
    dot_general x1, matrix products, token_columns(): lax.dot_general(head_weight, onehot, (((1,), (1,)), ((), ())), preferred_...  7.37 us
  transfers between devices with their start and end apart: 29, of which 13 were waited for; matrix products, arithmetic and copies ran while one was open for 14% of the time, Pallas kernels for 0%

profile of v7, /device:TPU:30, one launch (start us, length us, event | category | flops | bytes accessed | tf_op | source)
XLA Modules:
  0.0 238.1 jit_solution(12436458780254774365)
XLA Ops:
  2.0 4.8 %all-to-all-start = ((s32[8,1,256]{2,1,0:T(1,128)}), s32[8,1,256]{2,1,0:T(1,128)S(1)}, u32[]{:S(2)}, u32[]{:S(2)}) async-start(s32[8,1,256]{2,1,0:T(1,128)} %broadcast_in_dim.17), calls=%async_computation | async-start | bytes 16384 | tf_op jit(solution)/shard_map/all_to_all | solution.py:20
  6.8 3.9 %fusion.37 = (bf16[320,2432]{1,0:T(8,128)(2,1)}, bf16[320,2432]{1,0:T(8,128)(2,1)}) fusion(bf16[640,2432]{1,0:T(8,128)(2,1)} %rest_0_.1), kind=kLoop, calls=%fused_computation.95 | loop fusion | bytes 6225920 | tf_op jit(solution)/shard_map/slice | solution.py:159
  10.7 2.0 collective-permute-start.2
  12.7 7.4 %fusion.4 = bf16[640,2048]{1,0:T(8,128)(2,1)S(1)} fusion(bf16[640,2432]{1,0:T(8,128)(2,1)S(1)} %copy-done.1, s32[2432]{0:T(1024)S(1)} %iota_add_fusion, s32[2048]{0:T(1024)S(1)} %bitcast.133), kind=kOutput, calls=%fused_computation.4 | convolution fusion | flops 6381633536 | bytes 5752320 | tf_op jit(solution)/shard_map/dot_general | solution.py:187
  21.0 1.7 bitcast_bitcast_fusion
  22.6 24.4 %collective-permute-done.1.rest_2_ = bf16[320,2432]{1,0:T(8,128)(2,1)} collective-permute-done((bf16[320,2432]{1,0:T(8,128)(2,1)}, bf16[320,2432]{1,0:T(8,128)(2,1)}, u32[]{:S(2)}, u32[]{:S(2)}) %collective-permute-start.1) | collective-permute-done | bytes 1556512 | tf_op jit(solution)/shard_map/ppermute | solution.py:25
  48.4 4.8 %all-to-all-start.1 = ((bf16[4,8,160,256]{3,1,2,0:T(8,128)(2,1)}), bf16[4,8,160,256]{3,1,2,0:T(8,128)(2,1)S(1)}, u32[]{:S(2)}, u32[]{:S(2)}) async-start(bf16[4,8,160,256]{3,1,2,0:T(8,128)(2,1)} %bitcast_bitcast_fusion), calls=%async_computation.1 | async-start | bytes 5242880 | tf_op jit(solution)/shard_map/all_to_all | solution.py:192
  53.6 1.6 collective-permute-start.7
  55.2 1.7 collective-permute-start.9
  57.2 25.4 %all-to-all-done.1 = bf16[4,8,160,256]{3,1,2,0:T(8,128)(2,1)S(1)} async-done(((bf16[4,8,160,256]{3,1,2,0:T(8,128)(2,1)}), bf16[4,8,160,256]{3,1,2,0:T(8,128)(2,1)S(1)}, u32[]{:S(2)}, u32[]{:S(2)}) %all-to-all-start.1) | async-done | bytes 2621472 | tf_op jit(solution)/shard_map/all_to_all | solution.py:192
  83.6 27.1 %all_to_all.31 = bf16[8,160,256]{2,1,0:T(8,128)(2,1)S(1)} all-to-all(bf16[8,160,256]{2,1,0:T(8,128)(2,1)S(1)} %copy.33), channel_id=1, replica_groups=mesh['y'=4,'c'=2,'z'=8,'x'=4] {'z'}, dimensions={0} | all-to-all | bytes 1310720 | tf_op jit(solution)/shard_map/all_to_all | solution.py:194
  111.9 9.7 %collective-permute-done.9.rest_10_ = bf16[320,2432]{1,0:T(8,128)(2,1)} collective-permute-done((bf16[320,2432]{1,0:T(8,128)(2,1)}, bf16[320,2432]{1,0:T(8,128)(2,1)}, u32[]{:S(2)}, u32[]{:S(2)}) %collective-permute-start.9) | collective-permute-done | bytes 1556512 | tf_op jit(solution)/shard_map/ppermute | solution.py:25
  121.6 1.5 collective-permute-done.11.rest_12_
  123.9 1.4 copy.38
  127.8 2.0 collective-permute-done.12.rest_13_
  129.8 27.7 %head.1 = (f32[256,2432]{1,0:T(8,128)}, f32[32,8,256]{2,1,0:T(8,128)}, bf16[896,256]{1,0:T(8,128)(2,1)}, bf16[896,256]{1,0:T(8,128)(2,1)}, bf16[896,256]{1,0:T(8...) custom-call(s32[15]{0:T(128)} %stack.99.place_ref, bf16[256,5120]{1,0:T(8,128)(2,1)} %bitcast.146, ...), custom_call_target="tpu_custom_call" | custom-call | flops 12750684160 | bytes 29884416 | tf_op jit(solution)/shard_map/head/pallas_call | solution.py:128
  157.5 11.6 %all-to-all-start.3 = ((f32[32,8,256]{2,1,0:T(8,128)}), f32[32,8,256]{2,1,0:T(8,128)S(1)}, u32[]{:S(2)}, u32[]{:S(2)}) async-start(f32[32,8,256]{2,1,0:T(8,128)} %get-tuple-element.27), calls=%async_computation.3 | async-start | bytes 524288 | tf_op jit(solution)/shard_map/all_to_all | solution.py:238
  170.3 6.8 %collective-permute-start.23 = (bf16[160,256]{1,0:T(8,128)(2,1)}, bf16[160,256]{1,0:T(8,128)(2,1)}, u32[]{:S(2)}, u32[]{:S(2)}) collective-permute-start(bf16[160,256]{1,0:T(8,128)(2,1)} %reduce_sum.133), channel_id=1, source_target_pairs={{0,0},{4,32},{8,64},{12,96},{16,128},{20,160},{24,192},{28,224},{3... | collective-permute-start | bytes 245768 | tf_op jit(solution)/shard_map/ppermute | solution.py:222
  177.7 2.4 collective-permute-start.18
  180.1 1.3 all-to-all-done.3
  183.4 3.7 %all-to-all-start.5 = ((bf16[8,192,256]{2,1,0:T(8,128)(2,1)}), bf16[8,192,256]{2,1,0:T(8,128)(2,1)S(1)}, u32[]{:S(2)}, u32[]{:S(2)}) async-start(bf16[8,192,256]{2,1,0:T(8,128)(2,1)} %get-tuple-element.35), calls=%async_computation.5 | async-start | bytes 1572864 | tf_op jit(solution)/shard_map/all_to_all | solution.py:240
  190.9 2.1 collective-permute-done.18
  193.0 7.8 %collective-permute-done.19 = bf16[896,256]{1,0:T(8,128)(2,1)} collective-permute-done((bf16[896,256]{1,0:T(8,128)(2,1)}, bf16[896,256]{1,0:T(8,128)(2,1)}, u32[]{:S(2)}, u32[]{:S(2)}) %collective-permute-start.19) | collective-permute-done | bytes 458784 | tf_op jit(solution)/shard_map/ppermute | solution.py:25
  200.8 2.6 %add_convert_fusion = bf16[896,256]{1,0:T(8,128)(2,1)} fusion(bf16[896,256]{1,0:T(8,128)(2,1)} %collective-permute-done.19, bf16[896,256]{1,0:T(8,128)(2,1)} %collective-permute-done.18, bf16[896,256]{1,0:T(8,128)(2,1)} %collective-permute-done.17, bf16[896,256]{1,0:T(8,128)(2,1)} %get-tuple-element.31, f32[256]{0:T(256)S(1)} %bitcast.135, ...), kind=kLoop, calls=%fused_computation.11 | loop fusion | flops 2752512 | bytes 2297856 | tf_op jit(solution)/shard_map/convert_element_type | solution.py:260
  203.5 4.6 %collective-permute-start.15 = (f32[2,2,2,128]{3,2,1,0:T(2,128)S(1)}, f32[2,2,2,128]{3,2,1,0:T(2,128)S(1)}, u32[]{:S(2)}, u32[]{:S(2)}) collective-permute-start(f32[2,2,2,128]{3,2,1,0:T(2,128)S(1)} %get-tuple-element.78), channel_id=1, source_target_pairs={{0,128},{64,192},{128,0},{192,64},{1,129},{65,193},{129,1},{193,65... | collective-permute-start | bytes 12296 | tf_op jit(solution)/shard_map/ppermute | solution.py:25
  208.1 1.5 collective-permute-done.15
  209.7 3.2 %collective-permute-done.16 = f32[2,2,2,128]{3,2,1,0:T(2,128)S(1)} collective-permute-done((f32[2,2,2,128]{3,2,1,0:T(2,128)S(1)}, f32[2,2,2,128]{3,2,1,0:T(2,128)S(1)}, u32[]{:S(2)}, u32[]{:S(2)}) %collective-permute-start.16) | collective-permute-done | bytes 4128 | tf_op jit(solution)/shard_map/ppermute | solution.py:25
  216.5 4.1 %all-to-all-start.4 = ((bf16[8,112,256]{2,1,0:T(8,128)(2,1)}), bf16[8,112,256]{2,1,0:T(8,128)(2,1)}, u32[]{:S(2)}, u32[]{:S(2)}) async-start(bf16[8,112,256]{2,1,0:T(8,128)(2,1)} %bitcast.123), calls=%async_computation.4 | async-start | bytes 917504 | tf_op jit(solution)/shard_map/all_to_all | solution.py:261
  220.6 2.5 %multiply_convert_fusion = bf16[256,2432]{1,0:T(8,128)(2,1)} fusion(f32[256,2432]{1,0:T(8,128)S(1)} %copy-done.2, s32[2432]{0:T(1024)S(1)} %iota_add_fusion, f32[256]{0:T(256)S(1)} %get-tuple-element.61, f32[256]{0:T(256)S(1)} %get-tuple-element.58, s32[256]{0:T(256)} %bitcast.132), kind=kLoop, calls=%fused_computation.6 | loop fusion | flops 3735552 | bytes 3748352 | tf_op jit(solution)/shard_map/convert_element_type | solution.py:311
  224.3 2.1 collective-permute-start.21
  226.5 8.9 %all-to-all-done.4 = bf16[8,112,256]{2,1,0:T(8,128)(2,1)} async-done(((bf16[8,112,256]{2,1,0:T(8,128)(2,1)}), bf16[8,112,256]{2,1,0:T(8,128)(2,1)}, u32[]{:S(2)}, u32[]{:S(2)}) %all-to-all-start.4) | async-done | bytes 458784 | tf_op jit(solution)/shard_map/all_to_all | solution.py:261
  236.6 1.6 copy_bitcast_fusion
  (92 shorter events, 21.5 us)
Async XLA Ops:
  0.6 12.1 %collective-permute-start = (bf16[640,2432]{1,0:T(8,128)(2,1)}, bf16[640,2432]{1,0:T(8,128)(2,1)}, u32[]{:S(2)}, u32[]{:S(2)}) collective-permute-start(bf16[640,2432]{1,0:T(8,128)(2,1)} %rest_0_.1), channel_id=1, source_target_pairs={{0,32},{32,0},{1,33},{33,1},{2,34},{34,2},{3,35},{35,3},{4,36},{36... | collective-permute-start | bytes 9338888 | tf_op jit(solution)/shard_map/ppermute | solution.py:25
  2.0 10.7 %all-to-all-start = ((s32[8,1,256]{2,1,0:T(1,128)}), s32[8,1,256]{2,1,0:T(1,128)S(1)}, u32[]{:S(2)}, u32[]{:S(2)}) async-start(s32[8,1,256]{2,1,0:T(1,128)} %broadcast_in_dim.17), calls=%async_computation | async-start | bytes 16384 | tf_op jit(solution)/shard_map/all_to_all | solution.py:20
  10.7 36.4 %collective-permute-start.1 = (bf16[320,2432]{1,0:T(8,128)(2,1)}, bf16[320,2432]{1,0:T(8,128)(2,1)}, u32[]{:S(2)}, u32[]{:S(2)}) collective-permute-start(bf16[320,2432]{1,0:T(8,128)(2,1)} %get-tuple-element.63), channel_id=1, source_target_pairs={{0,64},{64,128},{128,192},{192,0},{1,65},{65,129},{129,193},{193,1... | collective-permute-start | bytes 4669448 | tf_op jit(solution)/shard_map/ppermute | solution.py:25
  10.7 37.7 %collective-permute-start.2 = (bf16[320,2432]{1,0:T(8,128)(2,1)}, bf16[320,2432]{1,0:T(8,128)(2,1)}, u32[]{:S(2)}, u32[]{:S(2)}) collective-permute-start(bf16[320,2432]{1,0:T(8,128)(2,1)} %get-tuple-element.62), channel_id=1, source_target_pairs={{0,192},{64,0},{128,64},{192,128},{1,193},{65,1},{129,65},{193,129... | collective-permute-start | bytes 4669448 | tf_op jit(solution)/shard_map/ppermute | solution.py:25
  48.4 34.2 %all-to-all-start.1 = ((bf16[4,8,160,256]{3,1,2,0:T(8,128)(2,1)}), bf16[4,8,160,256]{3,1,2,0:T(8,128)(2,1)S(1)}, u32[]{:S(2)}, u32[]{:S(2)}) async-start(bf16[4,8,160,256]{3,1,2,0:T(8,128)(2,1)} %bitcast_bitcast_fusion), calls=%async_computation.1 | async-start | bytes 5242880 | tf_op jit(solution)/shard_map/all_to_all | solution.py:192
  53.1 58.2 %collective-permute-start.5 = (bf16[320,2432]{1,0:T(8,128)(2,1)}, bf16[320,2432]{1,0:T(8,128)(2,1)}, u32[]{:S(2)}, u32[]{:S(2)}) collective-permute-start(bf16[320,2432]{1,0:T(8,128)(2,1)} %get-tuple-element.62), channel_id=1, source_target_pairs={{0,64},{64,128},{128,192},{192,0},{1,65},{65,129},{129,193},{193,1... | collective-permute-start | bytes 4669448 | tf_op jit(solution)/shard_map/ppermute | solution.py:25
  53.6 57.8 %collective-permute-start.7 = (bf16[320,2432]{1,0:T(8,128)(2,1)}, bf16[320,2432]{1,0:T(8,128)(2,1)}, u32[]{:S(2)}, u32[]{:S(2)}) collective-permute-start(bf16[320,2432]{1,0:T(8,128)(2,1)} %get-tuple-element.63), channel_id=1, source_target_pairs={{0,192},{64,0},{128,64},{192,128},{1,193},{65,1},{129,65},{193,129... | collective-permute-start | bytes 4669448 | tf_op jit(solution)/shard_map/ppermute | solution.py:25
  55.2 66.4 %collective-permute-start.9 = (bf16[320,2432]{1,0:T(8,128)(2,1)}, bf16[320,2432]{1,0:T(8,128)(2,1)}, u32[]{:S(2)}, u32[]{:S(2)}) collective-permute-start(bf16[320,2432]{1,0:T(8,128)(2,1)} %collective-permute-done.1.rest_2_), channel_id=1, source_target_pairs={{0,64},{64,128},{128,192},{192,0},{1,65},{65,129},{129,193},{193,1... | collective-permute-start | bytes 4669448 | tf_op jit(solution)/shard_map/ppermute | solution.py:25
  56.8 66.3 %collective-permute-start.11 = (bf16[320,2432]{1,0:T(8,128)(2,1)}, bf16[320,2432]{1,0:T(8,128)(2,1)}, u32[]{:S(2)}, u32[]{:S(2)}) collective-permute-start(bf16[320,2432]{1,0:T(8,128)(2,1)} %collective-permute-done.2.rest_4_), channel_id=1, source_target_pairs={{0,192},{64,0},{128,64},{192,128},{1,193},{65,1},{129,65},{193,129... | collective-permute-start | bytes 4669448 | tf_op jit(solution)/shard_map/ppermute | solution.py:25
  57.2 65.9 %collective-permute-start.3 = (bf16[320,2432]{1,0:T(8,128)(2,1)}, bf16[320,2432]{1,0:T(8,128)(2,1)}, u32[]{:S(2)}, u32[]{:S(2)}) collective-permute-start(bf16[320,2432]{1,0:T(8,128)(2,1)} %collective-permute-done.1.rest_2_), channel_id=1, source_target_pairs={{0,32},{32,0},{1,33},{33,1},{2,34},{34,2},{3,35},{35,3},{4,36},{36... | collective-permute-start | bytes 4669448 | tf_op jit(solution)/shard_map/ppermute | solution.py:25
  83.4 40.2 %copy-start = (bf16[2,128,2432]{2,1,0:T(8,128)(2,1)S(1)}, bf16[2,128,2432]{2,1,0:T(8,128)(2,1)}, u32[]{:S(2)}) copy-start(bf16[2,128,2432]{2,1,0:T(8,128)(2,1)} %param.9) | copy-start | bytes 3735556
  111.4 16.3 %collective-permute-start.4 = (bf16[320,2432]{1,0:T(8,128)(2,1)}, bf16[320,2432]{1,0:T(8,128)(2,1)S(1)}, u32[]{:S(2)}, u32[]{:S(2)}) collective-permute-start(bf16[320,2432]{1,0:T(8,128)(2,1)} %collective-permute-done.2.rest_4_), channel_id=1, source_target_pairs={{0,32},{32,0},{1,33},{33,1},{2,34},{34,2},{3,35},{35,3},{4,36},{36... | collective-permute-start | bytes 4669448 | tf_op jit(solution)/shard_map/ppermute | solution.py:25
  111.4 16.3 %collective-permute-start.6 = (bf16[320,2432]{1,0:T(8,128)(2,1)}, bf16[320,2432]{1,0:T(8,128)(2,1)}, u32[]{:S(2)}, u32[]{:S(2)}) collective-permute-start(bf16[320,2432]{1,0:T(8,128)(2,1)} %collective-permute-done.5.rest_6_), channel_id=1, source_target_pairs={{0,32},{32,0},{1,33},{33,1},{2,34},{34,2},{3,35},{35,3},{4,36},{36... | collective-permute-start | bytes 4669448 | tf_op jit(solution)/shard_map/ppermute | solution.py:25
  121.6 6.1 %collective-permute-start.8 = (bf16[320,2432]{1,0:T(8,128)(2,1)}, bf16[320,2432]{1,0:T(8,128)(2,1)}, u32[]{:S(2)}, u32[]{:S(2)}) collective-permute-start(bf16[320,2432]{1,0:T(8,128)(2,1)} %collective-permute-done.7.rest_8_), channel_id=1, source_target_pairs={{0,32},{32,0},{1,33},{33,1},{2,34},{34,2},{3,35},{35,3},{4,36},{36... | collective-permute-start | bytes 4669448 | tf_op jit(solution)/shard_map/ppermute | solution.py:25
  123.1 4.6 %collective-permute-start.10 = (bf16[320,2432]{1,0:T(8,128)(2,1)}, bf16[320,2432]{1,0:T(8,128)(2,1)}, u32[]{:S(2)}, u32[]{:S(2)}) collective-permute-start(bf16[320,2432]{1,0:T(8,128)(2,1)} %collective-permute-done.9.rest_10_), channel_id=1, source_target_pairs={{0,32},{32,0},{1,33},{33,1},{2,34},{34,2},{3,35},{35,3},{4,36},{36... | collective-permute-start | bytes 4669448 | tf_op jit(solution)/shard_map/ppermute | solution.py:25
  123.1 6.6 %collective-permute-start.12 = (bf16[320,2432]{1,0:T(8,128)(2,1)}, bf16[320,2432]{1,0:T(8,128)(2,1)}, u32[]{:S(2)}, u32[]{:S(2)}) collective-permute-start(bf16[320,2432]{1,0:T(8,128)(2,1)} %collective-permute-done.11.rest_12_), channel_id=1, source_target_pairs={{0,32},{32,0},{1,33},{33,1},{2,34},{34,2},{3,35},{35,3},{4,36},{36... | collective-permute-start | bytes 4669448 | tf_op jit(solution)/shard_map/ppermute | solution.py:25
  157.5 23.9 %all-to-all-start.3 = ((f32[32,8,256]{2,1,0:T(8,128)}), f32[32,8,256]{2,1,0:T(8,128)S(1)}, u32[]{:S(2)}, u32[]{:S(2)}) async-start(f32[32,8,256]{2,1,0:T(8,128)} %get-tuple-element.27), calls=%async_computation.3 | async-start | bytes 524288 | tf_op jit(solution)/shard_map/all_to_all | solution.py:238
  170.3 66.3 %collective-permute-start.23 = (bf16[160,256]{1,0:T(8,128)(2,1)}, bf16[160,256]{1,0:T(8,128)(2,1)}, u32[]{:S(2)}, u32[]{:S(2)}) collective-permute-start(bf16[160,256]{1,0:T(8,128)(2,1)} %reduce_sum.133), channel_id=1, source_target_pairs={{0,0},{4,32},{8,64},{12,96},{16,128},{20,160},{24,192},{28,224},{3... | collective-permute-start | bytes 245768 | tf_op jit(solution)/shard_map/ppermute | solution.py:222
  177.1 13.8 %collective-permute-start.17 = (bf16[896,256]{1,0:T(8,128)(2,1)}, bf16[896,256]{1,0:T(8,128)(2,1)}, u32[]{:S(2)}, u32[]{:S(2)}) collective-permute-start(bf16[896,256]{1,0:T(8,128)(2,1)} %get-tuple-element.32), channel_id=1, source_target_pairs={{0,1},{1,2},{2,3},{3,0},{4,5},{5,6},{6,7},{7,4},{8,9},{9,10},{10,1... | collective-permute-start | bytes 1376264 | tf_op jit(solution)/shard_map/ppermute | solution.py:25
  177.7 15.3 %collective-permute-start.18 = (bf16[896,256]{1,0:T(8,128)(2,1)}, bf16[896,256]{1,0:T(8,128)(2,1)}, u32[]{:S(2)}, u32[]{:S(2)}) collective-permute-start(bf16[896,256]{1,0:T(8,128)(2,1)} %get-tuple-element.33), channel_id=1, source_target_pairs={{0,2},{1,3},{2,0},{3,1},{4,6},{5,7},{6,4},{7,5},{8,10},{9,11},{10,... | collective-permute-start | bytes 1376264 | tf_op jit(solution)/shard_map/ppermute | solution.py:25
  180.1 20.7 %collective-permute-start.19 = (bf16[896,256]{1,0:T(8,128)(2,1)}, bf16[896,256]{1,0:T(8,128)(2,1)}, u32[]{:S(2)}, u32[]{:S(2)}) collective-permute-start(bf16[896,256]{1,0:T(8,128)(2,1)} %get-tuple-element.34), channel_id=1, source_target_pairs={{0,3},{1,0},{2,1},{3,2},{4,7},{5,4},{6,5},{7,6},{8,11},{9,8},{10,9... | collective-permute-start | bytes 1376264 | tf_op jit(solution)/shard_map/ppermute | solution.py:25
  183.4 37.2 %copy-start.2 = (f32[256,2432]{1,0:T(8,128)S(1)}, f32[256,2432]{1,0:T(8,128)}, u32[]{:S(2)}) copy-start(f32[256,2432]{1,0:T(8,128)} %get-tuple-element.30) | copy-start | bytes 7471108
  183.4 33.0 %all-to-all-start.5 = ((bf16[8,192,256]{2,1,0:T(8,128)(2,1)}), bf16[8,192,256]{2,1,0:T(8,128)(2,1)S(1)}, u32[]{:S(2)}, u32[]{:S(2)}) async-start(bf16[8,192,256]{2,1,0:T(8,128)(2,1)} %get-tuple-element.35), calls=%async_computation.5 | async-start | bytes 1572864 | tf_op jit(solution)/shard_map/all_to_all | solution.py:240
  187.9 28.5 %copy-start.6 = (f32[256]{0:T(256)S(1)}, f32[256]{0:T(256)}, u32[]{:S(2)}) copy-start(f32[256]{0:T(256)} %get-tuple-element.69) | copy-start | bytes 3076
  188.8 14.6 %collective-permute-start.13 = (f32[2,2,128]{2,1,0:T(2,128)S(1)}, f32[2,2,128]{2,1,0:T(2,128)S(1)}, u32[]{:S(2)}, u32[]{:S(2)}) collective-permute-start(f32[2,2,128]{2,1,0:T(2,128)S(1)} %get-tuple-element.80), channel_id=1, source_target_pairs={{0,32},{32,0},{1,33},{33,1},{2,34},{34,2},{3,35},{35,3},{4,36},{36... | collective-permute-start | bytes 6152 | tf_op jit(solution)/shard_map/ppermute | solution.py:25
  203.4 4.7 %collective-permute-start.14 = (f32[2,2,2,128]{3,2,1,0:T(2,128)S(1)}, f32[2,2,2,128]{3,2,1,0:T(2,128)S(1)}, u32[]{:S(2)}, u32[]{:S(2)}) collective-permute-start(f32[2,2,2,128]{3,2,1,0:T(2,128)S(1)} %get-tuple-element.78), channel_id=1, source_target_pairs={{0,64},{64,128},{128,192},{192,0},{1,65},{65,129},{129,193},{193,1... | collective-permute-start | bytes 12296 | tf_op jit(solution)/shard_map/ppermute | solution.py:25
  203.5 6.2 %collective-permute-start.15 = (f32[2,2,2,128]{3,2,1,0:T(2,128)S(1)}, f32[2,2,2,128]{3,2,1,0:T(2,128)S(1)}, u32[]{:S(2)}, u32[]{:S(2)}) collective-permute-start(f32[2,2,2,128]{3,2,1,0:T(2,128)S(1)} %get-tuple-element.78), channel_id=1, source_target_pairs={{0,128},{64,192},{128,0},{192,64},{1,129},{65,193},{129,1},{193,65... | collective-permute-start | bytes 12296 | tf_op jit(solution)/shard_map/ppermute | solution.py:25
  208.1 4.8 %collective-permute-start.16 = (f32[2,2,2,128]{3,2,1,0:T(2,128)S(1)}, f32[2,2,2,128]{3,2,1,0:T(2,128)S(1)}, u32[]{:S(2)}, u32[]{:S(2)}) collective-permute-start(f32[2,2,2,128]{3,2,1,0:T(2,128)S(1)} %get-tuple-element.78), channel_id=1, source_target_pairs={{0,192},{64,0},{128,64},{192,128},{1,193},{65,1},{129,65},{193,129... | collective-permute-start | bytes 12296 | tf_op jit(solution)/shard_map/ppermute | solution.py:25
  216.5 19.0 %all-to-all-start.4 = ((bf16[8,112,256]{2,1,0:T(8,128)(2,1)}), bf16[8,112,256]{2,1,0:T(8,128)(2,1)}, u32[]{:S(2)}, u32[]{:S(2)}) async-start(bf16[8,112,256]{2,1,0:T(8,128)(2,1)} %bitcast.123), calls=%async_computation.4 | async-start | bytes 917504 | tf_op jit(solution)/shard_map/all_to_all | solution.py:261
  223.3 13.2 %collective-permute-start.20 = (bf16[48,256]{1,0:T(8,128)(2,1)S(1)}, bf16[48,256]{1,0:T(8,128)(2,1)S(1)}, u32[]{:S(2)}, u32[]{:S(2)}) collective-permute-start(bf16[48,256]{1,0:T(8,128)(2,1)S(1)} %get-tuple-element.70), channel_id=1, source_target_pairs={{0,1},{1,2},{2,3},{3,0},{4,5},{5,6},{6,7},{7,4},{8,9},{9,10},{10,1... | collective-permute-start | bytes 73736 | tf_op jit(solution)/shard_map/ppermute | solution.py:25
  224.3 12.3 %collective-permute-start.21 = (bf16[48,256]{1,0:T(8,128)(2,1)S(1)}, bf16[48,256]{1,0:T(8,128)(2,1)S(1)}, u32[]{:S(2)}, u32[]{:S(2)}) collective-permute-start(bf16[48,256]{1,0:T(8,128)(2,1)S(1)} %get-tuple-element.72), channel_id=1, source_target_pairs={{0,2},{1,3},{2,0},{3,1},{4,6},{5,7},{6,4},{7,5},{8,10},{9,11},{10,... | collective-permute-start | bytes 73736 | tf_op jit(solution)/shard_map/ppermute | solution.py:25
  226.4 10.2 %collective-permute-start.22 = (bf16[48,256]{1,0:T(8,128)(2,1)S(1)}, bf16[48,256]{1,0:T(8,128)(2,1)S(1)}, u32[]{:S(2)}, u32[]{:S(2)}) collective-permute-start(bf16[48,256]{1,0:T(8,128)(2,1)S(1)} %get-tuple-element.71), channel_id=1, source_target_pairs={{0,3},{1,0},{2,1},{3,2},{4,7},{5,4},{6,5},{7,6},{8,11},{9,8},{10,9... | collective-permute-start | bytes 73736 | tf_op jit(solution)/shard_map/ppermute | solution.py:25
  (5 other events, 44.0 us)

commit v8 on v7

--- a/solution.py
+++ b/solution.py
@@ -219,7 +219,6 @@
         (hidden.reshape(rows, width), turned_refs, own_columns, ref_lse)
     )
     pairs = [(i * zs + j, j * zs + i) for i in range(seqs) for j in range(zs)]
-    own_columns = lax.ppermute(own_columns, SEQ + ("z",), pairs)
     tokens = token_ids.reshape(rows, 1)
     x_index = lax.axis_index("x")
     logits, stats, *backs, other = run_head(
@@ -249,6 +248,8 @@
     lse_ref = top_ref + jnp.log(jnp.sum(jnp.exp(stats[:, 4] - top_ref[None]), axis=0))
     lse_policy = top_policy + jnp.log(total)
     kl_value = (weighted / total - lse_policy + lse_ref).reshape(batch, segment)
+    own_columns, kl_value = lax.optimization_barrier((own_columns, kl_value))
+    own_columns = lax.ppermute(own_columns, SEQ + ("z",), pairs)
 
     z_index = lax.axis_index("z")
     share = (scale / total[None]).reshape(zs, xs, rows)
@@ -278,7 +279,9 @@
     ys = lax.axis_size("y")
     both = jnp.stack([reward, live])
     both = jnp.stack([both, rotate(both, "c", 1)])
-    both = jnp.stack([both] + [rotate(both, "y", step) for step in range(1, ys)])
+    both = both[None]
+    for reach in (1, 2):
+        both = jnp.concatenate([both, rotate(both, "y", reach)])
     both = both.reshape((seqs,) + both.shape[2:])
     rewards, lives = both[:, 0], both[:, 1]
     step = lax.broadcasted_iota(jnp.int32, (seqs, seqs), 0)

time: 239 us -> 236 us (0.987)
  other arithmetic: 17.1 us -> 10.3 us
  waiting for transfers between devices: 90.5 us -> 95.7 us
  starting transfers between devices: 53.9 us -> 51.3 us
    ppermute x23 -> x22, waiting for transfers between devices: 55 us -> 44.6 us  [rotate(): lax.ppermute(value, axis, [(i, (i + by) % count) for i in range(count)])]
    all_to_all x1, waiting for transfers between devices: 1.3 us -> 8.45 us  [per_device(): stats = lax.all_to_all(stats, VOC, 0, 0)]
    all_to_all x1, waiting for transfers between devices: 0.01 us -> 5.63 us  [per_device(): other = lax.all_to_all(other, 'z', 0, 0)]
    ppermute x23 -> x22, starting transfers between devices: 18.2 us -> 15.2 us  [rotate(): lax.ppermute(value, axis, [(i, (i + by) % count) for i in range(count)])]
    all_to_all x1, waiting for transfers between devices: 8.89 us -> 11.6 us  [per_device(): back = lax.all_to_all(back, 'z', 0, 0)]
  transfers between devices with their start and end apart: 29 -> 28, of which waited for: 13 -> 11; matrix products, arithmetic and copies ran while one was open for 14% -> 12% of each run, Pallas kernels for 0% -> 0%
where the time goes in v8:
time: 236 us; the launch traced here: 233 us
  waiting for transfers between devices  95.7 us (41%)
  starting transfers between devices  51.3 us (22%)
  Pallas kernels  27.8 us (12%)
  blocking collectives  27.1 us (11%)
  other arithmetic  10.3 us (4%)
  local copies, waits for them, and re-layouts  10 us (4%)
  matrix products  8.13 us (3%)
  between operations  3.07 us (1%)
    ppermute x22, waiting for transfers between devices, rotate(): lax.ppermute(value, axis, [(i, (i + by) % count) for i in range(count)])  44.6 us
    pallas_call x1, Pallas kernels, run_head(): pl.pallas_call(functools.partial(head_kernel, len(heads), blocks), out_sh...  27.8 us
    all_to_all x1, blocking collectives, token_columns(): found = lax.all_to_all(found, 'z', 0, 0)  27.1 us
    all_to_all x1, waiting for transfers between devices, token_columns(): found = lax.all_to_all(found, 'x', 0, 0)  25.4 us
    ppermute x22, starting transfers between devices, rotate(): lax.ppermute(value, axis, [(i, (i + by) % count) for i in range(count)])  15.2 us
    all_to_all x1, starting transfers between devices, per_device(): stats = lax.all_to_all(stats, VOC, 0, 0)  11.6 us
    all_to_all x1, waiting for transfers between devices, per_device(): back = lax.all_to_all(back, 'z', 0, 0)  11.6 us
    all_to_all x1, waiting for transfers between devices, per_device(): stats = lax.all_to_all(stats, VOC, 0, 0)  8.45 us
  transfers between devices with their start and end apart: 28, of which 11 were waited for; matrix products, arithmetic and copies ran while one was open for 12% of the time, Pallas kernels for 0%

profile of v8, /device:TPU:30, one launch (start us, length us, event | category | flops | bytes accessed | tf_op | source)
XLA Modules:
  0.0 233.4 jit_solution(7179957593666403208)
XLA Ops:
  0.7 1.3 broadcast_in_dim.19
  2.0 4.8 %all-to-all-start = ((s32[8,1,256]{2,1,0:T(1,128)}), s32[8,1,256]{2,1,0:T(1,128)S(1)}, u32[]{:S(2)}, u32[]{:S(2)}) async-start(s32[8,1,256]{2,1,0:T(1,128)} %broadcast_in_dim.19), calls=%async_computation | async-start | bytes 16384 | tf_op jit(solution)/shard_map/all_to_all | solution.py:20
  6.8 3.9 %fusion.36 = (bf16[320,2432]{1,0:T(8,128)(2,1)}, bf16[320,2432]{1,0:T(8,128)(2,1)}) fusion(bf16[640,2432]{1,0:T(8,128)(2,1)} %rest_0_.1), kind=kLoop, calls=%fused_computation.95 | loop fusion | bytes 6225920 | tf_op jit(solution)/shard_map/slice | solution.py:159
  10.7 2.0 collective-permute-start.2
  12.7 7.4 %fusion.4 = bf16[640,2048]{1,0:T(8,128)(2,1)S(1)} fusion(bf16[640,2432]{1,0:T(8,128)(2,1)S(1)} %copy-done.1, s32[2432]{0:T(1024)S(1)} %iota_add_fusion, s32[2048]{0:T(1024)S(1)} %bitcast.128), kind=kOutput, calls=%fused_computation.4 | convolution fusion | flops 6381633536 | bytes 5752320 | tf_op jit(solution)/shard_map/dot_general | solution.py:187
  21.0 1.7 bitcast_bitcast_fusion
  22.6 24.4 %collective-permute-done.1.rest_2_ = bf16[320,2432]{1,0:T(8,128)(2,1)} collective-permute-done((bf16[320,2432]{1,0:T(8,128)(2,1)}, bf16[320,2432]{1,0:T(8,128)(2,1)}, u32[]{:S(2)}, u32[]{:S(2)}) %collective-permute-start.1) | collective-permute-done | bytes 1556512 | tf_op jit(solution)/shard_map/ppermute | solution.py:25
  47.1 1.3 collective-permute-done.2.rest_4_
  48.4 4.8 %all-to-all-start.1 = ((bf16[4,8,160,256]{3,1,2,0:T(8,128)(2,1)}), bf16[4,8,160,256]{3,1,2,0:T(8,128)(2,1)S(1)}, u32[]{:S(2)}, u32[]{:S(2)}) async-start(bf16[4,8,160,256]{3,1,2,0:T(8,128)(2,1)} %bitcast_bitcast_fusion), calls=%async_computation.1 | async-start | bytes 5242880 | tf_op jit(solution)/shard_map/all_to_all | solution.py:192
  53.6 1.6 collective-permute-start.7
  55.2 1.7 collective-permute-start.9
  57.2 25.4 %all-to-all-done.1 = bf16[4,8,160,256]{3,1,2,0:T(8,128)(2,1)S(1)} async-done(((bf16[4,8,160,256]{3,1,2,0:T(8,128)(2,1)}), bf16[4,8,160,256]{3,1,2,0:T(8,128)(2,1)S(1)}, u32[]{:S(2)}, u32[]{:S(2)}) %all-to-all-start.1) | async-done | bytes 2621472 | tf_op jit(solution)/shard_map/all_to_all | solution.py:192
  83.6 27.1 %all_to_all.31 = bf16[8,160,256]{2,1,0:T(8,128)(2,1)S(1)} all-to-all(bf16[8,160,256]{2,1,0:T(8,128)(2,1)S(1)} %copy.33), channel_id=1, replica_groups=mesh['y'=4,'c'=2,'z'=8,'x'=4] {'z'}, dimensions={0} | all-to-all | bytes 1310720 | tf_op jit(solution)/shard_map/all_to_all | solution.py:194
  111.4 10.2 %collective-permute-done.9.rest_10_ = bf16[320,2432]{1,0:T(8,128)(2,1)} collective-permute-done((bf16[320,2432]{1,0:T(8,128)(2,1)}, bf16[320,2432]{1,0:T(8,128)(2,1)}, u32[]{:S(2)}, u32[]{:S(2)}) %collective-permute-start.9) | collective-permute-done | bytes 1556512 | tf_op jit(solution)/shard_map/ppermute | solution.py:25
  121.6 1.5 collective-permute-done.11.rest_12_
  123.9 1.4 copy.38
  127.7 2.1 collective-permute-done.12.rest_13_
  129.8 27.8 %head.1 = (f32[256,2432]{1,0:T(8,128)}, f32[32,8,256]{2,1,0:T(8,128)}, bf16[896,256]{1,0:T(8,128)(2,1)}, bf16[896,256]{1,0:T(8,128)(2,1)}, bf16[896,256]{1,0:T(8...) custom-call(s32[15]{0:T(128)} %stack.84.place_ref, bf16[256,5120]{1,0:T(8,128)(2,1)} %bitcast.138, ...), custom_call_target="tpu_custom_call" | custom-call | flops 12750684160 | bytes 29884416 | tf_op jit(solution)/shard_map/head/pallas_call | solution.py:128
  157.6 11.6 %all-to-all-start.3 = ((f32[32,8,256]{2,1,0:T(8,128)}), f32[32,8,256]{2,1,0:T(8,128)S(1)}, u32[]{:S(2)}, u32[]{:S(2)}) async-start(f32[32,8,256]{2,1,0:T(8,128)} %get-tuple-element.30), calls=%async_computation.3 | async-start | bytes 524288 | tf_op jit(solution)/shard_map/all_to_all | solution.py:237
  169.7 2.7 %collective-permute-start.17 = (bf16[896,256]{1,0:T(8,128)(2,1)}, bf16[896,256]{1,0:T(8,128)(2,1)}, u32[]{:S(2)}, u32[]{:S(2)}) collective-permute-start(bf16[896,256]{1,0:T(8,128)(2,1)} %get-tuple-element.37), channel_id=1, source_target_pairs={{0,2},{1,3},{2,0},{3,1},{4,6},{5,7},{6,4},{7,5},{8,10},{9,11},{10,... | collective-permute-start | bytes 1376264 | tf_op jit(solution)/shard_map/ppermute | solution.py:25
  172.4 8.5 %all-to-all-done.3 = f32[32,8,256]{2,1,0:T(8,128)S(1)} async-done(((f32[32,8,256]{2,1,0:T(8,128)}), f32[32,8,256]{2,1,0:T(8,128)S(1)}, u32[]{:S(2)}, u32[]{:S(2)}) %all-to-all-start.3) | async-done | bytes 262176 | tf_op jit(solution)/shard_map/all_to_all | solution.py:237
  181.4 3.7 %all-to-all-start.5 = ((bf16[8,192,256]{2,1,0:T(8,128)(2,1)}), bf16[8,192,256]{2,1,0:T(8,128)(2,1)S(1)}, u32[]{:S(2)}, u32[]{:S(2)}) async-start(bf16[8,192,256]{2,1,0:T(8,128)(2,1)} %get-tuple-element.39), calls=%async_computation.5 | async-start | bytes 1572864 | tf_op jit(solution)/shard_map/all_to_all | solution.py:239
  185.1 7.2 %collective-permute-start.22 = (bf16[160,256]{1,0:T(8,128)(2,1)S(1)}, bf16[160,256]{1,0:T(8,128)(2,1)S(1)}, u32[]{:S(2)}, u32[]{:S(2)}) collective-permute-start(bf16[160,256]{1,0:T(8,128)(2,1)S(1)} %reduce_sum.133), channel_id=1, source_target_pairs={{0,0},{4,32},{8,64},{12,96},{16,128},{20,160},{24,192},{28,224},{3... | collective-permute-start | bytes 245768 | tf_op jit(solution)/shard_map/ppermute | solution.py:252
  192.4 4.2 %collective-permute-done.14 = f32[1,2,2,2,128]{4,3,2,1,0:T(2,128)S(1)} collective-permute-done((f32[1,2,2,2,128]{4,3,2,1,0:T(2,128)S(1)}, f32[1,2,2,2,128]{4,3,2,1,0:T(2,128)S(1)}, u32[]{:S(2)}, u32[]{:S(2)}) %collective-permute-start.14) | collective-permute-done | bytes 4128 | tf_op jit(solution)/shard_map/ppermute | solution.py:25
  196.6 1.8 collective-permute-start.15
  198.5 2.5 %add_convert_fusion = bf16[896,256]{1,0:T(8,128)(2,1)} fusion(bf16[896,256]{1,0:T(8,128)(2,1)} %collective-permute-done.18, bf16[896,256]{1,0:T(8,128)(2,1)} %collective-permute-done.17, bf16[896,256]{1,0:T(8,128)(2,1)} %collective-permute-done.16, bf16[896,256]{1,0:T(8,128)(2,1)} %get-tuple-element.35, f32[256]{0:T(256)S(1)} %bitcast.130, ...), kind=kLoop, calls=%fused_computation.11 | loop fusion | flops 2752512 | bytes 2297856 | tf_op jit(solution)/shard_map/convert_element_type | solution.py:261
  205.3 5.6 %all-to-all-done.5 = bf16[8,192,256]{2,1,0:T(8,128)(2,1)S(1)} async-done(((bf16[8,192,256]{2,1,0:T(8,128)(2,1)}), bf16[8,192,256]{2,1,0:T(8,128)(2,1)S(1)}, u32[]{:S(2)}, u32[]{:S(2)}) %all-to-all-start.5) | async-done | bytes 786464 | tf_op jit(solution)/shard_map/all_to_all | solution.py:239
  211.0 4.1 %all-to-all-start.4 = ((bf16[8,112,256]{2,1,0:T(8,128)(2,1)}), bf16[8,112,256]{2,1,0:T(8,128)(2,1)}, u32[]{:S(2)}, u32[]{:S(2)}) async-start(bf16[8,112,256]{2,1,0:T(8,128)(2,1)} %bitcast.118), calls=%async_computation.4 | async-start | bytes 917504 | tf_op jit(solution)/shard_map/all_to_all | solution.py:262
  215.1 1.8 multiply_convert_fusion
  217.1 1.9 collective-permute-start.19
  220.0 11.6 %all-to-all-done.4 = bf16[8,112,256]{2,1,0:T(8,128)(2,1)} async-done(((bf16[8,112,256]{2,1,0:T(8,128)(2,1)}), bf16[8,112,256]{2,1,0:T(8,128)(2,1)}, u32[]{:S(2)}, u32[]{:S(2)}) %all-to-all-start.4) | async-done | bytes 458784 | tf_op jit(solution)/shard_map/all_to_all | solution.py:262
  231.6 1.1 convert_reduce_fusion
  (94 shorter events, 11.7 us)
Async XLA Ops:
  0.6 12.1 %collective-permute-start = (bf16[640,2432]{1,0:T(8,128)(2,1)}, bf16[640,2432]{1,0:T(8,128)(2,1)}, u32[]{:S(2)}, u32[]{:S(2)}) collective-permute-start(bf16[640,2432]{1,0:T(8,128)(2,1)} %rest_0_.1), channel_id=1, source_target_pairs={{0,32},{32,0},{1,33},{33,1},{2,34},{34,2},{3,35},{35,3},{4,36},{36... | collective-permute-start | bytes 9338888 | tf_op jit(solution)/shard_map/ppermute | solution.py:25
  2.0 10.7 %all-to-all-start = ((s32[8,1,256]{2,1,0:T(1,128)}), s32[8,1,256]{2,1,0:T(1,128)S(1)}, u32[]{:S(2)}, u32[]{:S(2)}) async-start(s32[8,1,256]{2,1,0:T(1,128)} %broadcast_in_dim.19), calls=%async_computation | async-start | bytes 16384 | tf_op jit(solution)/shard_map/all_to_all | solution.py:20
  10.7 36.4 %collective-permute-start.1 = (bf16[320,2432]{1,0:T(8,128)(2,1)}, bf16[320,2432]{1,0:T(8,128)(2,1)}, u32[]{:S(2)}, u32[]{:S(2)}) collective-permute-start(bf16[320,2432]{1,0:T(8,128)(2,1)} %get-tuple-element.68), channel_id=1, source_target_pairs={{0,64},{64,128},{128,192},{192,0},{1,65},{65,129},{129,193},{193,1... | collective-permute-start | bytes 4669448 | tf_op jit(solution)/shard_map/ppermute | solution.py:25
  10.7 37.7 %collective-permute-start.2 = (bf16[320,2432]{1,0:T(8,128)(2,1)}, bf16[320,2432]{1,0:T(8,128)(2,1)}, u32[]{:S(2)}, u32[]{:S(2)}) collective-permute-start(bf16[320,2432]{1,0:T(8,128)(2,1)} %get-tuple-element.67), channel_id=1, source_target_pairs={{0,192},{64,0},{128,64},{192,128},{1,193},{65,1},{129,65},{193,129... | collective-permute-start | bytes 4669448 | tf_op jit(solution)/shard_map/ppermute | solution.py:25
  48.4 34.2 %all-to-all-start.1 = ((bf16[4,8,160,256]{3,1,2,0:T(8,128)(2,1)}), bf16[4,8,160,256]{3,1,2,0:T(8,128)(2,1)S(1)}, u32[]{:S(2)}, u32[]{:S(2)}) async-start(bf16[4,8,160,256]{3,1,2,0:T(8,128)(2,1)} %bitcast_bitcast_fusion), calls=%async_computation.1 | async-start | bytes 5242880 | tf_op jit(solution)/shard_map/all_to_all | solution.py:192
  53.1 57.6 %collective-permute-start.5 = (bf16[320,2432]{1,0:T(8,128)(2,1)}, bf16[320,2432]{1,0:T(8,128)(2,1)}, u32[]{:S(2)}, u32[]{:S(2)}) collective-permute-start(bf16[320,2432]{1,0:T(8,128)(2,1)} %get-tuple-element.67), channel_id=1, source_target_pairs={{0,64},{64,128},{128,192},{192,0},{1,65},{65,129},{129,193},{193,1... | collective-permute-start | bytes 4669448 | tf_op jit(solution)/shard_map/ppermute | solution.py:25
  53.6 57.3 %collective-permute-start.7 = (bf16[320,2432]{1,0:T(8,128)(2,1)}, bf16[320,2432]{1,0:T(8,128)(2,1)}, u32[]{:S(2)}, u32[]{:S(2)}) collective-permute-start(bf16[320,2432]{1,0:T(8,128)(2,1)} %get-tuple-element.68), channel_id=1, source_target_pairs={{0,192},{64,0},{128,64},{192,128},{1,193},{65,1},{129,65},{193,129... | collective-permute-start | bytes 4669448 | tf_op jit(solution)/shard_map/ppermute | solution.py:25
  55.2 66.4 %collective-permute-start.9 = (bf16[320,2432]{1,0:T(8,128)(2,1)}, bf16[320,2432]{1,0:T(8,128)(2,1)}, u32[]{:S(2)}, u32[]{:S(2)}) collective-permute-start(bf16[320,2432]{1,0:T(8,128)(2,1)} %collective-permute-done.1.rest_2_), channel_id=1, source_target_pairs={{0,64},{64,128},{128,192},{192,0},{1,65},{65,129},{129,193},{193,1... | collective-permute-start | bytes 4669448 | tf_op jit(solution)/shard_map/ppermute | solution.py:25
  56.8 66.3 %collective-permute-start.11 = (bf16[320,2432]{1,0:T(8,128)(2,1)}, bf16[320,2432]{1,0:T(8,128)(2,1)}, u32[]{:S(2)}, u32[]{:S(2)}) collective-permute-start(bf16[320,2432]{1,0:T(8,128)(2,1)} %collective-permute-done.2.rest_4_), channel_id=1, source_target_pairs={{0,192},{64,0},{128,64},{192,128},{1,193},{65,1},{129,65},{193,129... | collective-permute-start | bytes 4669448 | tf_op jit(solution)/shard_map/ppermute | solution.py:25
  57.2 65.9 %collective-permute-start.3 = (bf16[320,2432]{1,0:T(8,128)(2,1)}, bf16[320,2432]{1,0:T(8,128)(2,1)}, u32[]{:S(2)}, u32[]{:S(2)}) collective-permute-start(bf16[320,2432]{1,0:T(8,128)(2,1)} %collective-permute-done.1.rest_2_), channel_id=1, source_target_pairs={{0,32},{32,0},{1,33},{33,1},{2,34},{34,2},{3,35},{35,3},{4,36},{36... | collective-permute-start | bytes 4669448 | tf_op jit(solution)/shard_map/ppermute | solution.py:25
  83.4 40.2 %copy-start = (bf16[2,128,2432]{2,1,0:T(8,128)(2,1)S(1)}, bf16[2,128,2432]{2,1,0:T(8,128)(2,1)}, u32[]{:S(2)}) copy-start(bf16[2,128,2432]{2,1,0:T(8,128)(2,1)} %param.9) | copy-start | bytes 3735556
  110.8 16.9 %collective-permute-start.4 = (bf16[320,2432]{1,0:T(8,128)(2,1)}, bf16[320,2432]{1,0:T(8,128)(2,1)S(1)}, u32[]{:S(2)}, u32[]{:S(2)}) collective-permute-start(bf16[320,2432]{1,0:T(8,128)(2,1)} %collective-permute-done.2.rest_4_), channel_id=1, source_target_pairs={{0,32},{32,0},{1,33},{33,1},{2,34},{34,2},{3,35},{35,3},{4,36},{36... | collective-permute-start | bytes 4669448 | tf_op jit(solution)/shard_map/ppermute | solution.py:25
  110.9 16.8 %collective-permute-start.6 = (bf16[320,2432]{1,0:T(8,128)(2,1)}, bf16[320,2432]{1,0:T(8,128)(2,1)}, u32[]{:S(2)}, u32[]{:S(2)}) collective-permute-start(bf16[320,2432]{1,0:T(8,128)(2,1)} %collective-permute-done.5.rest_6_), channel_id=1, source_target_pairs={{0,32},{32,0},{1,33},{33,1},{2,34},{34,2},{3,35},{35,3},{4,36},{36... | collective-permute-start | bytes 4669448 | tf_op jit(solution)/shard_map/ppermute | solution.py:25
  121.6 6.0 %collective-permute-start.8 = (bf16[320,2432]{1,0:T(8,128)(2,1)}, bf16[320,2432]{1,0:T(8,128)(2,1)}, u32[]{:S(2)}, u32[]{:S(2)}) collective-permute-start(bf16[320,2432]{1,0:T(8,128)(2,1)} %collective-permute-done.7.rest_8_), channel_id=1, source_target_pairs={{0,32},{32,0},{1,33},{33,1},{2,34},{34,2},{3,35},{35,3},{4,36},{36... | collective-permute-start | bytes 4669448 | tf_op jit(solution)/shard_map/ppermute | solution.py:25
  123.1 4.5 %collective-permute-start.10 = (bf16[320,2432]{1,0:T(8,128)(2,1)}, bf16[320,2432]{1,0:T(8,128)(2,1)}, u32[]{:S(2)}, u32[]{:S(2)}) collective-permute-start(bf16[320,2432]{1,0:T(8,128)(2,1)} %collective-permute-done.9.rest_10_), channel_id=1, source_target_pairs={{0,32},{32,0},{1,33},{33,1},{2,34},{34,2},{3,35},{35,3},{4,36},{36... | collective-permute-start | bytes 4669448 | tf_op jit(solution)/shard_map/ppermute | solution.py:25
  123.1 6.6 %collective-permute-start.12 = (bf16[320,2432]{1,0:T(8,128)(2,1)}, bf16[320,2432]{1,0:T(8,128)(2,1)}, u32[]{:S(2)}, u32[]{:S(2)}) collective-permute-start(bf16[320,2432]{1,0:T(8,128)(2,1)} %collective-permute-done.11.rest_12_), channel_id=1, source_target_pairs={{0,32},{32,0},{1,33},{33,1},{2,34},{34,2},{3,35},{35,3},{4,36},{36... | collective-permute-start | bytes 4669448 | tf_op jit(solution)/shard_map/ppermute | solution.py:25
  129.8 51.3 %copy-start.5 = (s32[2,128]{1,0:T(2,128)S(1)}, s32[2,128]{1,0:T(2,128)}, u32[]{:S(2)}) copy-start(s32[2,128]{1,0:T(2,128)} %param.12) | copy-start | bytes 3076
  129.8 51.4 %copy-start.6 = (f32[2]{0:T(128)S(1)}, f32[2]{0:T(128)}, u32[]{:S(2)}) copy-start(f32[2]{0:T(128)} %param.13) | copy-start | bytes 28
  129.8 51.4 %copy-start.7 = (s32[2]{0:T(128)S(1)}, s32[2]{0:T(128)}, u32[]{:S(2)}) copy-start(s32[2]{0:T(128)} %param.11) | copy-start | bytes 28
  157.6 23.2 %all-to-all-start.3 = ((f32[32,8,256]{2,1,0:T(8,128)}), f32[32,8,256]{2,1,0:T(8,128)S(1)}, u32[]{:S(2)}, u32[]{:S(2)}) async-start(f32[32,8,256]{2,1,0:T(8,128)} %get-tuple-element.30), calls=%async_computation.3 | async-start | bytes 524288 | tf_op jit(solution)/shard_map/all_to_all | solution.py:237
  169.3 29.1 %collective-permute-start.16 = (bf16[896,256]{1,0:T(8,128)(2,1)}, bf16[896,256]{1,0:T(8,128)(2,1)}, u32[]{:S(2)}, u32[]{:S(2)}) collective-permute-start(bf16[896,256]{1,0:T(8,128)(2,1)} %get-tuple-element.36), channel_id=1, source_target_pairs={{0,1},{1,2},{2,3},{3,0},{4,5},{5,6},{6,7},{7,4},{8,9},{9,10},{10,1... | collective-permute-start | bytes 1376264 | tf_op jit(solution)/shard_map/ppermute | solution.py:25
  169.7 28.8 %collective-permute-start.17 = (bf16[896,256]{1,0:T(8,128)(2,1)}, bf16[896,256]{1,0:T(8,128)(2,1)}, u32[]{:S(2)}, u32[]{:S(2)}) collective-permute-start(bf16[896,256]{1,0:T(8,128)(2,1)} %get-tuple-element.37), channel_id=1, source_target_pairs={{0,2},{1,3},{2,0},{3,1},{4,6},{5,7},{6,4},{7,5},{8,10},{9,11},{10,... | collective-permute-start | bytes 1376264 | tf_op jit(solution)/shard_map/ppermute | solution.py:25
  172.3 26.1 %collective-permute-start.18 = (bf16[896,256]{1,0:T(8,128)(2,1)}, bf16[896,256]{1,0:T(8,128)(2,1)}, u32[]{:S(2)}, u32[]{:S(2)}) collective-permute-start(bf16[896,256]{1,0:T(8,128)(2,1)} %get-tuple-element.38), channel_id=1, source_target_pairs={{0,3},{1,0},{2,1},{3,2},{4,7},{5,4},{6,5},{7,6},{8,11},{9,8},{10,9... | collective-permute-start | bytes 1376264 | tf_op jit(solution)/shard_map/ppermute | solution.py:25
  181.3 11.1 %collective-permute-start.13 = (f32[2,2,128]{2,1,0:T(2,128)S(1)}, f32[2,2,128]{2,1,0:T(2,128)S(1)}, u32[]{:S(2)}, u32[]{:S(2)}) collective-permute-start(f32[2,2,128]{2,1,0:T(2,128)S(1)} %get-tuple-element.83), channel_id=1, source_target_pairs={{0,32},{32,0},{1,33},{33,1},{2,34},{34,2},{3,35},{35,3},{4,36},{36... | collective-permute-start | bytes 6152 | tf_op jit(solution)/shard_map/ppermute | solution.py:25
  181.4 29.6 %all-to-all-start.5 = ((bf16[8,192,256]{2,1,0:T(8,128)(2,1)}), bf16[8,192,256]{2,1,0:T(8,128)(2,1)S(1)}, u32[]{:S(2)}, u32[]{:S(2)}) async-start(bf16[8,192,256]{2,1,0:T(8,128)(2,1)} %get-tuple-element.39), calls=%async_computation.5 | async-start | bytes 1572864 | tf_op jit(solution)/shard_map/all_to_all | solution.py:239
  185.1 47.7 %collective-permute-start.22 = (bf16[160,256]{1,0:T(8,128)(2,1)S(1)}, bf16[160,256]{1,0:T(8,128)(2,1)S(1)}, u32[]{:S(2)}, u32[]{:S(2)}) collective-permute-start(bf16[160,256]{1,0:T(8,128)(2,1)S(1)} %reduce_sum.133), channel_id=1, source_target_pairs={{0,0},{4,32},{8,64},{12,96},{16,128},{20,160},{24,192},{28,224},{3... | collective-permute-start | bytes 245768 | tf_op jit(solution)/shard_map/ppermute | solution.py:252
  192.3 4.3 %collective-permute-start.14 = (f32[1,2,2,2,128]{4,3,2,1,0:T(2,128)S(1)}, f32[1,2,2,2,128]{4,3,2,1,0:T(2,128)S(1)}, u32[]{:S(2)}, u32[]{:S(2)}) collective-permute-start(f32[1,2,2,2,128]{4,3,2,1,0:T(2,128)S(1)} %maximum_bitcast_fusion), channel_id=1, source_target_pairs={{0,64},{64,128},{128,192},{192,0},{1,65},{65,129},{129,193},{193,1... | collective-permute-start | bytes 12296 | tf_op jit(solution)/shard_map/ppermute | solution.py:25
  196.6 5.2 %collective-permute-start.15 = (f32[2,2,2,2,128]{4,3,2,1,0:T(2,128)S(1)}, f32[2,2,2,2,128]{4,3,2,1,0:T(2,128)S(1)}, u32[]{:S(2)}, u32[]{:S(2)}) collective-permute-start(f32[2,2,2,2,128]{4,3,2,1,0:T(2,128)S(1)} %pad_maximum_fusion.1), channel_id=1, source_target_pairs={{0,128},{64,192},{128,0},{192,64},{1,129},{65,193},{129,1},{193,65... | collective-permute-start | bytes 24584 | tf_op jit(solution)/shard_map/ppermute | solution.py:25
  211.0 20.6 %all-to-all-start.4 = ((bf16[8,112,256]{2,1,0:T(8,128)(2,1)}), bf16[8,112,256]{2,1,0:T(8,128)(2,1)}, u32[]{:S(2)}, u32[]{:S(2)}) async-start(bf16[8,112,256]{2,1,0:T(8,128)(2,1)} %bitcast.118), calls=%async_computation.4 | async-start | bytes 917504 | tf_op jit(solution)/shard_map/all_to_all | solution.py:262
  217.1 15.6 %collective-permute-start.19 = (bf16[48,256]{1,0:T(8,128)(2,1)S(1)}, bf16[48,256]{1,0:T(8,128)(2,1)S(1)}, u32[]{:S(2)}, u32[]{:S(2)}) collective-permute-start(bf16[48,256]{1,0:T(8,128)(2,1)S(1)} %get-tuple-element.75), channel_id=1, source_target_pairs={{0,1},{1,2},{2,3},{3,0},{4,5},{5,6},{6,7},{7,4},{8,9},{9,10},{10,1... | collective-permute-start | bytes 73736 | tf_op jit(solution)/shard_map/ppermute | solution.py:25
  219.1 13.6 %collective-permute-start.20 = (bf16[48,256]{1,0:T(8,128)(2,1)S(1)}, bf16[48,256]{1,0:T(8,128)(2,1)S(1)}, u32[]{:S(2)}, u32[]{:S(2)}) collective-permute-start(bf16[48,256]{1,0:T(8,128)(2,1)S(1)} %get-tuple-element.77), channel_id=1, source_target_pairs={{0,2},{1,3},{2,0},{3,1},{4,6},{5,7},{6,4},{7,5},{8,10},{9,11},{10,... | collective-permute-start | bytes 73736 | tf_op jit(solution)/shard_map/ppermute | solution.py:25
  220.0 12.7 %collective-permute-start.21 = (bf16[48,256]{1,0:T(8,128)(2,1)S(1)}, bf16[48,256]{1,0:T(8,128)(2,1)S(1)}, u32[]{:S(2)}, u32[]{:S(2)}) collective-permute-start(bf16[48,256]{1,0:T(8,128)(2,1)S(1)} %get-tuple-element.76), channel_id=1, source_target_pairs={{0,3},{1,0},{2,1},{3,2},{4,7},{5,4},{6,5},{7,6},{8,11},{9,8},{10,9... | collective-permute-start | bytes 73736 | tf_op jit(solution)/shard_map/ppermute | solution.py:25
  (5 other events, 56.4 us)
